TPU v7x, 32 devices: a whole 2x2x4 slice. The times are simulated.
32 devices in a mesh: chan: 16 (over z, x, core), win: 2 (over y).
Axes of the slice: x: 2, y: 2, z: 4, core: 2. Of those that a mesh axis runs over, the one named last changes fastest.
Arguments:
- records: bfloat16 [2048, 8192], P('chan', 'win')
- fir_taps: float32 [64], replicated, may hold values from -0.75 to 0.75
- pair_offsets: int32 [16, 2], P('chan'), may hold values from -4 to 5, as said below
Outputs:
- correlations: float32 [2048, 2, 33, 128], P(('chan', 'win'))
Inputs may be any that keep to these rules, and one draw needn't show every extreme that they name: `pair_offsets`: each row lists one to 2 distinct offsets of -4 to 4 in its first slots and fills the remaining slots with 5, which lists no pair.
All inputs are finite; a program needn't handle non-finite values.
Results may differ from a plain program's by a relative error of at most 0.0037.
Values may be sent and summed in bfloat16 or wider, within the bound.
No kernel may reach another device: no remote copies, remote signals or barrier semaphores. Data moves between devices by JAX's collectives and lax.ppermute only.
A program may use at most 64 MiB of HBM per device.

v0:
```python
import math

import jax
import jax.numpy as jnp
from jax import lax
from jax.sharding import PartitionSpec as P

SAMPLES = 4096
TAPS = 64
DECIM = 4
MAXLAG = 16
T_DEC = 1024
LAGS = 33


def from_behind(value, axis, steps):
    count = lax.axis_size(axis)
    initial, last = (max(0, -steps), min(count, count - steps))
    return lax.ppermute(value, axis, [(source, source + steps) for source in range(initial, last)])


def from_behind_2(x, axis, by):
    length = lax.axis_size(axis)
    return lax.ppermute(x, axis, [(i, (i + by) % length) for i in range(length)])


def whiten_local(records, fir_taps):
    channels, length = records.shape
    history_len = TAPS - DECIM
    tail_part = records[:, length - history_len :]
    before = from_behind(tail_part, "win", 1)
    signal = jnp.concatenate([before, records], axis=1).astype(jnp.float32)
    n_out = length // DECIM
    phases = [signal[:, phase_id::DECIM] for phase_id in range(DECIM)]
    filtered = jnp.zeros((channels, n_out), jnp.float32)
    for shift_id in range(TAPS // DECIM):
        for phase_id in range(DECIM):
            filtered = (
                filtered
                + fir_taps[DECIM * shift_id + phase_id]
                * phases[phase_id][:, shift_id : shift_id + n_out]
            )
    filtered = filtered.reshape(channels, length // SAMPLES, T_DEC)
    energy = jnp.sqrt(jnp.mean(filtered * filtered, axis=2, keepdims=True) + 1e-06)
    return (filtered / energy).astype(jnp.bfloat16)


def correlate(own_rows, other):
    length = other.shape[2]
    padded = jnp.pad(other, ((0, 0), (0, 0), (MAXLAG, MAXLAG)))
    pieces = []
    for first_lag in range(0, LAGS, 16):
        last_lag = min(first_lag + 16, LAGS)
        stacked = jnp.stack(
            [padded[:, :, lag_id : lag_id + length] for lag_id in range(first_lag, last_lag)]
        )
        pieces.append(
            lax.dot_general(
                own_rows, stacked, (((1, 2), (2, 3)), ((), ())), preferred_element_type=jnp.float32
            )
        )
    return jnp.concatenate(pieces, axis=1)


def body(records, fir_taps, pair_offsets):
    whitened = whiten_local(records, fir_taps)
    channels = whitened.shape[0]
    windows_all = whitened.shape[1] * lax.axis_size("win")
    factor = 1.0 / math.sqrt(T_DEC * windows_all)
    reach = lax.axis_size("chan") // 4
    offset_row = pair_offsets[0]
    n_slots = offset_row.shape[0]
    partner_width = whitened.shape[0]

    def process(totals, block, offset):
        listed = offset_row == offset

        def add_pair(current):
            result = correlate(whitened, block) * factor
            weights = listed.astype(jnp.float32)
            for slot_id in range(n_slots):
                current = current.at[:, slot_id].add(weights[slot_id] * result)
            return current

        def keep_same(current):
            return current

        return lax.cond(jnp.any(listed), add_pair, keep_same, totals)

    totals = jnp.zeros((channels, n_slots, LAGS, partner_width), jnp.float32)
    first_block = from_behind_2(whitened, "chan", reach)
    totals = process(totals, first_block, -reach)

    def one_side(station, carry):
        current, moving = carry
        moving = from_behind_2(moving, "chan", -1)
        current = process(current, moving, station - reach)
        return (current, moving)

    totals, moving = lax.fori_loop(1, 2 * reach + 1, one_side, (totals, first_block))
    return lax.psum_scatter(totals, "win", scatter_dimension=0, tiled=True)


def solution(mesh):
    placed = (P("chan", "win"), P(), P("chan", None))
    return jax.shard_map(
        body,
        mesh=mesh,
        in_specs=placed,
        out_specs=P(("chan", "win"), None, None, None),
        check_vma=False,
    )
```

profile of v0, /device:TPU:0, one launch (start us, length us, event | category | flops | bytes accessed | tf_op | source)
XLA Modules:
  0.0 413.5 jit_solution(12274540564540926791)
XLA Ops:
  7.4 4.9 %collective-permute-start.1 = (bf16[128,60]{1,0:T(8,128)(2,1)S(1)}, bf16[128,60]{1,0:T(8,128)(2,1)S(1)}, u32[]{:S(2)}, u32[]{:S(2)}) collective-permute-start(bf16[128,60]{1,0:T(8,128)(2,1)S(1)} %slice.709), channel_id=1, source_target_pairs={{0,1},{2,3},{4,5},{6,7},{8,9},{10,11},{12,13},{14,15},{16,17},{18,... | collective-permute-start | bytes 46088 | tf_op jit(solution)/shard_map/ppermute | solution.py:19
  12.2 2.1 fusion.104
  20.0 2.9 maximum_convert_fusion
  23.0 18.8 %slice.710 = f32[128,1039]{1,0:T(8,128)S(1)} slice(f32[128,4156]{1,0:T(8,128)} %maximum_convert_fusion), slice={[0:128:1], [0:4156:4]} | slice | bytes 1063936 | tf_op jit(solution)/shard_map/slice | solution.py:34
  41.8 18.8 %slice.713 = f32[128,1039]{1,0:T(8,128)S(1)} slice(f32[128,4156]{1,0:T(8,128)} %maximum_convert_fusion), slice={[0:128:1], [1:4156:4]} | slice | bytes 1063936 | tf_op jit(solution)/shard_map/slice | solution.py:34
  60.6 18.8 %slice.716 = f32[128,1039]{1,0:T(8,128)S(1)} slice(f32[128,4156]{1,0:T(8,128)} %maximum_convert_fusion), slice={[0:128:1], [2:4156:4]} | slice | bytes 1063936 | tf_op jit(solution)/shard_map/slice | solution.py:34
  79.4 29.9 %slice.719 = f32[128,1039]{1,0:T(8,128)S(1)} slice(f32[128,4156]{1,0:T(8,128)} %maximum_convert_fusion), slice={[0:128:1], [3:4156:4]} | slice | bytes 1063936 | tf_op jit(solution)/shard_map/slice | solution.py:34
  109.4 48.7 %multiply_reduce_fusion = (f32[128]{0:T(128)S(1)}, f32[128,1024]{1,0:T(8,128)S(1)}) fusion(f32[128,1039]{1,0:T(8,128)S(1)} %slice.719, f32[]{:T(128)} %bitcast.184, f32[128,1039]{1,0:T(8,128)S(1)} %slice.716, f32[]{:T(128)} %bitcast.183, f32[128,1039]{1,0:T(8,128)S(1)} %slice.713, f32[]{:T(128)} %bitcast.182, f32[128,1039]{1,0:T(8,128)S(1)} %slice.710, ...), kind=kLoop, calls=%fused_computation.228 | loop fusion | flops 16908160 | bytes 34079488 | tf_op jit(solution)/shard_map/reduce_sum | solution.py:44
  161.1 6.8 %collective-permute-done.2 = bf16[128,1,1024]{2,0,1:T(8,128)(2,1)S(1)} collective-permute-done((bf16[128,1,1024]{2,0,1:T(8,128)(2,1)S(1)}, bf16[128,1,1024]{2,0,1:T(8,128)(2,1)S(1)}, u32[]{:S(2)}, u32[]{:S(2)}) %collective-permute-start.2) | collective-permute-done | bytes 262176 | tf_op jit(solution)/shard_map/ppermute | solution.py:24
  167.8 2.6 conditional.2
  167.8 2.6 broadcast_in_dim.0
  170.4 111.0 %while.26 = (s32[]{:T(128)}, f32[128,2,33,128]{0,3,2,1:T(8,128)}, bf16[128,1,1024]{2,0,1:T(8,128)(2,1)S(1)}, s32[2]{0:T(128)S(1)}, bf16[128,1,1024]{2,0,1:T(8,128)(2,1)S(1)}, /*index=5*/s32[]{:T(128)}, s32[]{:T(128)}) while((s32[]{:T(128)}, f32[128,2,33,128]{0,3,2,1:T(8,128)}, bf16[128,1,1024]{2,0,1:T(8,128)(2,1)S(1)}, s32[2]{0:T(128)S(1)}, ...), condition=%wide.region_8.0_spmd, body=%wide.region_4.8_spmd.sunk | while | flops 1111621632 | bytes 42927344 | solution.py:100
  172.6 2.6 collective-permute-done
  175.3 4.7 %collective-permute-start = (bf16[128,1,1024]{2,0,1:T(8,128)(2,1)S(1)}, bf16[128,1,1024]{2,0,1:T(8,128)(2,1)S(1)}, u32[]{:S(2)}, u32[]{:S(2)}) collective-permute-start(bf16[128,1,1024]{2,0,1:T(8,128)(2,1)S(1)} %get-tuple-element.392), channel_id=1, source_target_pairs={{0,30},{2,0},{4,2},{6,4},{8,6},{10,8},{12,10},{14,12},{16,14},{18,... | collective-permute-start | bytes 786440 | tf_op jit(solution)/shard_map/while/body/eval_jaxpr/ppermute | solution.py:24
  181.2 2.6 collective-permute-done
  183.9 4.7 %collective-permute-start = (bf16[128,1,1024]{2,0,1:T(8,128)(2,1)S(1)}, bf16[128,1,1024]{2,0,1:T(8,128)(2,1)S(1)}, u32[]{:S(2)}, u32[]{:S(2)}) collective-permute-start(bf16[128,1,1024]{2,0,1:T(8,128)(2,1)S(1)} %get-tuple-element.392), channel_id=1, source_target_pairs={{0,30},{2,0},{4,2},{6,4},{8,6},{10,8},{12,10},{14,12},{16,14},{18,... | collective-permute-start | bytes 786440 | tf_op jit(solution)/shard_map/while/body/eval_jaxpr/ppermute | solution.py:24
  189.8 2.6 collective-permute-done
  192.4 4.7 %collective-permute-start = (bf16[128,1,1024]{2,0,1:T(8,128)(2,1)S(1)}, bf16[128,1,1024]{2,0,1:T(8,128)(2,1)S(1)}, u32[]{:S(2)}, u32[]{:S(2)}) collective-permute-start(bf16[128,1,1024]{2,0,1:T(8,128)(2,1)S(1)} %get-tuple-element.392), channel_id=1, source_target_pairs={{0,30},{2,0},{4,2},{6,4},{8,6},{10,8},{12,10},{14,12},{16,14},{18,... | collective-permute-start | bytes 786440 | tf_op jit(solution)/shard_map/while/body/eval_jaxpr/ppermute | solution.py:24
  198.4 2.6 collective-permute-done
  201.0 16.0 %collective-permute-start = (bf16[128,1,1024]{2,0,1:T(8,128)(2,1)S(1)}, bf16[128,1,1024]{2,0,1:T(8,128)(2,1)S(1)}, u32[]{:S(2)}, u32[]{:S(2)}) collective-permute-start(bf16[128,1,1024]{2,0,1:T(8,128)(2,1)S(1)} %get-tuple-element.392), channel_id=1, source_target_pairs={{0,30},{2,0},{4,2},{6,4},{8,6},{10,8},{12,10},{14,12},{16,14},{18,... | collective-permute-start | bytes 786440 | tf_op jit(solution)/shard_map/while/body/eval_jaxpr/ppermute | solution.py:24
  218.3 2.6 collective-permute-done
  221.0 4.7 %collective-permute-start = (bf16[128,1,1024]{2,0,1:T(8,128)(2,1)S(1)}, bf16[128,1,1024]{2,0,1:T(8,128)(2,1)S(1)}, u32[]{:S(2)}, u32[]{:S(2)}) collective-permute-start(bf16[128,1,1024]{2,0,1:T(8,128)(2,1)S(1)} %get-tuple-element.392), channel_id=1, source_target_pairs={{0,30},{2,0},{4,2},{6,4},{8,6},{10,8},{12,10},{14,12},{16,14},{18,... | collective-permute-start | bytes 786440 | tf_op jit(solution)/shard_map/while/body/eval_jaxpr/ppermute | solution.py:24
  226.9 9.6 %collective-permute-done = bf16[128,1,1024]{2,0,1:T(8,128)(2,1)S(1)} collective-permute-done((bf16[128,1,1024]{2,0,1:T(8,128)(2,1)S(1)}, bf16[128,1,1024]{2,0,1:T(8,128)(2,1)S(1)}, u32[]{:S(2)}, u32[]{:S(2)}) %collective-permute-start) | collective-permute-done | bytes 262176 | tf_op jit(solution)/shard_map/while/body/eval_jaxpr/ppermute | solution.py:24
  236.5 16.2 %conditional.4 = (f32[128,2,33,128]{0,3,2,1:T(8,128)}) conditional(s32[]{:T(128)} %convert_element_type.43, f32[128,2,33,128]{0,3,2,1:T(8,128)} %get-tuple-element.391, (f32[128,2,33,128]{0,3,2,1:T(8,128)}, bf16[128,1,1024]{2,0,1:T(8,128)(2,1)S(1)}, bf16[128,1,1024]{2,0,1:T(8,128)(2,1)S(1)}, pred[2]{0:T(512)(128)(4,1)S(1)}) %tuple.153), branch_computations={%region_6.6_spmd, %region_7.7_spmd} | conditional | flops 1111621632 | bytes 41354300 | solution.py:88
  245.1 3.4 add_dynamic-update-slice_fusion
  249.2 3.5 fusion.22
  254.1 2.6 collective-permute-done
  256.7 20.8 %collective-permute-start = (bf16[128,1,1024]{2,0,1:T(8,128)(2,1)S(1)}, bf16[128,1,1024]{2,0,1:T(8,128)(2,1)S(1)}, u32[]{:S(2)}, u32[]{:S(2)}) collective-permute-start(bf16[128,1,1024]{2,0,1:T(8,128)(2,1)S(1)} %get-tuple-element.392), channel_id=1, source_target_pairs={{0,30},{2,0},{4,2},{6,4},{8,6},{10,8},{12,10},{14,12},{16,14},{18,... | collective-permute-start | bytes 786440 | tf_op jit(solution)/shard_map/while/body/eval_jaxpr/ppermute | solution.py:24
  278.8 2.6 collective-permute-done
  281.5 7.8 %copy.65 = f32[128,2,33,128]{3,1,2,0:T(2,128)} copy(f32[128,2,33,128]{0,3,2,1:T(8,128)} %get-tuple-element.261) | data formatting | bytes 8650752 | tf_op jit(solution)/shard_map/while | solution.py:100
  291.1 112.1 %all-reduce.5.cloned.1.call-done = f32[128,2,33,128]{3,1,2,0:T(2,128)} async-done(((f32[128,2,33,128]{3,1,2,0:T(2,128)}), f32[128,2,33,128]{3,1,2,0:T(2,128)}) %all-reduce.5.cloned.1.call-update) | async-done | bytes 4325392
  403.2 3.1 constant_dynamic-slice_fusion
  (78 shorter events, 24.2 us)
Async XLA Ops:
  6.5 396.7 %all-reduce.5.cloned.1.call-start = ((), (), s32[]{:S(2)}) async-start(), calls=%async_computation | async-start | bytes 8650752
  7.4 12.7 %collective-permute-start.1 = (bf16[128,60]{1,0:T(8,128)(2,1)S(1)}, bf16[128,60]{1,0:T(8,128)(2,1)S(1)}, u32[]{:S(2)}, u32[]{:S(2)}) collective-permute-start(bf16[128,60]{1,0:T(8,128)(2,1)S(1)} %slice.709), channel_id=1, source_target_pairs={{0,1},{2,3},{4,5},{6,7},{8,9},{10,11},{12,13},{14,15},{16,17},{18,... | collective-permute-start | bytes 46088 | tf_op jit(solution)/shard_map/ppermute | solution.py:19
  109.4 50.4 %copy-start = (s32[1,2]{1,0:T(1,128)S(1)}, s32[1,2]{1,0:T(1,128)}, u32[]{:S(2)}) copy-start(s32[1,2]{1,0:T(1,128)} %param.19) | copy-start | bytes 28
  158.2 9.7 %collective-permute-start.2 = (bf16[128,1,1024]{2,0,1:T(8,128)(2,1)S(1)}, bf16[128,1,1024]{2,0,1:T(8,128)(2,1)S(1)}, u32[]{:S(2)}, u32[]{:S(2)}) collective-permute-start(bf16[128,1,1024]{2,0,1:T(8,128)(2,1)S(1)} %fusion.98), channel_id=1, source_target_pairs={{0,8},{2,10},{4,12},{6,14},{8,16},{10,18},{12,20},{14,22},{16,24},... | collective-permute-start | bytes 786440 | tf_op jit(solution)/shard_map/ppermute | solution.py:24
  170.4 4.8 %collective-permute-start = (bf16[128,1,1024]{2,0,1:T(8,128)(2,1)S(1)}, bf16[128,1,1024]{2,0,1:T(8,128)(2,1)S(1)}, u32[]{:S(2)}, u32[]{:S(2)}) collective-permute-start(bf16[128,1,1024]{2,0,1:T(8,128)(2,1)S(1)} %get-tuple-element.392), channel_id=1, source_target_pairs={{0,30},{2,0},{4,2},{6,4},{8,6},{10,8},{12,10},{14,12},{16,14},{18,... | collective-permute-start | bytes 786440 | tf_op jit(solution)/shard_map/while/body/eval_jaxpr/ppermute | solution.py:24
  175.3 8.5 %collective-permute-start = (bf16[128,1,1024]{2,0,1:T(8,128)(2,1)S(1)}, bf16[128,1,1024]{2,0,1:T(8,128)(2,1)S(1)}, u32[]{:S(2)}, u32[]{:S(2)}) collective-permute-start(bf16[128,1,1024]{2,0,1:T(8,128)(2,1)S(1)} %get-tuple-element.392), channel_id=1, source_target_pairs={{0,30},{2,0},{4,2},{6,4},{8,6},{10,8},{12,10},{14,12},{16,14},{18,... | collective-permute-start | bytes 786440 | tf_op jit(solution)/shard_map/while/body/eval_jaxpr/ppermute | solution.py:24
  183.9 8.5 %collective-permute-start = (bf16[128,1,1024]{2,0,1:T(8,128)(2,1)S(1)}, bf16[128,1,1024]{2,0,1:T(8,128)(2,1)S(1)}, u32[]{:S(2)}, u32[]{:S(2)}) collective-permute-start(bf16[128,1,1024]{2,0,1:T(8,128)(2,1)S(1)} %get-tuple-element.392), channel_id=1, source_target_pairs={{0,30},{2,0},{4,2},{6,4},{8,6},{10,8},{12,10},{14,12},{16,14},{18,... | collective-permute-start | bytes 786440 | tf_op jit(solution)/shard_map/while/body/eval_jaxpr/ppermute | solution.py:24
  192.4 8.5 %collective-permute-start = (bf16[128,1,1024]{2,0,1:T(8,128)(2,1)S(1)}, bf16[128,1,1024]{2,0,1:T(8,128)(2,1)S(1)}, u32[]{:S(2)}, u32[]{:S(2)}) collective-permute-start(bf16[128,1,1024]{2,0,1:T(8,128)(2,1)S(1)} %get-tuple-element.392), channel_id=1, source_target_pairs={{0,30},{2,0},{4,2},{6,4},{8,6},{10,8},{12,10},{14,12},{16,14},{18,... | collective-permute-start | bytes 786440 | tf_op jit(solution)/shard_map/while/body/eval_jaxpr/ppermute | solution.py:24
  201.0 19.9 %collective-permute-start = (bf16[128,1,1024]{2,0,1:T(8,128)(2,1)S(1)}, bf16[128,1,1024]{2,0,1:T(8,128)(2,1)S(1)}, u32[]{:S(2)}, u32[]{:S(2)}) collective-permute-start(bf16[128,1,1024]{2,0,1:T(8,128)(2,1)S(1)} %get-tuple-element.392), channel_id=1, source_target_pairs={{0,30},{2,0},{4,2},{6,4},{8,6},{10,8},{12,10},{14,12},{16,14},{18,... | collective-permute-start | bytes 786440 | tf_op jit(solution)/shard_map/while/body/eval_jaxpr/ppermute | solution.py:24
  221.0 15.5 %collective-permute-start = (bf16[128,1,1024]{2,0,1:T(8,128)(2,1)S(1)}, bf16[128,1,1024]{2,0,1:T(8,128)(2,1)S(1)}, u32[]{:S(2)}, u32[]{:S(2)}) collective-permute-start(bf16[128,1,1024]{2,0,1:T(8,128)(2,1)S(1)} %get-tuple-element.392), channel_id=1, source_target_pairs={{0,30},{2,0},{4,2},{6,4},{8,6},{10,8},{12,10},{14,12},{16,14},{18,... | collective-permute-start | bytes 786440 | tf_op jit(solution)/shard_map/while/body/eval_jaxpr/ppermute | solution.py:24
  252.7 3.9 collective-permute-start
  256.7 24.7 %collective-permute-start = (bf16[128,1,1024]{2,0,1:T(8,128)(2,1)S(1)}, bf16[128,1,1024]{2,0,1:T(8,128)(2,1)S(1)}, u32[]{:S(2)}, u32[]{:S(2)}) collective-permute-start(bf16[128,1,1024]{2,0,1:T(8,128)(2,1)S(1)} %get-tuple-element.392), channel_id=1, source_target_pairs={{0,30},{2,0},{4,2},{6,4},{8,6},{10,8},{12,10},{14,12},{16,14},{18,... | collective-permute-start | bytes 786440 | tf_op jit(solution)/shard_map/while/body/eval_jaxpr/ppermute | solution.py:24
  289.3 0.7 copy-start.1
Sparse Core Ops, SparseCore 0:
  289.4 113.7 all-reduce.4
where the time goes:
time: 416 us; the launch traced here: 414 us
  waiting for transfers between devices  147 us (35%)
  local copies, waits for them, and re-layouts  115 us (28%)
  other arithmetic  64.5 us (16%)
  starting transfers between devices  62.9 us (15%)
  between operations  15.2 us (4%)
  loops' own time  6.81 us (2%)
    unnamed x2, waiting for transfers between devices  112 us
    slice x4, local copies, waits for them, and re-layouts, whiten_local(): phases = [signal[:, phase_id::DECIM] for phase_id in range(DECIM)]  86.4 us
    ppermute x9, starting transfers between devices, from_behind_2(): lax.ppermute(x, axis, [(i, (i + by) % length) for i in range(length)])  58.1 us
    reduce_sum x1, other arithmetic, whiten_local(): jnp.mean(filtered * filtered, axis=2, keepdims=True) + 1e-06  48.7 us
    ppermute x9, waiting for transfers between devices, from_behind_2(): lax.ppermute(x, axis, [(i, (i + by) % length) for i in range(length)])  34.5 us
  transfers between devices with their start and end apart: 11, of which 10 were waited for; matrix products, arithmetic and copies ran while one was open for 3% of the time, Pallas kernels for 0%

commit v1 on v0

v1 whole, which is shorter than its diff:
```python
import functools
import math

import jax
import jax.numpy as jnp
from jax import lax
from jax.experimental import pallas as pl
from jax.experimental.pallas import tpu as pltpu
from jax.sharding import PartitionSpec as P

TAPS = 64
DECIM = 4
MAXLAG = 16
T_DEC = 1024
LAGS = 33
LANES = 128
HISTORY = TAPS - DECIM
SPAN = LANES * DECIM + LANES
CHUNKS = 2
T_CHUNK = T_DEC // CHUNKS
LAG_ROWS = 32
VMEM = pltpu.VMEM
F32 = jnp.float32
BF16 = jnp.bfloat16
NT = (((1,), (1,)), ((), ()))
VMEM_SPEC = pl.BlockSpec(memory_space=pltpu.VMEM)
SMEM_SPEC = pl.BlockSpec(memory_space=pltpu.SMEM)


def shift(x, axis, by):
    n = lax.axis_size(axis)
    return lax.ppermute(x, axis, [(i, (i + by) % n) for i in range(n)])


def flip_core(x):
    n = lax.axis_size("chan")
    return lax.ppermute(x, "chan", [(i, i ^ 1) for i in range(n)])


def whiten_kernel(win, rows, tail_ref, records_ref, taps_ref, *refs):
    chunk_refs = refs[:CHUNKS]
    row_refs = refs[CHUNKS : CHUNKS + win]
    taps_scr, filtered = refs[CHUNKS + win :]
    channels = records_ref.shape[0]
    taps_scr[...] = jnp.zeros_like(taps_scr)
    taps_scr[0:1, 0:TAPS] = taps_ref[...]
    line = jnp.broadcast_to(taps_scr[0:1, :], (LANES, SPAN))
    band = pltpu.roll(line, LANES - HISTORY, 1, stride=DECIM, stride_axis=0)
    high = band.astype(BF16)
    rest = band - high.astype(F32)
    mid = rest.astype(BF16)
    low = (rest - mid.astype(F32)).astype(BF16)
    weights = jnp.concatenate([high, mid, low], axis=0)
    squares = jnp.zeros((channels, LANES), F32)
    for tile in range(T_DEC // LANES):
        start = tile * LANES * DECIM
        if tile == 0:
            raw = jnp.concatenate([tail_ref[...], records_ref[:, : SPAN - LANES]], axis=1)
        else:
            raw = records_ref[:, start - LANES : start - LANES + SPAN]
        out = lax.dot_general(raw, weights, NT, preferred_element_type=F32)
        value = out[:, :LANES] + (out[:, LANES : 2 * LANES] + out[:, 2 * LANES :])
        filtered[:, tile * LANES : (tile + 1) * LANES] = value
        squares = squares + value * value
    energy = jnp.sqrt(jnp.sum(squares, axis=1, keepdims=True) * (1.0 / T_DEC) + 1e-06)
    inverse = 1.0 / energy
    for tile in range(T_DEC // LANES):
        lanes = slice(tile * LANES, (tile + 1) * LANES)
        filtered[:, lanes] = filtered[:, lanes] * inverse
    for chunk, ref in enumerate(chunk_refs):
        ref[...] = filtered[:, chunk * T_CHUNK : (chunk + 1) * T_CHUNK].astype(BF16)
    me = lax.axis_index("win")
    for step, ref in enumerate(row_refs):
        owner = lax.rem(me + step, win)
        first = pl.multiple_of(owner * rows, rows)
        ref[...] = filtered[pl.ds(first, rows), :].astype(BF16)


def whiten(records, before, fir_taps):
    channels = records.shape[0]
    win = lax.axis_size("win")
    rows = channels // win
    return pl.pallas_call(
        functools.partial(whiten_kernel, win, rows),
        out_shape=[jax.ShapeDtypeStruct((channels, T_CHUNK), BF16)] * CHUNKS
        + [jax.ShapeDtypeStruct((rows, T_DEC), BF16)] * win,
        in_specs=[VMEM_SPEC] * 3,
        out_specs=[VMEM_SPEC] * (CHUNKS + win),
        scratch_shapes=[VMEM((8, SPAN), F32), VMEM((channels, T_DEC), F32)],
        name="whiten",
    )(before, records, fir_taps.reshape(1, TAPS))


def lags_kernel(own_ref, lags_ref, last_ref, padded):
    rows = own_ref.shape[0]
    padded[...] = jnp.zeros_like(padded)
    padded[:, LANES : LANES + T_DEC] = own_ref[...].astype(F32)
    width = T_DEC + 2 * LANES
    last_ref[...] = padded[:, LANES - MAXLAG : LANES - MAXLAG + T_DEC].astype(BF16)

    def one(i, carry):
        line = jnp.broadcast_to(padded[pl.ds(i, 1), :], (8, width))
        parts = []
        for tile in range(LAG_ROWS // 8):
            by = (8 * tile - MAXLAG) % width
            parts.append(pltpu.roll(line, by, 1, stride=1, stride_axis=0)[:, LANES : LANES + T_DEC])
        first = pl.multiple_of(i * LAG_ROWS, LAG_ROWS)
        lags_ref[pl.ds(first, LAG_ROWS), :] = jnp.concatenate(parts, axis=0).astype(BF16)
        return carry

    lax.fori_loop(0, rows, one, 0)


def lay_out_lags(own):
    rows = own.shape[0]
    return pl.pallas_call(
        lags_kernel,
        out_shape=[
            jax.ShapeDtypeStruct((rows * LAG_ROWS, T_DEC), BF16),
            jax.ShapeDtypeStruct((rows, T_DEC), BF16),
        ],
        in_specs=[VMEM_SPEC],
        out_specs=[VMEM_SPEC] * 2,
        scratch_shapes=[VMEM((rows, T_DEC + 2 * LANES), F32)],
        cost_estimate=pl.CostEstimate(flops=0, bytes_accessed=16 << 20, transcendentals=0),
        name="lags",
    )(own)


def pick_kernel(reach, own_offsets, core_offsets, *refs):
    blocks = refs[: reach + 1]
    keep_ref, send_ref = refs[reach + 1 :]
    core = lax.rem(lax.axis_index("chan"), 2)
    for offsets, lane, out_ref in ((own_offsets, core, keep_ref), (core_offsets, 1 - core, send_ref)):
        for slot in range(offsets.shape[1]):
            chip = jnp.minimum((lane + offsets[0, slot]) >> 1, reach // 2)
            for place in range(reach + 1):

                @pl.when(chip == place - reach // 2)
                def _(place=place, slot=slot, out_ref=out_ref):
                    out_ref[slot] = blocks[place][...]


def pick(reach, own_offsets, core_offsets, blocks):
    slots = own_offsets.shape[1]
    shape = jax.ShapeDtypeStruct((slots,) + blocks[0].shape, BF16)
    return pl.pallas_call(
        functools.partial(pick_kernel, reach),
        out_shape=[shape] * 2,
        in_specs=[SMEM_SPEC] * 2 + [VMEM_SPEC] * (reach + 1),
        out_specs=[VMEM_SPEC] * 2,
        name="pick",
    )(own_offsets, core_offsets, *blocks)


def merge_kernel(offsets, keep_ref, got_ref, out_ref):
    for slot in range(offsets.shape[1]):
        odd = (offsets[0, slot] & 1) == 1

        @pl.when(odd)
        def _(slot=slot):
            out_ref[slot] = got_ref[slot]

        @pl.when(jnp.logical_not(odd))
        def _(slot=slot):
            out_ref[slot] = keep_ref[slot]


def merge(offsets, keep, got):
    return pl.pallas_call(
        merge_kernel,
        out_shape=jax.ShapeDtypeStruct(keep.shape, BF16),
        in_specs=[SMEM_SPEC] + [VMEM_SPEC] * 2,
        out_specs=VMEM_SPEC,
        name="merge",
    )(offsets, keep, got)


GROUP = 8


def correlate_kernel(reach, factor, win, offsets, *refs):
    lags = refs[: 2 * win : 2]
    lasts = refs[1 : 2 * win : 2]
    others = refs[2 * win : 2 * win + win * CHUNKS]
    out_ref, stage, sems = refs[2 * win + win * CHUNKS :]
    rows = lasts[0].shape[0]
    slots = offsets.shape[1]
    steps = rows // GROUP

    def total(pick_rows):
        acc = None
        for w in range(win):
            for chunk in range(CHUNKS):
                other = others[w * CHUNKS + chunk]
                other = other[...].reshape(slots * LANES, T_CHUNK)
                part = lax.dot_general(
                    pick_rows(w, slice(chunk * T_CHUNK, (chunk + 1) * T_CHUNK)),
                    other,
                    NT,
                    preferred_element_type=F32,
                )
                acc = part if acc is None else acc + part
        return acc * factor

    last = total(lambda w, t: lasts[w][:, t])
    listed = [offsets[0, slot] <= reach for slot in range(slots)]

    def out_copy(step, place):
        first = step * GROUP
        return pltpu.make_async_copy(stage.at[place], out_ref.at[pl.ds(first, GROUP)], sems.at[place])

    for step in range(steps):
        place = step % 2
        first = step * GROUP
        acc = total(lambda w, t: lags[w][first * LAG_ROWS : (first + GROUP) * LAG_ROWS, t])
        if step >= 2:
            out_copy(step - 2, place).wait()
        for slot in range(slots):
            lanes = slice(slot * LANES, (slot + 1) * LANES)
            value = jnp.where(listed[slot], acc[:, lanes], 0.0)
            stage[place, :, slot, 0:LAG_ROWS, :] = value.reshape(GROUP, LAG_ROWS, LANES)
            tail = jnp.where(listed[slot], last[first : first + GROUP, lanes], 0.0)
            stage[place, :, slot, LAG_ROWS, :] = tail
        out_copy(step, place).start()
    for step in range(max(0, steps - 2), steps):
        out_copy(step, step % 2).wait()


def correlate(reach, factor, offsets, lags, others):
    win = len(lags)
    slots = offsets.shape[1]
    rows = lags[0][1].shape[0]
    operands = [array for pair in lags for array in pair] + others
    return pl.pallas_call(
        functools.partial(correlate_kernel, reach, factor, win),
        out_shape=jax.ShapeDtypeStruct((rows, slots, LAGS, LANES), F32),
        in_specs=[SMEM_SPEC] + [VMEM_SPEC] * len(operands),
        out_specs=pl.BlockSpec(memory_space=pl.ANY),
        scratch_shapes=[
            VMEM((2, GROUP, slots, LAGS, LANES), F32),
            pltpu.SemaphoreType.DMA((2,)),
        ],
        name="correlate",
    )(offsets, *operands)


def body(records, fir_taps, pair_offsets):
    win = lax.axis_size("win")
    reach = lax.axis_size("chan") // 4
    factor = 1.0 / math.sqrt(T_DEC * win)

    tail = records[:, records.shape[1] - LANES :]
    before = lax.ppermute(tail, "win", [(i, i + 1) for i in range(win - 1)])
    core_offsets = flip_core(pair_offsets)
    outs = whiten(records, before, fir_taps)
    chunks, row_parts = outs[:CHUNKS], outs[CHUNKS:]

    places = []
    for chunk in range(CHUNKS):
        found = {0: chunks[chunk]}
        for by in range(reach, 0, -2):
            found[-by] = shift(chunks[chunk], "chan", by)
            found[by] = shift(chunks[chunk], "chan", -by)
        places.append([found[by] for by in range(-reach, reach + 1, 2)])
    own = [row_parts[0]] + [shift(row_parts[step], "win", step) for step in range(1, win)]
    lags = [lay_out_lags(part) for part in own]

    others = [[None] * CHUNKS for _ in range(win)]
    for chunk in range(CHUNKS):
        keep, send = pick(reach, pair_offsets, core_offsets, places[chunk])
        chosen = merge(pair_offsets, keep, flip_core(send))
        others[0][chunk] = chosen
        for step in range(1, win):
            others[step][chunk] = shift(chosen, "win", step)
    flat = [array for group in others for array in group]
    return correlate(reach, factor, pair_offsets, lags, flat)


def solution(mesh):
    placed = (P("chan", "win"), P(), P("chan", None))
    return jax.shard_map(
        body,
        mesh=mesh,
        in_specs=placed,
        out_specs=P(("chan", "win"), None, None, None),
        check_vma=False,
    )
```

time: 416 us -> 82.4 us (0.20)
  waiting for transfers between devices: 147 us -> 9.72 us
  local copies, waits for them, and re-layouts: 115 us -> 10.3 us
  other arithmetic: 64.5 us -> 0 us
  starting transfers between devices: 62.9 us -> 22.5 us
  Pallas kernels: 0 us -> 39.5 us
  between operations: 15.2 us -> 0.11 us
  loops' own time: 6.81 us -> 0 us
    unnamed x2 -> x0, waiting for transfers between devices: 112 us -> none
    slice x10 -> x1, local copies, waits for them, and re-layouts: 95.6 us -> 0.76 us  [body(): tail = records[:, records.shape[1] - LANES:]]
    reduce_sum x1 -> x0, other arithmetic: 48.7 us -> none  [whiten_local(): jnp.mean(filtered * filtered, axis=2, keepdims=True) + 1e-06]
    ppermute x10 -> x15, starting transfers between devices: 62.9 us -> 22.5 us  [the longest x11 17.6 us: shift(): return lax.ppermute(x, axis, [(i, (i + by) % n) for i in range(n)])]
    pallas_call x0 -> x8, Pallas kernels: none -> 39.5 us  [the longest x2 18.3 us: lay_out_lags(): pl.pallas_call(lags_kernel, out_shape=[jax.ShapeDtypeStruct((rows * LAG_R...]
    ppermute x10 -> x15, waiting for transfers between devices: 34.5 us -> 9.72 us  [the longest x11 7.82 us: shift(): return lax.ppermute(x, axis, [(i, (i + by) % n) for i in range(n)])]
    while x9 -> x0, local copies, waits for them, and re-layouts: 7.93 us -> none  [the longest x1 7.79 us: body(): lax.fori_loop(1, 2 * reach + 1, one_side, (totals, first_block))]
    scatter-add x2 -> x0, other arithmetic: 6.93 us -> none  [add_pair(): current = current.at[:, slot_id].add(weights[slot_id] * result)]
  transfers between devices with their start and end apart: 11 -> 15, of which waited for: 10 -> 6; matrix products, arithmetic and copies ran while one was open for 3% -> 0% of each run, Pallas kernels for 0% -> 32%
where the time goes in v1:
time: 82.4 us; the launch traced here: 82.1 us
  Pallas kernels  39.5 us (48%)
  starting transfers between devices  22.5 us (27%)
  local copies, waits for them, and re-layouts  10.3 us (12%)
  waiting for transfers between devices  9.72 us (12%)
    pallas_call x2, Pallas kernels, lay_out_lags(): pl.pallas_call(lags_kernel, out_shape=[jax.ShapeDtypeStruct((rows * LAG_R...  18.3 us
    ppermute x11, starting transfers between devices, shift(): return lax.ppermute(x, axis, [(i, (i + by) % n) for i in range(n)])  17.6 us
    pallas_call x1, Pallas kernels, correlate(): pl.pallas_call(functools.partial(correlate_kernel, reach, factor, win), o...  9.91 us
    ppermute x11, waiting for transfers between devices, shift(): return lax.ppermute(x, axis, [(i, (i + by) % n) for i in range(n)])  7.82 us
    unnamed x30, local copies, waits for them, and re-layouts  5.34 us
    ppermute x1, starting transfers between devices, body(): before = lax.ppermute(tail, 'win', [(i, i + 1) for i in range(win - 1)])  4.86 us
    pallas_call x2, Pallas kernels, pick(): pl.pallas_call(functools.partial(pick_kernel, reach), out_shape=[shape] *...  4.22 us
    pallas_call x1, local copies, waits for them, and re-layouts, correlate(): pl.pallas_call(functools.partial(correlate_kernel, reach, factor, win), o...  4.19 us
  transfers between devices with their start and end apart: 15, of which 6 were waited for; matrix products, arithmetic and copies ran while one was open for 0% of the time, Pallas kernels for 32%

profile of v1, /device:TPU:0, one launch (start us, length us, event | category | flops | bytes accessed | tf_op | source)
XLA Modules:
  0.0 82.1 jit_solution(12652287439521320597)
XLA Ops:
  0.0 0.8 slice.3
  0.8 4.9 %collective-permute-start = (bf16[128,128]{1,0:T(8,128)(2,1)S(1)}, bf16[128,128]{1,0:T(8,128)(2,1)S(1)}, u32[]{:S(2)}, u32[]{:S(2)}) collective-permute-start(bf16[128,128]{1,0:T(8,128)(2,1)S(1)} %slice.3), channel_id=1, source_target_pairs={{0,1},{2,3},{4,5},{6,7},{8,9},{10,11},{12,13},{14,15},{16,17},{18,... | collective-permute-start | bytes 98312 | tf_op jit(solution)/shard_map/ppermute | solution.py:254
  5.6 1.6 %collective-permute-done.tail_ref = bf16[128,128]{1,0:T(8,128)(2,1)S(1)} collective-permute-done((bf16[128,128]{1,0:T(8,128)(2,1)S(1)}, bf16[128,128]{1,0:T(8,128)(2,1)S(1)}, u32[]{:S(2)}, u32[]{:S(2)}) %collective-permute-start) | collective-permute-done | bytes 32800 | tf_op jit(solution)/shard_map/ppermute | solution.py:254
  7.2 0.6 copy-done.13
  7.8 3.5 %whiten.1 = (bf16[128,512]{1,0:T(8,128)(2,1)}, bf16[128,512]{1,0:T(8,128)(2,1)}, bf16[64,1024]{1,0:T(8,128)(2,1)}, bf16[64,1024]{1,0:T(8,128)(2,1)}) custom-call(bf16[128,128]{1,0:T(8,128)(2,1)} %copy-done.13, bf16[128,4096]{1,0:T(8,128)(2,1)} %records_ref.1, f32[1,64]{1,0:T(1,128)} %bitcast.1), custom_call_target="tpu_custom_call" | custom-call | tf_op jit(solution)/shard_map/whiten/pallas_call | solution.py:83
  11.3 3.6 %collective-permute-start.11 = (bf16[128,512]{1,0:T(8,128)(2,1)}, bf16[128,512]{1,0:T(8,128)(2,1)S(1)}, u32[]{:S(2)}, u32[]{:S(2)}) collective-permute-start(bf16[128,512]{1,0:T(8,128)(2,1)} %get-tuple-element.26.refs_2_), channel_id=1, source_target_pairs={{0,24},{2,26},{4,28},{6,30},{8,0},{10,2},{12,4},{14,6},{16,8},{18,... | collective-permute-start | bytes 393224 | tf_op jit(solution)/shard_map/ppermute | solution.py:32
  14.9 1.4 %collective-permute-start.10 = (bf16[128,512]{1,0:T(8,128)(2,1)}, bf16[128,512]{1,0:T(8,128)(2,1)S(1)}, u32[]{:S(2)}, u32[]{:S(2)}) collective-permute-start(bf16[128,512]{1,0:T(8,128)(2,1)} %get-tuple-element.26.refs_2_), channel_id=1, source_target_pairs={{0,28},{2,30},{4,0},{6,2},{8,4},{10,6},{12,8},{14,10},{16,12},{18,... | collective-permute-start | bytes 393224 | tf_op jit(solution)/shard_map/ppermute | solution.py:32
  16.3 0.6 collective-permute-start.9
  17.0 0.9 %collective-permute-start.8 = (bf16[128,512]{1,0:T(8,128)(2,1)}, bf16[128,512]{1,0:T(8,128)(2,1)S(1)}, u32[]{:S(2)}, u32[]{:S(2)}) collective-permute-start(bf16[128,512]{1,0:T(8,128)(2,1)} %get-tuple-element.26.refs_2_), channel_id=1, source_target_pairs={{0,8},{2,10},{4,12},{6,14},{8,16},{10,18},{12,20},{14,22},{16,24},... | collective-permute-start | bytes 393224 | tf_op jit(solution)/shard_map/ppermute | solution.py:32
  18.2 2.6 %collective-permute-start.6 = (bf16[128,512]{1,0:T(8,128)(2,1)}, bf16[128,512]{1,0:T(8,128)(2,1)S(1)}, u32[]{:S(2)}, u32[]{:S(2)}) collective-permute-start(bf16[128,512]{1,0:T(8,128)(2,1)} %get-tuple-element.23.refs_2_), channel_id=1, source_target_pairs={{0,24},{2,26},{4,28},{6,30},{8,0},{10,2},{12,4},{14,6},{16,8},{18,... | collective-permute-start | bytes 393224 | tf_op jit(solution)/shard_map/ppermute | solution.py:32
  20.8 3.2 %collective-permute-start.5 = (bf16[128,512]{1,0:T(8,128)(2,1)}, bf16[128,512]{1,0:T(8,128)(2,1)S(1)}, u32[]{:S(2)}, u32[]{:S(2)}) collective-permute-start(bf16[128,512]{1,0:T(8,128)(2,1)} %get-tuple-element.23.refs_2_), channel_id=1, source_target_pairs={{0,28},{2,30},{4,0},{6,2},{8,4},{10,6},{12,8},{14,10},{16,12},{18,... | collective-permute-start | bytes 393224 | tf_op jit(solution)/shard_map/ppermute | solution.py:32
  24.0 0.6 collective-permute-done.9.refs_1_
  24.6 0.7 collective-permute-start.3
  25.4 0.6 copy-done.10
  26.0 2.1 %pick.3 = (bf16[2,128,512]{2,1,0:T(8,128)(2,1)}, bf16[2,128,512]{2,1,0:T(8,128)(2,1)}) custom-call(s32[1,2]{1,0:T(1,128)} %offsets.5, s32[1,2]{1,0:T(1,128)} %copy-done.14, bf16[128,512]{1,0:T(8,128)(2,1)} %copy-done.10, bf16[128,512]{1,0:T(8,128)(2,1)} %copy-done.8, bf16[128,512]{1,0:T(8,128)(2,1)} %get-tuple-element.26.refs_2_, ...), custom_call_target="tpu_custom_call" | custom-call | tf_op jit(solution)/shard_map/pick/pallas_call | solution.py:147
  28.2 1.3 %collective-permute-done.5.refs_3_ = bf16[128,512]{1,0:T(8,128)(2,1)S(1)} collective-permute-done((bf16[128,512]{1,0:T(8,128)(2,1)}, bf16[128,512]{1,0:T(8,128)(2,1)S(1)}, u32[]{:S(2)}, u32[]{:S(2)}) %collective-permute-start.5) | collective-permute-done | bytes 131104 | tf_op jit(solution)/shard_map/ppermute | solution.py:32
  29.5 3.8 %collective-permute-done.4.refs_1_ = bf16[128,512]{1,0:T(8,128)(2,1)S(1)} collective-permute-done((bf16[128,512]{1,0:T(8,128)(2,1)}, bf16[128,512]{1,0:T(8,128)(2,1)S(1)}, u32[]{:S(2)}, u32[]{:S(2)}) %collective-permute-start.4) | collective-permute-done | bytes 131104 | tf_op jit(solution)/shard_map/ppermute | solution.py:32
  34.0 0.6 copy-done.11
  34.6 2.1 %pick.2 = (bf16[2,128,512]{2,1,0:T(8,128)(2,1)}, bf16[2,128,512]{2,1,0:T(8,128)(2,1)}) custom-call(s32[1,2]{1,0:T(1,128)} %offsets.5, s32[1,2]{1,0:T(1,128)} %copy-done.14, bf16[128,512]{1,0:T(8,128)(2,1)} %copy-done.11, bf16[128,512]{1,0:T(8,128)(2,1)} %copy-done.9, bf16[128,512]{1,0:T(8,128)(2,1)} %get-tuple-element.23.refs_2_, ...), custom_call_target="tpu_custom_call" | custom-call | tf_op jit(solution)/shard_map/pick/pallas_call | solution.py:147
  36.7 0.7 copy-done.2
  37.4 1.8 %merge.3.refs_5_ = bf16[2,128,512]{2,1,0:T(8,128)(2,1)} custom-call(s32[1,2]{1,0:T(1,128)} %offsets.5, bf16[2,128,512]{2,1,0:T(8,128)(2,1)} %get-tuple-element.27.keep_ref, bf16[2,128,512]{2,1,0:T(8,128)(2,1)} %copy-done.2), custom_call_target="tpu_custom_call" | custom-call | tf_op jit(solution)/shard_map/merge/pallas_call | solution.py:170
  39.2 2.5 %collective-permute-start.14 = (bf16[2,128,512]{2,1,0:T(8,128)(2,1)}, bf16[2,128,512]{2,1,0:T(8,128)(2,1)S(1)}, u32[]{:S(2)}, u32[]{:S(2)}) collective-permute-start(bf16[2,128,512]{2,1,0:T(8,128)(2,1)} %merge.3.refs_5_), channel_id=1, source_target_pairs={{0,1},{1,0},{2,3},{3,2},{4,5},{5,4},{6,7},{7,6},{8,9},{9,8},{10,11... | collective-permute-start | bytes 786440 | tf_op jit(solution)/shard_map/ppermute | solution.py:32
  41.7 0.7 copy-done.3
  42.4 1.8 %merge.2.refs_4_ = bf16[2,128,512]{2,1,0:T(8,128)(2,1)} custom-call(s32[1,2]{1,0:T(1,128)} %offsets.5, bf16[2,128,512]{2,1,0:T(8,128)(2,1)} %get-tuple-element.24.keep_ref, bf16[2,128,512]{2,1,0:T(8,128)(2,1)} %copy-done.3), custom_call_target="tpu_custom_call" | custom-call | tf_op jit(solution)/shard_map/merge/pallas_call | solution.py:170
  44.2 2.0 %collective-permute-start.1 = (bf16[64,1024]{1,0:T(8,128)(2,1)}, bf16[64,1024]{1,0:T(8,128)(2,1)S(1)}, u32[]{:S(2)}, u32[]{:S(2)}) collective-permute-start(bf16[64,1024]{1,0:T(8,128)(2,1)} %get-tuple-element.20), channel_id=1, source_target_pairs={{0,1},{1,0},{2,3},{3,2},{4,5},{5,4},{6,7},{7,6},{8,9},{9,8},{10,11... | collective-permute-start | bytes 393224 | tf_op jit(solution)/shard_map/ppermute | solution.py:32
  46.2 9.1 %lags.2 = (bf16[2048,1024]{1,0:T(8,128)(2,1)}, bf16[64,1024]{1,0:T(8,128)(2,1)}) custom-call(bf16[64,1024]{1,0:T(8,128)(2,1)} %get-tuple-element.17.own_ref), custom_call_target="tpu_custom_call" | custom-call | bytes 16777216 | tf_op jit(solution)/shard_map/lags/pallas_call | solution.py:116
  55.3 2.0 %collective-permute-done.1.own_ref = bf16[64,1024]{1,0:T(8,128)(2,1)S(1)} collective-permute-done((bf16[64,1024]{1,0:T(8,128)(2,1)}, bf16[64,1024]{1,0:T(8,128)(2,1)S(1)}, u32[]{:S(2)}, u32[]{:S(2)}) %collective-permute-start.1) | collective-permute-done | bytes 131104 | tf_op jit(solution)/shard_map/ppermute | solution.py:32
  57.3 0.7 copy-done.12
  58.0 9.2 %lags.3 = (bf16[2048,1024]{1,0:T(8,128)(2,1)}, bf16[64,1024]{1,0:T(8,128)(2,1)}) custom-call(bf16[64,1024]{1,0:T(8,128)(2,1)} %copy-done.12), custom_call_target="tpu_custom_call" | custom-call | bytes 16777216 | tf_op jit(solution)/shard_map/lags/pallas_call | solution.py:116
  67.2 0.7 copy-done
  67.9 9.9 %correlate.1 = f32[64,2,33,128]{3,2,1,0:T(8,128)} custom-call(s32[1,2]{1,0:T(1,128)} %offsets.5, bf16[2048,1024]{1,0:T(8,128)(2,1)} %get-tuple-element.18.refs_0_, bf16[64,1024]{1,0:T(8,128)(2,1)} %get-tuple-element.19.refs_1_, bf16[2048,1024]{1,0:T(8,128)(2,1)} %get-tuple-element.21.refs_2_, bf16[64,1024]{1,0:T(8,128)(2,1)} %get-tuple-element.22.refs_3_, ...), custom_call_target="tpu_custom_call" | custom-call | tf_op jit(solution)/shard_map/correlate/pallas_call | solution.py:235
  77.9 4.2 %copy.4 = f32[64,2,33,128]{3,1,2,0:T(2,128)} copy(f32[64,2,33,128]{3,2,1,0:T(8,128)} %correlate.1) | data formatting | bytes 4325376 | tf_op jit(solution)/shard_map/correlate/pallas_call | solution.py:235
  (38 shorter events, 1.1 us)
Async XLA Ops:
  0.8 6.4 %collective-permute-start = (bf16[128,128]{1,0:T(8,128)(2,1)S(1)}, bf16[128,128]{1,0:T(8,128)(2,1)S(1)}, u32[]{:S(2)}, u32[]{:S(2)}) collective-permute-start(bf16[128,128]{1,0:T(8,128)(2,1)S(1)} %slice.3), channel_id=1, source_target_pairs={{0,1},{2,3},{4,5},{6,7},{8,9},{10,11},{12,13},{14,15},{16,17},{18,... | collective-permute-start | bytes 98312 | tf_op jit(solution)/shard_map/ppermute | solution.py:254
  7.2 0.6 copy-start.13
  11.3 9.5 %collective-permute-start.11 = (bf16[128,512]{1,0:T(8,128)(2,1)}, bf16[128,512]{1,0:T(8,128)(2,1)S(1)}, u32[]{:S(2)}, u32[]{:S(2)}) collective-permute-start(bf16[128,512]{1,0:T(8,128)(2,1)} %get-tuple-element.26.refs_2_), channel_id=1, source_target_pairs={{0,24},{2,26},{4,28},{6,30},{8,0},{10,2},{12,4},{14,6},{16,8},{18,... | collective-permute-start | bytes 393224 | tf_op jit(solution)/shard_map/ppermute | solution.py:32
  14.9 9.0 %collective-permute-start.10 = (bf16[128,512]{1,0:T(8,128)(2,1)}, bf16[128,512]{1,0:T(8,128)(2,1)S(1)}, u32[]{:S(2)}, u32[]{:S(2)}) collective-permute-start(bf16[128,512]{1,0:T(8,128)(2,1)} %get-tuple-element.26.refs_2_), channel_id=1, source_target_pairs={{0,28},{2,30},{4,0},{6,2},{8,4},{10,6},{12,8},{14,10},{16,12},{18,... | collective-permute-start | bytes 393224 | tf_op jit(solution)/shard_map/ppermute | solution.py:32
  16.3 8.3 %collective-permute-start.9 = (bf16[128,512]{1,0:T(8,128)(2,1)}, bf16[128,512]{1,0:T(8,128)(2,1)S(1)}, u32[]{:S(2)}, u32[]{:S(2)}) collective-permute-start(bf16[128,512]{1,0:T(8,128)(2,1)} %get-tuple-element.26.refs_2_), channel_id=1, source_target_pairs={{0,4},{2,6},{4,8},{6,10},{8,12},{10,14},{12,16},{14,18},{16,20},{1... | collective-permute-start | bytes 393224 | tf_op jit(solution)/shard_map/ppermute | solution.py:32
  17.0 1.3 %collective-permute-start.2 = (s32[1,2]{1,0:T(1,128)}, s32[1,2]{1,0:T(1,128)S(1)}, u32[]{:S(2)}, u32[]{:S(2)}) collective-permute-start(s32[1,2]{1,0:T(1,128)} %offsets.5), channel_id=1, source_target_pairs={{0,2},{2,0},{4,6},{6,4},{8,10},{10,8},{12,14},{14,12},{16,18},{18,... | collective-permute-start | bytes 32 | tf_op jit(solution)/shard_map/ppermute | solution.py:37
  17.0 8.4 %collective-permute-start.8 = (bf16[128,512]{1,0:T(8,128)(2,1)}, bf16[128,512]{1,0:T(8,128)(2,1)S(1)}, u32[]{:S(2)}, u32[]{:S(2)}) collective-permute-start(bf16[128,512]{1,0:T(8,128)(2,1)} %get-tuple-element.26.refs_2_), channel_id=1, source_target_pairs={{0,8},{2,10},{4,12},{6,14},{8,16},{10,18},{12,20},{14,22},{16,24},... | collective-permute-start | bytes 393224 | tf_op jit(solution)/shard_map/ppermute | solution.py:32
  18.2 7.1 %copy-start.14 = (s32[1,2]{1,0:T(1,128)}, s32[1,2]{1,0:T(1,128)S(1)}, u32[]{:S(2)}) copy-start(s32[1,2]{1,0:T(1,128)S(1)} %collective-permute-done.2.core_offsets) | copy-start | bytes 28
  18.2 9.9 %collective-permute-start.6 = (bf16[128,512]{1,0:T(8,128)(2,1)}, bf16[128,512]{1,0:T(8,128)(2,1)S(1)}, u32[]{:S(2)}, u32[]{:S(2)}) collective-permute-start(bf16[128,512]{1,0:T(8,128)(2,1)} %get-tuple-element.23.refs_2_), channel_id=1, source_target_pairs={{0,24},{2,26},{4,28},{6,30},{8,0},{10,2},{12,4},{14,6},{16,8},{18,... | collective-permute-start | bytes 393224 | tf_op jit(solution)/shard_map/ppermute | solution.py:32
  20.8 4.6 %copy-start.5 = (bf16[128,512]{1,0:T(8,128)(2,1)}, bf16[128,512]{1,0:T(8,128)(2,1)S(1)}, u32[]{:S(2)}) copy-start(bf16[128,512]{1,0:T(8,128)(2,1)S(1)} %collective-permute-done.11.refs_4_) | copy-start | bytes 393220
  20.8 8.7 %collective-permute-start.5 = (bf16[128,512]{1,0:T(8,128)(2,1)}, bf16[128,512]{1,0:T(8,128)(2,1)S(1)}, u32[]{:S(2)}, u32[]{:S(2)}) collective-permute-start(bf16[128,512]{1,0:T(8,128)(2,1)} %get-tuple-element.23.refs_2_), channel_id=1, source_target_pairs={{0,28},{2,30},{4,0},{6,2},{8,4},{10,6},{12,8},{14,10},{16,12},{18,... | collective-permute-start | bytes 393224 | tf_op jit(solution)/shard_map/ppermute | solution.py:32
  24.0 1.4 %copy-start.6 = (bf16[128,512]{1,0:T(8,128)(2,1)}, bf16[128,512]{1,0:T(8,128)(2,1)S(1)}, u32[]{:S(2)}) copy-start(bf16[128,512]{1,0:T(8,128)(2,1)S(1)} %collective-permute-done.10.refs_3_) | copy-start | bytes 393220
  24.0 9.3 %collective-permute-start.4 = (bf16[128,512]{1,0:T(8,128)(2,1)}, bf16[128,512]{1,0:T(8,128)(2,1)S(1)}, u32[]{:S(2)}, u32[]{:S(2)}) collective-permute-start(bf16[128,512]{1,0:T(8,128)(2,1)} %get-tuple-element.23.refs_2_), channel_id=1, source_target_pairs={{0,4},{2,6},{4,8},{6,10},{8,12},{10,14},{12,16},{14,18},{16,20},{1... | collective-permute-start | bytes 393224 | tf_op jit(solution)/shard_map/ppermute | solution.py:32
  24.6 0.8 copy-start.8
  24.6 8.7 %collective-permute-start.3 = (bf16[128,512]{1,0:T(8,128)(2,1)}, bf16[128,512]{1,0:T(8,128)(2,1)S(1)}, u32[]{:S(2)}, u32[]{:S(2)}) collective-permute-start(bf16[128,512]{1,0:T(8,128)(2,1)} %get-tuple-element.23.refs_2_), channel_id=1, source_target_pairs={{0,8},{2,10},{4,12},{6,14},{8,16},{10,18},{12,20},{14,22},{16,24},... | collective-permute-start | bytes 393224 | tf_op jit(solution)/shard_map/ppermute | solution.py:32
  25.4 0.7 copy-start.10
  28.2 8.6 %collective-permute-start.12 = (bf16[2,128,512]{2,1,0:T(8,128)(2,1)}, bf16[2,128,512]{2,1,0:T(8,128)(2,1)S(1)}, u32[]{:S(2)}, u32[]{:S(2)}) collective-permute-start(bf16[2,128,512]{2,1,0:T(8,128)(2,1)} %get-tuple-element.28), channel_id=1, source_target_pairs={{0,2},{2,0},{4,6},{6,4},{8,10},{10,8},{12,14},{14,12},{16,18},{18,... | collective-permute-start | bytes 786440 | tf_op jit(solution)/shard_map/ppermute | solution.py:37
  28.2 5.2 %copy-start.4 = (bf16[128,512]{1,0:T(8,128)(2,1)}, bf16[128,512]{1,0:T(8,128)(2,1)S(1)}, u32[]{:S(2)}) copy-start(bf16[128,512]{1,0:T(8,128)(2,1)S(1)} %collective-permute-done.6.refs_4_) | copy-start | bytes 393220
  29.5 3.9 %copy-start.7 = (bf16[128,512]{1,0:T(8,128)(2,1)}, bf16[128,512]{1,0:T(8,128)(2,1)S(1)}, u32[]{:S(2)}) copy-start(bf16[128,512]{1,0:T(8,128)(2,1)S(1)} %collective-permute-done.5.refs_3_) | copy-start | bytes 393220
  33.3 0.7 copy-start.9
  34.0 0.6 copy-start.11
  36.7 5.0 %collective-permute-start.7 = (bf16[2,128,512]{2,1,0:T(8,128)(2,1)}, bf16[2,128,512]{2,1,0:T(8,128)(2,1)S(1)}, u32[]{:S(2)}, u32[]{:S(2)}) collective-permute-start(bf16[2,128,512]{2,1,0:T(8,128)(2,1)} %get-tuple-element.25), channel_id=1, source_target_pairs={{0,2},{2,0},{4,6},{6,4},{8,10},{10,8},{12,14},{14,12},{16,18},{18,... | collective-permute-start | bytes 786440 | tf_op jit(solution)/shard_map/ppermute | solution.py:37
  36.7 0.7 copy-start.2
  39.2 28.0 %collective-permute-start.14 = (bf16[2,128,512]{2,1,0:T(8,128)(2,1)}, bf16[2,128,512]{2,1,0:T(8,128)(2,1)S(1)}, u32[]{:S(2)}, u32[]{:S(2)}) collective-permute-start(bf16[2,128,512]{2,1,0:T(8,128)(2,1)} %merge.3.refs_5_), channel_id=1, source_target_pairs={{0,1},{1,0},{2,3},{3,2},{4,5},{5,4},{6,7},{7,6},{8,9},{9,8},{10,11... | collective-permute-start | bytes 786440 | tf_op jit(solution)/shard_map/ppermute | solution.py:32
  41.7 0.7 copy-start.3
  44.2 23.0 %collective-permute-start.13 = (bf16[2,128,512]{2,1,0:T(8,128)(2,1)}, bf16[2,128,512]{2,1,0:T(8,128)(2,1)S(1)}, u32[]{:S(2)}, u32[]{:S(2)}) collective-permute-start(bf16[2,128,512]{2,1,0:T(8,128)(2,1)} %merge.2.refs_4_), channel_id=1, source_target_pairs={{0,1},{1,0},{2,3},{3,2},{4,5},{5,4},{6,7},{7,6},{8,9},{9,8},{10,11... | collective-permute-start | bytes 786440 | tf_op jit(solution)/shard_map/ppermute | solution.py:32
  44.2 13.1 %collective-permute-start.1 = (bf16[64,1024]{1,0:T(8,128)(2,1)}, bf16[64,1024]{1,0:T(8,128)(2,1)S(1)}, u32[]{:S(2)}, u32[]{:S(2)}) collective-permute-start(bf16[64,1024]{1,0:T(8,128)(2,1)} %get-tuple-element.20), channel_id=1, source_target_pairs={{0,1},{1,0},{2,3},{3,2},{4,5},{5,4},{6,7},{7,6},{8,9},{9,8},{10,11... | collective-permute-start | bytes 393224 | tf_op jit(solution)/shard_map/ppermute | solution.py:32
  57.3 0.7 copy-start.12
  67.2 0.7 copy-start
  67.2 0.8 copy-start.1

commit v2 on v1

--- a/solution.py
+++ b/solution.py
@@ -18,7 +18,7 @@
 SPAN = LANES * DECIM + LANES
 CHUNKS = 2
 T_CHUNK = T_DEC // CHUNKS
-LAG_ROWS = 32
+GROUP = 16
 VMEM = pltpu.VMEM
 F32 = jnp.float32
 BF16 = jnp.bfloat16
@@ -87,42 +87,35 @@
         in_specs=[VMEM_SPEC] * 3,
         out_specs=[VMEM_SPEC] * (CHUNKS + win),
         scratch_shapes=[VMEM((8, SPAN), F32), VMEM((channels, T_DEC), F32)],
+        compiler_params=pltpu.CompilerParams(vmem_limit_bytes=8 << 20),
         name="whiten",
     )(before, records, fir_taps.reshape(1, TAPS))
 
 
-def lags_kernel(own_ref, lags_ref, last_ref, padded):
+def lags_kernel(own_ref, lags_ref, padded):
     rows = own_ref.shape[0]
-    padded[...] = jnp.zeros_like(padded)
-    padded[:, LANES : LANES + T_DEC] = own_ref[...].astype(F32)
-    width = T_DEC + 2 * LANES
-    last_ref[...] = padded[:, LANES - MAXLAG : LANES - MAXLAG + T_DEC].astype(BF16)
-
-    def one(i, carry):
-        line = jnp.broadcast_to(padded[pl.ds(i, 1), :], (8, width))
-        parts = []
-        for tile in range(LAG_ROWS // 8):
-            by = (8 * tile - MAXLAG) % width
-            parts.append(pltpu.roll(line, by, 1, stride=1, stride_axis=0)[:, LANES : LANES + T_DEC])
-        first = pl.multiple_of(i * LAG_ROWS, LAG_ROWS)
-        lags_ref[pl.ds(first, LAG_ROWS), :] = jnp.concatenate(parts, axis=0).astype(BF16)
-        return carry
-
-    lax.fori_loop(0, rows, one, 0)
+    zeros = jnp.zeros((rows, LANES), BF16)
+    padded[:, :LANES] = zeros
+    padded[:, LANES + T_DEC :] = zeros
+    padded[:, LANES : LANES + T_DEC] = own_ref[...]
+    for group in range(rows // GROUP):
+        block = padded[group * GROUP : (group + 1) * GROUP, :]
+        for lag in range(LAGS):
+            first = LANES + MAXLAG - lag
+            row = (group * LAGS + lag) * GROUP
+            lags_ref[row : row + GROUP, :] = block[:, first : first + T_DEC]
 
 
 def lay_out_lags(own):
     rows = own.shape[0]
     return pl.pallas_call(
         lags_kernel,
-        out_shape=[
-            jax.ShapeDtypeStruct((rows * LAG_ROWS, T_DEC), BF16),
-            jax.ShapeDtypeStruct((rows, T_DEC), BF16),
-        ],
+        out_shape=jax.ShapeDtypeStruct((rows * LAGS, T_DEC), BF16),
         in_specs=[VMEM_SPEC],
-        out_specs=[VMEM_SPEC] * 2,
-        scratch_shapes=[VMEM((rows, T_DEC + 2 * LANES), F32)],
-        cost_estimate=pl.CostEstimate(flops=0, bytes_accessed=16 << 20, transcendentals=0),
+        out_specs=VMEM_SPEC,
+        scratch_shapes=[VMEM((rows, T_DEC + 2 * LANES), BF16)],
+        compiler_params=pltpu.CompilerParams(vmem_limit_bytes=8 << 20),
+        cost_estimate=pl.CostEstimate(flops=0, bytes_accessed=8 << 20, transcendentals=0),
         name="lags",
     )(own)
 
@@ -149,6 +142,7 @@
         out_shape=[shape] * 2,
         in_specs=[SMEM_SPEC] * 2 + [VMEM_SPEC] * (reach + 1),
         out_specs=[VMEM_SPEC] * 2,
+        compiler_params=pltpu.CompilerParams(vmem_limit_bytes=4 << 20),
         name="pick",
     )(own_offsets, core_offsets, *blocks)
 
@@ -172,77 +166,67 @@
         out_shape=jax.ShapeDtypeStruct(keep.shape, BF16),
         in_specs=[SMEM_SPEC] + [VMEM_SPEC] * 2,
         out_specs=VMEM_SPEC,
+        compiler_params=pltpu.CompilerParams(vmem_limit_bytes=4 << 20),
         name="merge",
     )(offsets, keep, got)
 
 
-GROUP = 8
-
-
 def correlate_kernel(reach, factor, win, offsets, *refs):
-    lags = refs[: 2 * win : 2]
-    lasts = refs[1 : 2 * win : 2]
-    others = refs[2 * win : 2 * win + win * CHUNKS]
-    out_ref, stage, sems = refs[2 * win + win * CHUNKS :]
-    rows = lasts[0].shape[0]
+    lags = refs[:win]
+    others = refs[win : win + win * CHUNKS]
+    out_ref, stage, sems = refs[win + win * CHUNKS :]
     slots = offsets.shape[1]
-    steps = rows // GROUP
-
-    def total(pick_rows):
+    block = GROUP * LAGS
+    groups = lags[0].shape[0] // block
+    stride = LAGS * slots
+    listed = [offsets[0, slot] <= reach for slot in range(slots)]
+
+    def out_copy(group):
+        rows = pl.ds(group * block * slots, block * slots)
+        return pltpu.make_async_copy(stage.at[rows], out_ref.at[rows], sems.at[group])
+
+    for group in range(groups):
         acc = None
         for w in range(win):
             for chunk in range(CHUNKS):
-                other = others[w * CHUNKS + chunk]
-                other = other[...].reshape(slots * LANES, T_CHUNK)
                 part = lax.dot_general(
-                    pick_rows(w, slice(chunk * T_CHUNK, (chunk + 1) * T_CHUNK)),
-                    other,
+                    lags[w][group * block : (group + 1) * block, chunk * T_CHUNK : (chunk + 1) * T_CHUNK],
+                    others[w * CHUNKS + chunk][...].reshape(slots * LANES, T_CHUNK),
                     NT,
                     preferred_element_type=F32,
                 )
                 acc = part if acc is None else acc + part
-        return acc * factor
-
-    last = total(lambda w, t: lasts[w][:, t])
-    listed = [offsets[0, slot] <= reach for slot in range(slots)]
-
-    def out_copy(step, place):
-        first = step * GROUP
-        return pltpu.make_async_copy(stage.at[place], out_ref.at[pl.ds(first, GROUP)], sems.at[place])
-
-    for step in range(steps):
-        place = step % 2
-        first = step * GROUP
-        acc = total(lambda w, t: lags[w][first * LAG_ROWS : (first + GROUP) * LAG_ROWS, t])
-        if step >= 2:
-            out_copy(step - 2, place).wait()
         for slot in range(slots):
-            lanes = slice(slot * LANES, (slot + 1) * LANES)
-            value = jnp.where(listed[slot], acc[:, lanes], 0.0)
-            stage[place, :, slot, 0:LAG_ROWS, :] = value.reshape(GROUP, LAG_ROWS, LANES)
-            tail = jnp.where(listed[slot], last[first : first + GROUP, lanes], 0.0)
-            stage[place, :, slot, LAG_ROWS, :] = tail
-        out_copy(step, place).start()
-    for step in range(max(0, steps - 2), steps):
-        out_copy(step, step % 2).wait()
+            scaled = acc[:, slot * LANES : (slot + 1) * LANES] * factor
+            value = jnp.where(listed[slot], scaled, 0.0)
+            for lag in range(LAGS):
+                for half in range(GROUP // 8):
+                    row = lag * GROUP + half * 8
+                    first = (group * GROUP + half * 8) * stride + lag * slots + slot
+                    stage[pl.ds(first, 8, stride=stride), :] = value[row : row + 8, :]
+        out_copy(group).start()
+    for group in range(groups):
+        out_copy(group).wait()
 
 
 def correlate(reach, factor, offsets, lags, others):
     win = len(lags)
     slots = offsets.shape[1]
-    rows = lags[0][1].shape[0]
-    operands = [array for pair in lags for array in pair] + others
-    return pl.pallas_call(
+    total = lags[0].shape[0]
+    operands = lags + others
+    out = pl.pallas_call(
         functools.partial(correlate_kernel, reach, factor, win),
-        out_shape=jax.ShapeDtypeStruct((rows, slots, LAGS, LANES), F32),
+        out_shape=jax.ShapeDtypeStruct((total * slots, LANES), F32),
         in_specs=[SMEM_SPEC] + [VMEM_SPEC] * len(operands),
         out_specs=pl.BlockSpec(memory_space=pl.ANY),
         scratch_shapes=[
-            VMEM((2, GROUP, slots, LAGS, LANES), F32),
-            pltpu.SemaphoreType.DMA((2,)),
+            VMEM((total * slots, LANES), F32),
+            pltpu.SemaphoreType.DMA((total // (GROUP * LAGS),)),
         ],
+        compiler_params=pltpu.CompilerParams(vmem_limit_bytes=24 << 20),
         name="correlate",
     )(offsets, *operands)
+    return out.reshape(total // LAGS, LAGS, slots, LANES).transpose(0, 2, 1, 3)
 
 
 def body(records, fir_taps, pair_offsets):
@@ -266,6 +250,10 @@
     own = [row_parts[0]] + [shift(row_parts[step], "win", step) for step in range(1, win)]
     lags = [lay_out_lags(part) for part in own]
 
+    places[0], lags[0] = lax.optimization_barrier((places[0], lags[0]))
+    if CHUNKS > 1:
+        places[1], lags[1:] = lax.optimization_barrier((places[1], lags[1:]))
+
     others = [[None] * CHUNKS for _ in range(win)]
     for chunk in range(CHUNKS):
         keep, send = pick(reach, pair_offsets, core_offsets, places[chunk])

time: 82.4 us -> 53.9 us (0.65)
  Pallas kernels: 39.5 us -> 11 us
  waiting for transfers between devices: 9.72 us -> 17.9 us
  local copies, waits for them, and re-layouts: 10.3 us -> 2.64 us
    pallas_call x2, Pallas kernels: 18.3 us -> 2.85 us  [lay_out_lags(): pl.pallas_call(lags_kernel, out_shape=jax.ShapeDtypeStruct((rows * LAGS,...]
    ppermute x11, waiting for transfers between devices: 7.82 us -> 14.7 us  [shift(): return lax.ppermute(x, axis, [(i, (i + by) % n) for i in range(n)])]
    pallas_call x1, Pallas kernels: 9.91 us -> 4.09 us  [correlate(): pl.pallas_call(functools.partial(correlate_kernel, reach, factor, win), o...]
    pallas_call x1 -> x0, local copies, waits for them, and re-layouts: 4.19 us -> none  [correlate(): pl.pallas_call(functools.partial(correlate_kernel, reach, factor, win), o...]
    unnamed x30 -> x6, local copies, waits for them, and re-layouts: 5.34 us -> 1.88 us
    pallas_call x2, Pallas kernels: 4.22 us -> 1.38 us  [pick(): pl.pallas_call(functools.partial(pick_kernel, reach), out_shape=[shape] *...]
    pallas_call x2, Pallas kernels: 3.55 us -> 1.15 us  [merge(): pl.pallas_call(merge_kernel, out_shape=jax.ShapeDtypeStruct(keep.shape, B...]
    pallas_call x1, Pallas kernels: 3.51 us -> 1.53 us  [whiten(): pl.pallas_call(functools.partial(whiten_kernel, win, rows), out_shape=[ja...]
  transfers between devices with their start and end apart: 15 -> 15, of which waited for: 6 -> 7; matrix products, arithmetic and copies ran while one was open for 0% -> 0% of each run, Pallas kernels for 32% -> 10%
where the time goes in v2:
time: 53.9 us; the launch traced here: 53.7 us
  starting transfers between devices  22 us (41%)
  waiting for transfers between devices  17.9 us (33%)
  Pallas kernels  11 us (20%)
  local copies, waits for them, and re-layouts  2.64 us (5%)
    ppermute x11, starting transfers between devices, shift(): return lax.ppermute(x, axis, [(i, (i + by) % n) for i in range(n)])  16.7 us
    ppermute x11, waiting for transfers between devices, shift(): return lax.ppermute(x, axis, [(i, (i + by) % n) for i in range(n)])  14.7 us
    ppermute x1, starting transfers between devices, body(): before = lax.ppermute(tail, 'win', [(i, i + 1) for i in range(win - 1)])  4.86 us
    pallas_call x1, Pallas kernels, correlate(): pl.pallas_call(functools.partial(correlate_kernel, reach, factor, win), o...  4.09 us
    pallas_call x2, Pallas kernels, lay_out_lags(): pl.pallas_call(lags_kernel, out_shape=jax.ShapeDtypeStruct((rows * LAGS,...  2.85 us
    unnamed x6, local copies, waits for them, and re-layouts  1.88 us
    ppermute x3, waiting for transfers between devices, flip_core(): return lax.ppermute(x, 'chan', [(i, i ^ 1) for i in range(n)])  1.63 us
    ppermute x1, waiting for transfers between devices, body(): before = lax.ppermute(tail, 'win', [(i, i + 1) for i in range(win - 1)])  1.58 us
  transfers between devices with their start and end apart: 15, of which 7 were waited for; matrix products, arithmetic and copies ran while one was open for 0% of the time, Pallas kernels for 10%

profile of v2, /device:TPU:0, one launch (start us, length us, event | category | flops | bytes accessed | tf_op | source)
XLA Modules:
  0.0 53.7 jit_solution(190986355628344349)
XLA Ops:
  0.0 0.8 %slice.3 = bf16[128,128]{1,0:T(8,128)(2,1)S(1)} slice(bf16[128,4096]{1,0:T(8,128)(2,1)} %records_ref.1), slice={[0:128], [3968:4096]} | slice | bytes 65536 | tf_op jit(solution)/shard_map/slice | solution.py:237
  0.8 4.9 %collective-permute-start = (bf16[128,128]{1,0:T(8,128)(2,1)S(1)}, bf16[128,128]{1,0:T(8,128)(2,1)S(1)}, u32[]{:S(2)}, u32[]{:S(2)}) collective-permute-start(bf16[128,128]{1,0:T(8,128)(2,1)S(1)} %slice.3), channel_id=1, source_target_pairs={{0,1},{2,3},{4,5},{6,7},{8,9},{10,11},{12,13},{14,15},{16,17},{18,... | collective-permute-start | bytes 98312 | tf_op jit(solution)/shard_map/ppermute | solution.py:238
  5.6 1.6 %collective-permute-done.tail_ref = bf16[128,128]{1,0:T(8,128)(2,1)S(1)} collective-permute-done((bf16[128,128]{1,0:T(8,128)(2,1)S(1)}, bf16[128,128]{1,0:T(8,128)(2,1)S(1)}, u32[]{:S(2)}, u32[]{:S(2)}) %collective-permute-start) | collective-permute-done | bytes 32800 | tf_op jit(solution)/shard_map/ppermute | solution.py:238
  7.2 1.2 %copy-done = bf16[128,4096]{1,0:T(8,128)(2,1)S(1)} copy-done((bf16[128,4096]{1,0:T(8,128)(2,1)S(1)}, bf16[128,4096]{1,0:T(8,128)(2,1)}, u32[]{:S(2)}) %copy-start) | copy-done | bytes 1048600
  8.4 0.7 %copy-done.2 = f32[64]{0:T(128)S(1)} copy-done((f32[64]{0:T(128)S(1)}, f32[64]{0:T(128)}, u32[]{:S(2)}) %copy-start.2) | copy-done | bytes 280
  9.1 1.5 %whiten.1 = (bf16[128,512]{1,0:T(8,128)(2,1)S(1)}, bf16[128,512]{1,0:T(8,128)(2,1)S(1)}, bf16[64,1024]{1,0:T(8,128)(2,1)S(1)}, bf16[64,1024]{1,0:T(8,128)(2,1)S(1)}) custom-call(bf16[128,128]{1,0:T(8,128)(2,1)S(1)} %collective-permute-done.tail_ref, bf16[128,4096]{1,0:T(8,128)(2,1)S(1)} %copy-done, f32[1,64]{1,0:T(1,128)S(1)} %bitcast.4), custom_call_target="tpu_custom_call" | custom-call | tf_op jit(solution)/shard_map/whiten/pallas_call | solution.py:83
  10.6 2.4 %collective-permute-start.9 = (bf16[64,1024]{1,0:T(8,128)(2,1)S(1)}, bf16[64,1024]{1,0:T(8,128)(2,1)S(1)}, u32[]{:S(2)}, u32[]{:S(2)}) collective-permute-start(bf16[64,1024]{1,0:T(8,128)(2,1)S(1)} %get-tuple-element.29), channel_id=1, source_target_pairs={{0,1},{1,0},{2,3},{3,2},{4,5},{5,4},{6,7},{7,6},{8,9},{9,8},{10,11... | collective-permute-start | bytes 393224 | tf_op jit(solution)/shard_map/ppermute | solution.py:32
  13.0 3.6 %collective-permute-start.8 = (bf16[128,512]{1,0:T(8,128)(2,1)S(1)}, bf16[128,512]{1,0:T(8,128)(2,1)S(1)}, u32[]{:S(2)}, u32[]{:S(2)}) collective-permute-start(bf16[128,512]{1,0:T(8,128)(2,1)S(1)} %get-tuple-element.40.refs_2_), channel_id=1, source_target_pairs={{0,24},{2,26},{4,28},{6,30},{8,0},{10,2},{12,4},{14,6},{16,8},{18,... | collective-permute-start | bytes 393224 | tf_op jit(solution)/shard_map/ppermute | solution.py:32
  16.6 1.4 %collective-permute-start.7 = (bf16[128,512]{1,0:T(8,128)(2,1)S(1)}, bf16[128,512]{1,0:T(8,128)(2,1)S(1)}, u32[]{:S(2)}, u32[]{:S(2)}) collective-permute-start(bf16[128,512]{1,0:T(8,128)(2,1)S(1)} %get-tuple-element.40.refs_2_), channel_id=1, source_target_pairs={{0,28},{2,30},{4,0},{6,2},{8,4},{10,6},{12,8},{14,10},{16,12},{18,... | collective-permute-start | bytes 393224 | tf_op jit(solution)/shard_map/ppermute | solution.py:32
  18.0 0.6 %collective-permute-start.6 = (bf16[128,512]{1,0:T(8,128)(2,1)S(1)}, bf16[128,512]{1,0:T(8,128)(2,1)S(1)}, u32[]{:S(2)}, u32[]{:S(2)}) collective-permute-start(bf16[128,512]{1,0:T(8,128)(2,1)S(1)} %get-tuple-element.40.refs_2_), channel_id=1, source_target_pairs={{0,4},{2,6},{4,8},{6,10},{8,12},{10,14},{12,16},{14,18},{16,20},{1... | collective-permute-start | bytes 393224 | tf_op jit(solution)/shard_map/ppermute | solution.py:32
  18.6 0.9 %collective-permute-start.5 = (bf16[128,512]{1,0:T(8,128)(2,1)S(1)}, bf16[128,512]{1,0:T(8,128)(2,1)S(1)}, u32[]{:S(2)}, u32[]{:S(2)}) collective-permute-start(bf16[128,512]{1,0:T(8,128)(2,1)S(1)} %get-tuple-element.40.refs_2_), channel_id=1, source_target_pairs={{0,8},{2,10},{4,12},{6,14},{8,16},{10,18},{12,20},{14,22},{16,24},... | collective-permute-start | bytes 393224 | tf_op jit(solution)/shard_map/ppermute | solution.py:32
  19.6 2.9 %collective-permute-start.4 = (bf16[128,512]{1,0:T(8,128)(2,1)S(1)}, bf16[128,512]{1,0:T(8,128)(2,1)S(1)}, u32[]{:S(2)}, u32[]{:S(2)}) collective-permute-start(bf16[128,512]{1,0:T(8,128)(2,1)S(1)} %get-tuple-element.33.refs_2_), channel_id=1, source_target_pairs={{0,24},{2,26},{4,28},{6,30},{8,0},{10,2},{12,4},{14,6},{16,8},{18,... | collective-permute-start | bytes 393224 | tf_op jit(solution)/shard_map/ppermute | solution.py:32
  22.5 3.2 %collective-permute-start.3 = (bf16[128,512]{1,0:T(8,128)(2,1)S(1)}, bf16[128,512]{1,0:T(8,128)(2,1)S(1)}, u32[]{:S(2)}, u32[]{:S(2)}) collective-permute-start(bf16[128,512]{1,0:T(8,128)(2,1)S(1)} %get-tuple-element.33.refs_2_), channel_id=1, source_target_pairs={{0,28},{2,30},{4,0},{6,2},{8,4},{10,6},{12,8},{14,10},{16,12},{18,... | collective-permute-start | bytes 393224 | tf_op jit(solution)/shard_map/ppermute | solution.py:32
  25.7 1.2 %collective-permute-done.6.refs_1_ = bf16[128,512]{1,0:T(8,128)(2,1)S(1)} collective-permute-done((bf16[128,512]{1,0:T(8,128)(2,1)S(1)}, bf16[128,512]{1,0:T(8,128)(2,1)S(1)}, u32[]{:S(2)}, u32[]{:S(2)}) %collective-permute-start.6) | collective-permute-done | bytes 131104 | tf_op jit(solution)/shard_map/ppermute | solution.py:32
  26.9 0.0 collective-permute-start.1
  26.9 1.4 %lags.2.refs_0_ = bf16[2112,1024]{1,0:T(8,128)(2,1)S(1)} custom-call(bf16[64,1024]{1,0:T(8,128)(2,1)S(1)} %get-tuple-element.26.own_ref), custom_call_target="tpu_custom_call" | custom-call | bytes 8388608 | tf_op jit(solution)/shard_map/lags/pallas_call | solution.py:111
  28.3 1.4 %lags.3.refs_1_ = bf16[2112,1024]{1,0:T(8,128)(2,1)S(1)} custom-call(bf16[64,1024]{1,0:T(8,128)(2,1)S(1)} %collective-permute-done.9.own_ref), custom_call_target="tpu_custom_call" | custom-call | bytes 8388608 | tf_op jit(solution)/shard_map/lags/pallas_call | solution.py:111
  29.8 0.1 collective-permute-start.10
  29.9 1.1 %collective-permute-done.10.core_offsets = s32[1,2]{1,0:T(1,128)S(1)} collective-permute-done((s32[1,2]{1,0:T(1,128)S(1)}, s32[1,2]{1,0:T(1,128)S(1)}, u32[]{:S(2)}, u32[]{:S(2)}) %collective-permute-start.10) | collective-permute-done | bytes 40 | tf_op jit(solution)/shard_map/ppermute | solution.py:37
  31.0 0.7 %pick.3 = (bf16[2,128,512]{2,1,0:T(8,128)(2,1)S(1)}, bf16[2,128,512]{2,1,0:T(8,128)(2,1)S(1)}) custom-call(s32[1,2]{1,0:T(1,128)S(1)} %copy-done.1, s32[1,2]{1,0:T(1,128)S(1)} %collective-permute-done.10.core_offsets, bf16[128,512]{1,0:T(8,128)(2,1)S(1)} %collective-permute-done.5.refs_0_, bf16[128,512]{1,0:T(8,128)(2,1)S(1)} %collective-permute-done.6.refs_1_, ...), custom_call_target="tpu_custom_call" | custom-call | tf_op jit(solution)/shard_map/pick/pallas_call | solution.py:140
  31.7 0.3 collective-permute-start.12
  31.9 1.9 %collective-permute-done.2.refs_1_ = bf16[128,512]{1,0:T(8,128)(2,1)S(1)} collective-permute-done((bf16[128,512]{1,0:T(8,128)(2,1)S(1)}, bf16[128,512]{1,0:T(8,128)(2,1)S(1)}, u32[]{:S(2)}, u32[]{:S(2)}) %collective-permute-start.2) | collective-permute-done | bytes 131104 | tf_op jit(solution)/shard_map/ppermute | solution.py:32
  33.8 0.7 %pick.2 = (bf16[2,128,512]{2,1,0:T(8,128)(2,1)S(1)}, bf16[2,128,512]{2,1,0:T(8,128)(2,1)S(1)}) custom-call(s32[1,2]{1,0:T(1,128)S(1)} %copy-done.1, s32[1,2]{1,0:T(1,128)S(1)} %collective-permute-done.10.core_offsets, bf16[128,512]{1,0:T(8,128)(2,1)S(1)} %collective-permute-done.1.refs_0_, bf16[128,512]{1,0:T(8,128)(2,1)S(1)} %collective-permute-done.2.refs_1_, ...), custom_call_target="tpu_custom_call" | custom-call | tf_op jit(solution)/shard_map/pick/pallas_call | solution.py:140
  34.5 0.1 collective-permute-start.11
  34.6 0.6 %merge.3.refs_3_ = bf16[2,128,512]{2,1,0:T(8,128)(2,1)S(1)} custom-call(s32[1,2]{1,0:T(1,128)S(1)} %copy-done.1, bf16[2,128,512]{2,1,0:T(8,128)(2,1)S(1)} %get-tuple-element.43.keep_ref, bf16[2,128,512]{2,1,0:T(8,128)(2,1)S(1)} %collective-permute-done.12.got_ref), custom_call_target="tpu_custom_call" | custom-call | tf_op jit(solution)/shard_map/merge/pallas_call | solution.py:164
  35.2 0.4 collective-permute-start.14
  35.6 0.5 collective-permute-done.11.got_ref
  36.1 0.6 %merge.2.refs_2_ = bf16[2,128,512]{2,1,0:T(8,128)(2,1)S(1)} custom-call(s32[1,2]{1,0:T(1,128)S(1)} %copy-done.1, bf16[2,128,512]{2,1,0:T(8,128)(2,1)S(1)} %get-tuple-element.36.keep_ref, bf16[2,128,512]{2,1,0:T(8,128)(2,1)S(1)} %collective-permute-done.11.got_ref), custom_call_target="tpu_custom_call" | custom-call | tf_op jit(solution)/shard_map/merge/pallas_call | solution.py:164
  36.7 1.2 %collective-permute-start.13 = (bf16[2,128,512]{2,1,0:T(8,128)(2,1)S(1)}, bf16[2,128,512]{2,1,0:T(8,128)(2,1)S(1)}, u32[]{:S(2)}, u32[]{:S(2)}) collective-permute-start(bf16[2,128,512]{2,1,0:T(8,128)(2,1)S(1)} %merge.2.refs_2_), channel_id=1, source_target_pairs={{0,1},{1,0},{2,3},{3,2},{4,5},{5,4},{6,7},{7,6},{8,9},{9,8},{10,11... | collective-permute-start | bytes 786440 | tf_op jit(solution)/shard_map/ppermute | solution.py:32
  37.9 6.4 %collective-permute-done.14.refs_5_ = bf16[2,128,512]{2,1,0:T(8,128)(2,1)S(1)} collective-permute-done((bf16[2,128,512]{2,1,0:T(8,128)(2,1)S(1)}, bf16[2,128,512]{2,1,0:T(8,128)(2,1)S(1)}, u32[]{:S(2)}, u32[]{:S(2)}) %collective-permute-start.14) | collective-permute-done | bytes 262176 | tf_op jit(solution)/shard_map/ppermute | solution.py:32
  44.4 5.2 %collective-permute-done.13.refs_4_ = bf16[2,128,512]{2,1,0:T(8,128)(2,1)S(1)} collective-permute-done((bf16[2,128,512]{2,1,0:T(8,128)(2,1)S(1)}, bf16[2,128,512]{2,1,0:T(8,128)(2,1)S(1)}, u32[]{:S(2)}, u32[]{:S(2)}) %collective-permute-start.13) | collective-permute-done | bytes 262176 | tf_op jit(solution)/shard_map/ppermute | solution.py:32
  49.6 4.1 %correlate.1 = f32[4224,128]{1,0:T(8,128)} custom-call(s32[1,2]{1,0:T(1,128)S(1)} %copy-done.1, bf16[2112,1024]{1,0:T(8,128)(2,1)S(1)} %lags.2.refs_0_, bf16[2112,1024]{1,0:T(8,128)(2,1)S(1)} %lags.3.refs_1_, bf16[2,128,512]{2,1,0:T(8,128)(2,1)S(1)} %merge.2.refs_2_, bf16[2,128,512]{2,1,0:T(8,128)(2,1)S(1)} %merge.3.refs_3_, ...), custom_call_target="tpu_custom_call" | custom-call | tf_op jit(solution)/shard_map/correlate/pallas_call | solution.py:217
  (13 shorter events, 0.0 us)
Async XLA Ops:
  0.8 6.4 %collective-permute-start = (bf16[128,128]{1,0:T(8,128)(2,1)S(1)}, bf16[128,128]{1,0:T(8,128)(2,1)S(1)}, u32[]{:S(2)}, u32[]{:S(2)}) collective-permute-start(bf16[128,128]{1,0:T(8,128)(2,1)S(1)} %slice.3), channel_id=1, source_target_pairs={{0,1},{2,3},{4,5},{6,7},{8,9},{10,11},{12,13},{14,15},{16,17},{18,... | collective-permute-start | bytes 98312 | tf_op jit(solution)/shard_map/ppermute | solution.py:238
  7.2 1.2 %copy-start = (bf16[128,4096]{1,0:T(8,128)(2,1)S(1)}, bf16[128,4096]{1,0:T(8,128)(2,1)}, u32[]{:S(2)}) copy-start(bf16[128,4096]{1,0:T(8,128)(2,1)} %records_ref.1) | copy-start | bytes 3145732
  8.4 0.7 %copy-start.2 = (f32[64]{0:T(128)S(1)}, f32[64]{0:T(128)}, u32[]{:S(2)}) copy-start(f32[64]{0:T(128)} %param.4) | copy-start | bytes 772
  10.6 8.9 %collective-permute-start.9 = (bf16[64,1024]{1,0:T(8,128)(2,1)S(1)}, bf16[64,1024]{1,0:T(8,128)(2,1)S(1)}, u32[]{:S(2)}, u32[]{:S(2)}) collective-permute-start(bf16[64,1024]{1,0:T(8,128)(2,1)S(1)} %get-tuple-element.29), channel_id=1, source_target_pairs={{0,1},{1,0},{2,3},{3,2},{4,5},{5,4},{6,7},{7,6},{8,9},{9,8},{10,11... | collective-permute-start | bytes 393224 | tf_op jit(solution)/shard_map/ppermute | solution.py:32
  13.0 9.5 %collective-permute-start.8 = (bf16[128,512]{1,0:T(8,128)(2,1)S(1)}, bf16[128,512]{1,0:T(8,128)(2,1)S(1)}, u32[]{:S(2)}, u32[]{:S(2)}) collective-permute-start(bf16[128,512]{1,0:T(8,128)(2,1)S(1)} %get-tuple-element.40.refs_2_), channel_id=1, source_target_pairs={{0,24},{2,26},{4,28},{6,30},{8,0},{10,2},{12,4},{14,6},{16,8},{18,... | collective-permute-start | bytes 393224 | tf_op jit(solution)/shard_map/ppermute | solution.py:32
  16.6 9.1 %collective-permute-start.7 = (bf16[128,512]{1,0:T(8,128)(2,1)S(1)}, bf16[128,512]{1,0:T(8,128)(2,1)S(1)}, u32[]{:S(2)}, u32[]{:S(2)}) collective-permute-start(bf16[128,512]{1,0:T(8,128)(2,1)S(1)} %get-tuple-element.40.refs_2_), channel_id=1, source_target_pairs={{0,28},{2,30},{4,0},{6,2},{8,4},{10,6},{12,8},{14,10},{16,12},{18,... | collective-permute-start | bytes 393224 | tf_op jit(solution)/shard_map/ppermute | solution.py:32
  18.0 8.9 %collective-permute-start.6 = (bf16[128,512]{1,0:T(8,128)(2,1)S(1)}, bf16[128,512]{1,0:T(8,128)(2,1)S(1)}, u32[]{:S(2)}, u32[]{:S(2)}) collective-permute-start(bf16[128,512]{1,0:T(8,128)(2,1)S(1)} %get-tuple-element.40.refs_2_), channel_id=1, source_target_pairs={{0,4},{2,6},{4,8},{6,10},{8,12},{10,14},{12,16},{14,18},{16,20},{1... | collective-permute-start | bytes 393224 | tf_op jit(solution)/shard_map/ppermute | solution.py:32
  18.6 11.1 %collective-permute-start.5 = (bf16[128,512]{1,0:T(8,128)(2,1)S(1)}, bf16[128,512]{1,0:T(8,128)(2,1)S(1)}, u32[]{:S(2)}, u32[]{:S(2)}) collective-permute-start(bf16[128,512]{1,0:T(8,128)(2,1)S(1)} %get-tuple-element.40.refs_2_), channel_id=1, source_target_pairs={{0,8},{2,10},{4,12},{6,14},{8,16},{10,18},{12,20},{14,22},{16,24},... | collective-permute-start | bytes 393224 | tf_op jit(solution)/shard_map/ppermute | solution.py:32
  19.6 12.4 %collective-permute-start.4 = (bf16[128,512]{1,0:T(8,128)(2,1)S(1)}, bf16[128,512]{1,0:T(8,128)(2,1)S(1)}, u32[]{:S(2)}, u32[]{:S(2)}) collective-permute-start(bf16[128,512]{1,0:T(8,128)(2,1)S(1)} %get-tuple-element.33.refs_2_), channel_id=1, source_target_pairs={{0,24},{2,26},{4,28},{6,30},{8,0},{10,2},{12,4},{14,6},{16,8},{18,... | collective-permute-start | bytes 393224 | tf_op jit(solution)/shard_map/ppermute | solution.py:32
  22.5 9.5 %collective-permute-start.3 = (bf16[128,512]{1,0:T(8,128)(2,1)S(1)}, bf16[128,512]{1,0:T(8,128)(2,1)S(1)}, u32[]{:S(2)}, u32[]{:S(2)}) collective-permute-start(bf16[128,512]{1,0:T(8,128)(2,1)S(1)} %get-tuple-element.33.refs_2_), channel_id=1, source_target_pairs={{0,28},{2,30},{4,0},{6,2},{8,4},{10,6},{12,8},{14,10},{16,12},{18,... | collective-permute-start | bytes 393224 | tf_op jit(solution)/shard_map/ppermute | solution.py:32
  25.7 8.1 %collective-permute-start.2 = (bf16[128,512]{1,0:T(8,128)(2,1)S(1)}, bf16[128,512]{1,0:T(8,128)(2,1)S(1)}, u32[]{:S(2)}, u32[]{:S(2)}) collective-permute-start(bf16[128,512]{1,0:T(8,128)(2,1)S(1)} %get-tuple-element.33.refs_2_), channel_id=1, source_target_pairs={{0,4},{2,6},{4,8},{6,10},{8,12},{10,14},{12,16},{14,18},{16,20},{1... | collective-permute-start | bytes 393224 | tf_op jit(solution)/shard_map/ppermute | solution.py:32
  26.9 6.9 %collective-permute-start.1 = (bf16[128,512]{1,0:T(8,128)(2,1)S(1)}, bf16[128,512]{1,0:T(8,128)(2,1)S(1)}, u32[]{:S(2)}, u32[]{:S(2)}) collective-permute-start(bf16[128,512]{1,0:T(8,128)(2,1)S(1)} %get-tuple-element.33.refs_2_), channel_id=1, source_target_pairs={{0,8},{2,10},{4,12},{6,14},{8,16},{10,18},{12,20},{14,22},{16,24},... | collective-permute-start | bytes 393224 | tf_op jit(solution)/shard_map/ppermute | solution.py:32
  26.9 2.9 %copy-start.1 = (s32[1,2]{1,0:T(1,128)S(1)}, s32[1,2]{1,0:T(1,128)}, u32[]{:S(2)}) copy-start(s32[1,2]{1,0:T(1,128)} %offsets.5) | copy-start | bytes 28
  29.8 1.2 %collective-permute-start.10 = (s32[1,2]{1,0:T(1,128)S(1)}, s32[1,2]{1,0:T(1,128)S(1)}, u32[]{:S(2)}, u32[]{:S(2)}) collective-permute-start(s32[1,2]{1,0:T(1,128)S(1)} %copy-done.1), channel_id=1, source_target_pairs={{0,2},{2,0},{4,6},{6,4},{8,10},{10,8},{12,14},{14,12},{16,18},{18,... | collective-permute-start | bytes 32 | tf_op jit(solution)/shard_map/ppermute | solution.py:37
  31.7 2.9 %collective-permute-start.12 = (bf16[2,128,512]{2,1,0:T(8,128)(2,1)S(1)}, bf16[2,128,512]{2,1,0:T(8,128)(2,1)S(1)}, u32[]{:S(2)}, u32[]{:S(2)}) collective-permute-start(bf16[2,128,512]{2,1,0:T(8,128)(2,1)S(1)} %get-tuple-element.44), channel_id=1, source_target_pairs={{0,2},{2,0},{4,6},{6,4},{8,10},{10,8},{12,14},{14,12},{16,18},{18,... | collective-permute-start | bytes 786440 | tf_op jit(solution)/shard_map/ppermute | solution.py:37
  34.5 1.6 %collective-permute-start.11 = (bf16[2,128,512]{2,1,0:T(8,128)(2,1)S(1)}, bf16[2,128,512]{2,1,0:T(8,128)(2,1)S(1)}, u32[]{:S(2)}, u32[]{:S(2)}) collective-permute-start(bf16[2,128,512]{2,1,0:T(8,128)(2,1)S(1)} %get-tuple-element.37), channel_id=1, source_target_pairs={{0,2},{2,0},{4,6},{6,4},{8,10},{10,8},{12,14},{14,12},{16,18},{18,... | collective-permute-start | bytes 786440 | tf_op jit(solution)/shard_map/ppermute | solution.py:37
  35.2 9.2 %collective-permute-start.14 = (bf16[2,128,512]{2,1,0:T(8,128)(2,1)S(1)}, bf16[2,128,512]{2,1,0:T(8,128)(2,1)S(1)}, u32[]{:S(2)}, u32[]{:S(2)}) collective-permute-start(bf16[2,128,512]{2,1,0:T(8,128)(2,1)S(1)} %merge.3.refs_3_), channel_id=1, source_target_pairs={{0,1},{1,0},{2,3},{3,2},{4,5},{5,4},{6,7},{7,6},{8,9},{9,8},{10,11... | collective-permute-start | bytes 786440 | tf_op jit(solution)/shard_map/ppermute | solution.py:32
  36.7 12.9 %collective-permute-start.13 = (bf16[2,128,512]{2,1,0:T(8,128)(2,1)S(1)}, bf16[2,128,512]{2,1,0:T(8,128)(2,1)S(1)}, u32[]{:S(2)}, u32[]{:S(2)}) collective-permute-start(bf16[2,128,512]{2,1,0:T(8,128)(2,1)S(1)} %merge.2.refs_2_), channel_id=1, source_target_pairs={{0,1},{1,0},{2,3},{3,2},{4,5},{5,4},{6,7},{7,6},{8,9},{9,8},{10,11... | collective-permute-start | bytes 786440 | tf_op jit(solution)/shard_map/ppermute | solution.py:32

commit v3 on v2

v3 whole, which is shorter than its diff:
```python
import functools
import math

import jax
import jax.numpy as jnp
from jax import lax
from jax.experimental import pallas as pl
from jax.experimental.pallas import tpu as pltpu
from jax.sharding import PartitionSpec as P

TAPS = 64
DECIM = 4
MAXLAG = 16
T_DEC = 1024
LAGS = 33
LANES = 128
TILES = T_DEC // LANES
HISTORY = TAPS - DECIM
RAW = LANES * DECIM
SPAN = RAW + LANES
EDGES = (0, 512, 1024)
CHUNKS = len(EDGES) - 1
TEAM = 4
GROUP = 16
VMEM = pltpu.VMEM
F32 = jnp.float32
BF16 = jnp.bfloat16
NT = (((1,), (1,)), ((), ()))
VMEM_SPEC = pl.BlockSpec(memory_space=pltpu.VMEM)
HBM_SPEC = pl.BlockSpec(memory_space=pltpu.HBM)


def grant(mib):
    return pltpu.CompilerParams(vmem_limit_bytes=mib << 20)


def shift(x, axis, by):
    n = lax.axis_size(axis)
    return lax.ppermute(x, axis, [(i, (i + by) % n) for i in range(n)])


def swap(x, bit):
    n = lax.axis_size("chan")
    return lax.ppermute(x, "chan", [(i, i ^ bit) for i in range(n)])


def filter_kernel(records_ref, taps_ref, filtered, squares_ref, band_ref, line):
    channels = filtered.shape[0]
    line[...] = jnp.zeros_like(line)
    line[0:1, 0:TAPS] = taps_ref[...]
    band = pltpu.roll(
        jnp.broadcast_to(line[0:1, :], (LANES, SPAN)), LANES - HISTORY, 1, stride=DECIM, stride_axis=0
    )
    high = band.astype(BF16)
    rest = band - high.astype(F32)
    mid = rest.astype(BF16)
    low = (rest - mid.astype(F32)).astype(BF16)
    weights = jnp.concatenate([high, mid, low], axis=0)
    band_ref[...] = weights[:, :LANES]
    squares = jnp.zeros((channels, LANES), F32)
    for tile in range(TILES):
        if tile == 0:
            block, used = records_ref[:, :RAW], weights[:, LANES:]
        else:
            block, used = records_ref[:, tile * RAW - LANES : (tile + 1) * RAW], weights
        out = lax.dot_general(block, used, NT, preferred_element_type=F32)
        value = out[:, :LANES] + (out[:, LANES : 2 * LANES] + out[:, 2 * LANES :])
        filtered[:, tile * LANES : (tile + 1) * LANES] = value
        if tile > 0:
            squares = squares + value * value
    squares_ref[...] = squares


def bulk_filter(records, fir_taps):
    channels = records.shape[0]
    return pl.pallas_call(
        filter_kernel,
        out_shape=[
            jax.ShapeDtypeStruct((channels, T_DEC), F32),
            jax.ShapeDtypeStruct((channels, LANES), F32),
            jax.ShapeDtypeStruct((3 * LANES, LANES), BF16),
        ],
        in_specs=[VMEM_SPEC] * 2,
        out_specs=[VMEM_SPEC] * 3,
        scratch_shapes=[VMEM((8, SPAN), F32)],
        compiler_params=grant(4),
        name="bulk_filter",
    )(records, fir_taps.reshape(1, TAPS))


def whiten_kernel(win, tail_ref, band_ref, filtered, squares_ref, *refs):
    chunk_refs = refs[:CHUNKS]
    row_refs = refs[CHUNKS : CHUNKS + win]
    whole_ref, white = refs[CHUNKS + win :]
    rows = row_refs[0].shape[0]
    out = lax.dot_general(tail_ref[...], band_ref[...], NT, preferred_element_type=F32)
    first = filtered[:, :LANES] + (
        out[:, :LANES] + (out[:, LANES : 2 * LANES] + out[:, 2 * LANES :])
    )
    squares = squares_ref[...] + first * first
    energy = jnp.sqrt(jnp.sum(squares, axis=1, keepdims=True) * (1.0 / T_DEC) + 1e-06)
    inverse = 1.0 / energy
    white[:, :LANES] = first * inverse
    white[:, LANES:] = filtered[:, LANES:] * inverse
    for chunk, ref in enumerate(chunk_refs):
        ref[...] = white[:, EDGES[chunk] : EDGES[chunk + 1]].astype(BF16)
    whole_ref[...] = white[...].astype(BF16)
    me = lax.axis_index("win")
    for step, ref in enumerate(row_refs):
        owner = lax.rem(me + step, win)
        ref[...] = white[pl.ds(pl.multiple_of(owner * rows, rows), rows), :].astype(BF16)


def whiten(before, band, filtered, squares):
    channels = filtered.shape[0]
    win = lax.axis_size("win")
    return pl.pallas_call(
        functools.partial(whiten_kernel, win),
        out_shape=[
            jax.ShapeDtypeStruct((channels, EDGES[chunk + 1] - EDGES[chunk]), BF16)
            for chunk in range(CHUNKS)
        ]
        + [jax.ShapeDtypeStruct((channels // win, T_DEC), BF16)] * win
        + [jax.ShapeDtypeStruct((channels, T_DEC), BF16)],
        in_specs=[VMEM_SPEC] * 4,
        out_specs=[VMEM_SPEC] * (CHUNKS + win + 1),
        scratch_shapes=[VMEM((channels, T_DEC), F32)],
        compiler_params=grant(4),
        name="whiten",
    )(before, band, filtered, squares)


def lags_kernel(own_ref, lags_ref, padded):
    rows = own_ref.shape[0]
    zeros = jnp.zeros((rows, LANES), BF16)
    padded[:, :LANES] = zeros
    padded[:, LANES + T_DEC :] = zeros
    padded[:, LANES : LANES + T_DEC] = own_ref[...]
    for group in range(rows // GROUP):
        block = padded[group * GROUP : (group + 1) * GROUP, :]
        for lag in range(LAGS):
            first = LANES + MAXLAG - lag
            row = (group * LAGS + lag) * GROUP
            lags_ref[row : row + GROUP, :] = block[:, first : first + T_DEC]


def lay_out_lags(own):
    rows = own.shape[0]
    return pl.pallas_call(
        lags_kernel,
        out_shape=jax.ShapeDtypeStruct((rows * LAGS, T_DEC), BF16),
        in_specs=[VMEM_SPEC],
        out_specs=VMEM_SPEC,
        scratch_shapes=[VMEM((rows, T_DEC + 2 * LANES), BF16)],
        compiler_params=grant(8),
        cost_estimate=pl.CostEstimate(flops=0, bytes_accessed=8 << 20, transcendentals=0),
        name="lags",
    )(own)


def far_kernel(behind_ref, ahead_ref, *refs):
    second = lax.rem(lax.axis_index("chan"), TEAM) >= 2

    @pl.when(second)
    def _():
        refs[-1][...] = behind_ref[...]

    @pl.when(jnp.logical_not(second))
    def _():
        refs[-1][...] = ahead_ref[...]


def far(behind, ahead, after):
    return pl.pallas_call(
        far_kernel,
        out_shape=jax.ShapeDtypeStruct(behind.shape, BF16),
        in_specs=[VMEM_SPEC] * (2 + len(after)),
        out_specs=VMEM_SPEC,
        compiler_params=grant(2),
        name="far",
    )(behind, ahead, *after)


def pick_kernel(hops, first, own_offsets, core_offsets, *refs):
    sources = refs[: 4 * hops + 1]
    slots = own_offsets.shape[1]
    keep_ref, send_refs = refs[-1 - slots], refs[-slots:]
    lanes = keep_ref.shape[2]
    here = lax.rem(lax.axis_index("chan"), TEAM)
    second = here >> 1
    for slot in range(slots):
        for offsets, place in ((own_offsets, here), (core_offsets, here ^ 1)):
            target = place + offsets[...][0, slot]
            hop = jnp.clip(target >> 2, -hops, hops)
            same = ((target >> 1) & 1) == second
            other = jnp.where(jnp.abs(hop) < hops, 3 * hops + hop, 4 * hops)
            index = jnp.where(same, hops + hop, other)
            for source, ref in enumerate(sources):

                @pl.when(index == source)
                def _(ref=ref, slot=slot, own=offsets is own_offsets):
                    block = ref[...] if ref.shape[1] == lanes else ref[:, first : first + lanes]
                    if own:
                        keep_ref[slot] = block
                    else:
                        send_refs[slot][...] = block


def pick(hops, first, lanes, own_offsets, core_offsets, sources, after):
    slots = own_offsets.shape[1]
    block = (sources[0].shape[0], lanes)
    out = pl.pallas_call(
        functools.partial(pick_kernel, hops, first),
        out_shape=[jax.ShapeDtypeStruct((slots,) + block, BF16)] + [jax.ShapeDtypeStruct(block, BF16)] * slots,
        in_specs=[VMEM_SPEC] * (2 + len(sources) + len(after)),
        out_specs=[VMEM_SPEC] * (1 + slots),
        compiler_params=grant(4),
        name="pick",
    )(own_offsets, core_offsets, *sources, *after)
    return out[0], out[1:]


def merge_kernel(offsets, keep_ref, *refs):
    slots = offsets.shape[1]
    odd = (offsets[...] & 1) == 1
    for slot in range(slots):
        refs[-1][slot] = jnp.where(odd[0:1, slot : slot + 1], refs[slot][...], keep_ref[slot])


def merge(offsets, keep, got, after):
    return pl.pallas_call(
        merge_kernel,
        out_shape=jax.ShapeDtypeStruct(keep.shape, BF16),
        in_specs=[VMEM_SPEC] * (2 + len(got) + len(after)),
        out_specs=VMEM_SPEC,
        compiler_params=grant(2),
        name="merge",
    )(offsets, keep, *got, *after)


def products(lags_ref, rows, parts):
    acc = None
    for first, ref in parts:
        slots, channels, lanes = ref.shape
        part = lax.dot_general(
            lags_ref[rows, first : first + lanes],
            ref[...].reshape(slots * channels, lanes),
            NT,
            preferred_element_type=F32,
        )
        acc = part if acc is None else acc + part
    return acc


def accumulate_kernel(firsts, has_acc, lags_ref, *refs):
    others = refs[: len(firsts)]
    out_ref = refs[-1]
    block = GROUP * LAGS
    for group in range(lags_ref.shape[0] // block):
        rows = slice(group * block, (group + 1) * block)
        acc = products(lags_ref, rows, list(zip(firsts, others)))
        if has_acc:
            acc = acc + refs[len(firsts)][rows, :]
        out_ref[rows, :] = acc


def accumulate(acc, lags, parts):
    firsts = [first for first, _ in parts]
    slots, channels, _ = parts[0][1].shape
    operands = [lags] + [array for _, array in parts] + ([] if acc is None else [acc])
    return pl.pallas_call(
        functools.partial(accumulate_kernel, firsts, acc is not None),
        out_shape=jax.ShapeDtypeStruct((lags.shape[0], slots * channels), F32),
        in_specs=[VMEM_SPEC] * len(operands),
        out_specs=VMEM_SPEC,
        compiler_params=grant(8),
        name="accumulate",
    )(*operands)


def finish_kernel(reach, factor, first, offsets, lags_ref, other_ref, acc_ref, out_ref, stage, sems):
    slots = offsets.shape[1]
    block = GROUP * LAGS
    stride = LAGS * slots
    groups = lags_ref.shape[0] // block
    listed = offsets[...] <= reach

    def out_copy(group):
        rows = pl.ds(group * block * slots, block * slots)
        return pltpu.make_async_copy(stage.at[rows], out_ref.at[rows], sems.at[group])

    for group in range(groups):
        rows = slice(group * block, (group + 1) * block)
        acc = (acc_ref[rows, :] + products(lags_ref, rows, [(first, other_ref)])) * factor
        for slot in range(slots):
            value = jnp.where(listed[0:1, slot : slot + 1], acc[:, slot * LANES : (slot + 1) * LANES], 0.0)
            for lag in range(LAGS):
                for half in range(GROUP // 8):
                    row = lag * GROUP + half * 8
                    start = (group * GROUP + half * 8) * stride + lag * slots + slot
                    stage[pl.ds(start, 8, stride=stride), :] = value[row : row + 8, :]
        out_copy(group).start()
    for group in range(groups):
        out_copy(group).wait()


def finish(reach, factor, offsets, acc, lags, first, other):
    slots = offsets.shape[1]
    total = lags.shape[0]
    out = pl.pallas_call(
        functools.partial(finish_kernel, reach, factor, first),
        out_shape=jax.ShapeDtypeStruct((total * slots, LANES), F32),
        in_specs=[VMEM_SPEC] * 4,
        out_specs=HBM_SPEC,
        scratch_shapes=[
            VMEM((total * slots, LANES), F32),
            pltpu.SemaphoreType.DMA((total // (GROUP * LAGS),)),
        ],
        compiler_params=grant(12),
        name="finish",
    )(offsets, lags, other, acc)
    return out.reshape(total // LAGS, LAGS, slots, LANES).transpose(0, 2, 1, 3)


def body(records, fir_taps, pair_offsets):
    win = lax.axis_size("win")
    reach = lax.axis_size("chan") // 4
    hops = reach // TEAM
    factor = 1.0 / math.sqrt(T_DEC * win)

    tail = records[:, records.shape[1] - LANES :]
    before = lax.ppermute(tail, "win", [(i, i + 1) for i in range(win - 1)])
    core_offsets = swap(pair_offsets, 1)
    filtered, squares, band = bulk_filter(records, fir_taps)
    before, core_offsets = lax.optimization_barrier((before, core_offsets))
    outs = whiten(before, band, filtered, squares)
    chunks, row_parts, whole = outs[:CHUNKS], outs[CHUNKS:-1], outs[-1]

    def spread(block):
        direct = {0: block}
        for hop in range(hops, 0, -1):
            direct[-hop] = shift(block, "chan", TEAM * hop)
            direct[hop] = shift(block, "chan", -TEAM * hop)
        return direct

    def gather(chunk, direct, after_far, after_pick, after_merge):
        edge = swap(far(direct[-hops], direct[hops], after_far), 2)
        crossed = [beside if hop == 0 else swap(direct[hop], 2) for hop in range(1 - hops, hops)]
        sources = [direct[hop] for hop in range(-hops, hops + 1)] + crossed + [edge]
        first, last = EDGES[chunk], EDGES[chunk + 1]
        keep, send = pick(hops, first, last - first, pair_offsets, core_offsets, sources, after_pick)
        chosen = merge(pair_offsets, keep, [swap(part, 1) for part in send], after_merge)
        return [chosen] + [shift(chosen, "win", step) for step in range(1, win)], send

    directs = [spread(block) for block in chunks]
    beside = swap(whole, 2)
    own = [row_parts[0]] + [shift(row_parts[step], "win", step) for step in range(1, win)]
    lags = [lay_out_lags(part) for part in own]

    pieces = []
    after_far, after_pick, after_merge = lags[:1], [], []
    for chunk in range(CHUNKS):
        piece, send = gather(chunk, directs[chunk], after_far, after_pick, after_merge)
        after_far, after_pick, after_merge = [send[0]], [piece[0]] + lags[1:], piece[1:]
        pieces.append(piece)
    others = [[pieces[chunk][step] for chunk in range(CHUNKS)] for step in range(win)]
    acc = accumulate(None, lags[0], list(zip(EDGES, others[0])))
    left = [(step, chunk) for chunk in range(CHUNKS) for step in range(1, win)]
    for step, chunk in left[:-1]:
        acc = accumulate(acc, lags[step], [(EDGES[chunk], others[step][chunk])])
    step, chunk = left[-1]
    return finish(reach, factor, pair_offsets, acc, lags[step], EDGES[chunk], others[step][chunk])


def solution(mesh):
    placed = (P("chan", "win"), P(), P("chan", None))
    return jax.shard_map(
        body,
        mesh=mesh,
        in_specs=placed,
        out_specs=P(("chan", "win"), None, None, None),
        check_vma=False,
    )
```

time: 53.9 us -> 48.3 us (0.90)
  starting transfers between devices: 22 us -> 16 us
  waiting for transfers between devices: 17.9 us -> 19.7 us
  Pallas kernels: 11 us -> 9.6 us
    ppermute x11 -> x7, starting transfers between devices: 16.7 us -> 6.24 us  [shift(): return lax.ppermute(x, axis, [(i, (i + by) % n) for i in range(n)])]
    ppermute x3 -> x8, starting transfers between devices: 0.41 us -> 4.86 us  [swap(): return lax.ppermute(x, 'chan', [(i, i ^ bit) for i in range(n)])]
    ppermute x3 -> x8, waiting for transfers between devices: 1.63 us -> 3.86 us  [swap(): return lax.ppermute(x, 'chan', [(i, i ^ bit) for i in range(n)])]
    ppermute x1, waiting for transfers between devices: 1.58 us -> 0.01 us  [body(): before = lax.ppermute(tail, 'win', [(i, i + 1) for i in range(win - 1)])]
    ppermute x11 -> x7, waiting for transfers between devices: 14.7 us -> 15.8 us  [shift(): return lax.ppermute(x, axis, [(i, (i + by) % n) for i in range(n)])]
    pallas_call x2, Pallas kernels: 1.15 us -> 0.19 us  [merge(): pl.pallas_call(merge_kernel, out_shape=jax.ShapeDtypeStruct(keep.shape, B...]
    pallas_call x4 -> x9, Pallas kernels: 6.99 us -> 6.56 us  [the longest x2 2.07 us: accumulate(): pl.pallas_call(functools.partial(accumulate_kernel, firsts, acc is not No...]
  transfers between devices with their start and end apart: 15 -> 16, of which waited for: 7 -> 11; matrix products, arithmetic and copies ran while one was open for 0% -> 0% of each run, Pallas kernels for 10% -> 15%
where the time goes in v3:
time: 48.3 us; the launch traced here: 48 us
  waiting for transfers between devices  19.7 us (41%)
  starting transfers between devices  16 us (33%)
  Pallas kernels  9.6 us (20%)
  local copies, waits for them, and re-layouts  2.64 us (5%)
    ppermute x7, waiting for transfers between devices, shift(): return lax.ppermute(x, axis, [(i, (i + by) % n) for i in range(n)])  15.8 us
    ppermute x7, starting transfers between devices, shift(): return lax.ppermute(x, axis, [(i, (i + by) % n) for i in range(n)])  6.24 us
    ppermute x1, starting transfers between devices, body(): before = lax.ppermute(tail, 'win', [(i, i + 1) for i in range(win - 1)])  4.86 us
    ppermute x8, starting transfers between devices, swap(): return lax.ppermute(x, 'chan', [(i, i ^ bit) for i in range(n)])  4.86 us
    ppermute x8, waiting for transfers between devices, swap(): return lax.ppermute(x, 'chan', [(i, i ^ bit) for i in range(n)])  3.86 us
    pallas_call x2, Pallas kernels, lay_out_lags(): pl.pallas_call(lags_kernel, out_shape=jax.ShapeDtypeStruct((rows * LAGS,...  2.84 us
    pallas_call x2, Pallas kernels, accumulate(): pl.pallas_call(functools.partial(accumulate_kernel, firsts, acc is not No...  2.07 us
    pallas_call x1, Pallas kernels, finish(): pl.pallas_call(functools.partial(finish_kernel, reach, factor, first), ou...  1.92 us
  transfers between devices with their start and end apart: 16, of which 11 were waited for; matrix products, arithmetic and copies ran while one was open for 0% of the time, Pallas kernels for 15%

profile of v3, /device:TPU:0, one launch (start us, length us, event | category | flops | bytes accessed | tf_op | source)
XLA Modules:
  0.0 48.0 jit_solution(14906572303407610860)
XLA Ops:
  0.0 0.8 %slice.3 = bf16[128,128]{1,0:T(8,128)(2,1)S(1)} slice(bf16[128,4096]{1,0:T(8,128)(2,1)} %records_ref.1), slice={[0:128], [3968:4096]} | slice | bytes 65536 | tf_op jit(solution)/shard_map/slice | solution.py:331
  0.8 4.9 %collective-permute-start = (bf16[128,128]{1,0:T(8,128)(2,1)S(1)}, bf16[128,128]{1,0:T(8,128)(2,1)S(1)}, u32[]{:S(2)}, u32[]{:S(2)}) collective-permute-start(bf16[128,128]{1,0:T(8,128)(2,1)S(1)} %slice.3), channel_id=1, source_target_pairs={{0,1},{2,3},{4,5},{6,7},{8,9},{10,11},{12,13},{14,15},{16,17},{18,... | collective-permute-start | bytes 98312 | tf_op jit(solution)/shard_map/ppermute | solution.py:332
  5.7 1.2 %copy-done = bf16[128,4096]{1,0:T(8,128)(2,1)S(1)} copy-done((bf16[128,4096]{1,0:T(8,128)(2,1)S(1)}, bf16[128,4096]{1,0:T(8,128)(2,1)}, u32[]{:S(2)}) %copy-start) | copy-done | bytes 1048600
  6.9 0.7 %copy-done.2 = f32[64]{0:T(128)S(1)} copy-done((f32[64]{0:T(128)S(1)}, f32[64]{0:T(128)}, u32[]{:S(2)}) %copy-start.2) | copy-done | bytes 280
  7.6 1.3 %bulk_filter.1 = (f32[128,1024]{1,0:T(8,128)S(1)}, f32[128,128]{1,0:T(8,128)S(1)}, bf16[384,128]{1,0:T(8,128)(2,1)S(1)}) custom-call(bf16[128,4096]{1,0:T(8,128)(2,1)S(1)} %copy-done, f32[1,64]{1,0:T(1,128)S(1)} %bitcast.4), custom_call_target="tpu_custom_call" | custom-call | tf_op jit(solution)/shard_map/bulk_filter/pallas_call | solution.py:76
  9.0 0.4 whiten.1
  9.3 3.7 %collective-permute-start.7 = (bf16[128,512]{1,0:T(8,128)(2,1)S(1)}, bf16[128,512]{1,0:T(8,128)(2,1)S(1)}, u32[]{:S(2)}, u32[]{:S(2)}) collective-permute-start(bf16[128,512]{1,0:T(8,128)(2,1)S(1)} %get-tuple-element.29.refs_1_), channel_id=1, source_target_pairs={{0,24},{2,26},{4,28},{6,30},{8,0},{10,2},{12,4},{14,6},{16,8},{18,... | collective-permute-start | bytes 393224 | tf_op jit(solution)/shard_map/ppermute | solution.py:39
  13.0 1.5 %collective-permute-start.5 = (bf16[128,1024]{1,0:T(8,128)(2,1)S(1)}, bf16[128,1024]{1,0:T(8,128)(2,1)S(1)}, u32[]{:S(2)}, u32[]{:S(2)}) collective-permute-start(bf16[128,1024]{1,0:T(8,128)(2,1)S(1)} %get-tuple-element.28), channel_id=1, source_target_pairs={{0,4},{2,6},{4,0},{6,2},{8,12},{10,14},{12,8},{14,10},{16,20},{18,... | collective-permute-start | bytes 786440 | tf_op jit(solution)/shard_map/ppermute | solution.py:44
  14.5 1.4 %lags.3.refs_0_.lags_ref = bf16[2112,1024]{1,0:T(8,128)(2,1)S(1)} custom-call(bf16[64,1024]{1,0:T(8,128)(2,1)S(1)} %get-tuple-element.30.own_ref), custom_call_target="tpu_custom_call" | custom-call | bytes 8388608 | tf_op jit(solution)/shard_map/lags/pallas_call | solution.py:149
  15.9 0.9 %collective-permute-done.7.ahead_ref.refs_2_ = bf16[128,512]{1,0:T(8,128)(2,1)S(1)} collective-permute-done((bf16[128,512]{1,0:T(8,128)(2,1)S(1)}, bf16[128,512]{1,0:T(8,128)(2,1)S(1)}, u32[]{:S(2)}, u32[]{:S(2)}) %collective-permute-start.7) | collective-permute-done | bytes 131104 | tf_op jit(solution)/shard_map/ppermute | solution.py:39
  16.9 3.6 %collective-permute-done.6.behind_ref.refs_0_ = bf16[128,512]{1,0:T(8,128)(2,1)S(1)} collective-permute-done((bf16[128,512]{1,0:T(8,128)(2,1)S(1)}, bf16[128,512]{1,0:T(8,128)(2,1)S(1)}, u32[]{:S(2)}, u32[]{:S(2)}) %collective-permute-start.6) | collective-permute-done | bytes 131104 | tf_op jit(solution)/shard_map/ppermute | solution.py:39
  20.4 1.6 %collective-permute-start.8 = (bf16[128,512]{1,0:T(8,128)(2,1)S(1)}, bf16[128,512]{1,0:T(8,128)(2,1)S(1)}, u32[]{:S(2)}, u32[]{:S(2)}) collective-permute-start(bf16[128,512]{1,0:T(8,128)(2,1)S(1)} %far.2), channel_id=1, source_target_pairs={{0,4},{2,6},{4,0},{6,2},{8,12},{10,14},{12,8},{14,10},{16,20},{18,... | collective-permute-start | bytes 393224 | tf_op jit(solution)/shard_map/ppermute | solution.py:44
  22.0 1.5 %collective-permute-start.4 = (bf16[128,512]{1,0:T(8,128)(2,1)S(1)}, bf16[128,512]{1,0:T(8,128)(2,1)S(1)}, u32[]{:S(2)}, u32[]{:S(2)}) collective-permute-start(bf16[128,512]{1,0:T(8,128)(2,1)S(1)} %get-tuple-element.27.refs_1_), channel_id=1, source_target_pairs={{0,24},{2,26},{4,28},{6,30},{8,0},{10,2},{12,4},{14,6},{16,8},{18,... | collective-permute-start | bytes 393224 | tf_op jit(solution)/shard_map/ppermute | solution.py:39
  23.5 0.6 %collective-permute-start.3 = (bf16[128,512]{1,0:T(8,128)(2,1)S(1)}, bf16[128,512]{1,0:T(8,128)(2,1)S(1)}, u32[]{:S(2)}, u32[]{:S(2)}) collective-permute-start(bf16[128,512]{1,0:T(8,128)(2,1)S(1)} %get-tuple-element.27.refs_1_), channel_id=1, source_target_pairs={{0,8},{2,10},{4,12},{6,14},{8,16},{10,18},{12,20},{14,22},{16,24},... | collective-permute-start | bytes 393224 | tf_op jit(solution)/shard_map/ppermute | solution.py:39
  24.0 1.4 %collective-permute-done.8.refs_4_ = bf16[128,512]{1,0:T(8,128)(2,1)S(1)} collective-permute-done((bf16[128,512]{1,0:T(8,128)(2,1)S(1)}, bf16[128,512]{1,0:T(8,128)(2,1)S(1)}, u32[]{:S(2)}, u32[]{:S(2)}) %collective-permute-start.8) | collective-permute-done | bytes 131104 | tf_op jit(solution)/shard_map/ppermute | solution.py:44
  25.5 0.4 pick.2
  26.0 0.5 %collective-permute-start.10 = (bf16[128,512]{1,0:T(8,128)(2,1)S(1)}, bf16[128,512]{1,0:T(8,128)(2,1)S(1)}, u32[]{:S(2)}, u32[]{:S(2)}) collective-permute-start(bf16[128,512]{1,0:T(8,128)(2,1)S(1)} %get-tuple-element.31.refs_0_), channel_id=1, source_target_pairs={{0,2},{2,0},{4,6},{6,4},{8,10},{10,8},{12,14},{14,12},{16,18},{18,... | collective-permute-start | bytes 393224 | tf_op jit(solution)/shard_map/ppermute | solution.py:44
  26.5 0.8 %collective-permute-done.4.ahead_ref.refs_2_ = bf16[128,512]{1,0:T(8,128)(2,1)S(1)} collective-permute-done((bf16[128,512]{1,0:T(8,128)(2,1)S(1)}, bf16[128,512]{1,0:T(8,128)(2,1)S(1)}, u32[]{:S(2)}, u32[]{:S(2)}) %collective-permute-start.4) | collective-permute-done | bytes 131104 | tf_op jit(solution)/shard_map/ppermute | solution.py:39
  27.2 3.1 %collective-permute-done.3.behind_ref.refs_0_ = bf16[128,512]{1,0:T(8,128)(2,1)S(1)} collective-permute-done((bf16[128,512]{1,0:T(8,128)(2,1)S(1)}, bf16[128,512]{1,0:T(8,128)(2,1)S(1)}, u32[]{:S(2)}, u32[]{:S(2)}) %collective-permute-start.3) | collective-permute-done | bytes 131104 | tf_op jit(solution)/shard_map/ppermute | solution.py:39
  30.3 0.6 %collective-permute-start.9 = (bf16[128,512]{1,0:T(8,128)(2,1)S(1)}, bf16[128,512]{1,0:T(8,128)(2,1)S(1)}, u32[]{:S(2)}, u32[]{:S(2)}) collective-permute-start(bf16[128,512]{1,0:T(8,128)(2,1)S(1)} %far.3), channel_id=1, source_target_pairs={{0,4},{2,6},{4,0},{6,2},{8,12},{10,14},{12,8},{14,10},{16,20},{18,... | collective-permute-start | bytes 393224 | tf_op jit(solution)/shard_map/ppermute | solution.py:44
  31.1 1.4 %collective-permute-done.2.own_ref = bf16[64,1024]{1,0:T(8,128)(2,1)S(1)} collective-permute-done((bf16[64,1024]{1,0:T(8,128)(2,1)S(1)}, bf16[64,1024]{1,0:T(8,128)(2,1)S(1)}, u32[]{:S(2)}, u32[]{:S(2)}) %collective-permute-start.2) | collective-permute-done | bytes 131104 | tf_op jit(solution)/shard_map/ppermute | solution.py:39
  32.6 1.4 %lags.2.refs_6_.lags_ref = bf16[2112,1024]{1,0:T(8,128)(2,1)S(1)} custom-call(bf16[64,1024]{1,0:T(8,128)(2,1)S(1)} %collective-permute-done.2.own_ref), custom_call_target="tpu_custom_call" | custom-call | bytes 8388608 | tf_op jit(solution)/shard_map/lags/pallas_call | solution.py:149
  34.0 1.4 %collective-permute-done.9.refs_4_ = bf16[128,512]{1,0:T(8,128)(2,1)S(1)} collective-permute-done((bf16[128,512]{1,0:T(8,128)(2,1)S(1)}, bf16[128,512]{1,0:T(8,128)(2,1)S(1)}, u32[]{:S(2)}, u32[]{:S(2)}) %collective-permute-start.9) | collective-permute-done | bytes 131104 | tf_op jit(solution)/shard_map/ppermute | solution.py:44
  35.4 0.4 pick.3
  35.9 0.5 %collective-permute-start.13 = (bf16[128,512]{1,0:T(8,128)(2,1)S(1)}, bf16[128,512]{1,0:T(8,128)(2,1)S(1)}, u32[]{:S(2)}, u32[]{:S(2)}) collective-permute-start(bf16[128,512]{1,0:T(8,128)(2,1)S(1)} %get-tuple-element.36), channel_id=1, source_target_pairs={{0,2},{2,0},{4,6},{6,4},{8,10},{10,8},{12,14},{14,12},{16,18},{18,... | collective-permute-start | bytes 393224 | tf_op jit(solution)/shard_map/ppermute | solution.py:44
  36.4 0.8 %collective-permute-done.12.refs_0_ = bf16[128,512]{1,0:T(8,128)(2,1)S(1)} collective-permute-done((bf16[128,512]{1,0:T(8,128)(2,1)S(1)}, bf16[128,512]{1,0:T(8,128)(2,1)S(1)}, u32[]{:S(2)}, u32[]{:S(2)}) %collective-permute-start.12) | collective-permute-done | bytes 131104 | tf_op jit(solution)/shard_map/ppermute | solution.py:44
  37.2 0.2 collective-permute-done.13.refs_1_
  37.7 0.5 %collective-permute-start.15 = (bf16[2,128,512]{2,1,0:T(8,128)(2,1)S(1)}, bf16[2,128,512]{2,1,0:T(8,128)(2,1)S(1)}, u32[]{:S(2)}, u32[]{:S(2)}) collective-permute-start(bf16[2,128,512]{2,1,0:T(8,128)(2,1)S(1)} %merge.3.refs_1_), channel_id=1, source_target_pairs={{0,1},{1,0},{2,3},{3,2},{4,5},{5,4},{6,7},{7,6},{8,9},{9,8},{10,11... | collective-permute-start | bytes 786440 | tf_op jit(solution)/shard_map/ppermute | solution.py:39
  38.1 1.3 %accumulate.2.refs_1_ = f32[2112,256]{1,0:T(8,128)S(1)} custom-call(bf16[2112,1024]{1,0:T(8,128)(2,1)S(1)} %lags.3.refs_0_.lags_ref, bf16[2,128,512]{2,1,0:T(8,128)(2,1)S(1)} %merge.2.refs_5_.refs_0_, bf16[2,128,512]{2,1,0:T(8,128)(2,1)S(1)} %merge.3.refs_1_), custom_call_target="tpu_custom_call" | custom-call | tf_op jit(solution)/shard_map/accumulate/pallas_call | solution.py:271
  39.5 0.8 %accumulate.3.acc_ref = f32[2112,256]{1,0:T(8,128)S(1)} custom-call(bf16[2112,1024]{1,0:T(8,128)(2,1)S(1)} %lags.2.refs_6_.lags_ref, bf16[2,128,512]{2,1,0:T(8,128)(2,1)S(1)} %collective-permute-done.14.refs_2_.refs_0_, f32[2112,256]{1,0:T(8,128)S(1)} %accumulate.2.refs_1_), custom_call_target="tpu_custom_call" | custom-call | tf_op jit(solution)/shard_map/accumulate/pallas_call | solution.py:271
  40.2 5.9 %collective-permute-done.15.other_ref = bf16[2,128,512]{2,1,0:T(8,128)(2,1)S(1)} collective-permute-done((bf16[2,128,512]{2,1,0:T(8,128)(2,1)S(1)}, bf16[2,128,512]{2,1,0:T(8,128)(2,1)S(1)}, u32[]{:S(2)}, u32[]{:S(2)}) %collective-permute-start.15) | collective-permute-done | bytes 262176 | tf_op jit(solution)/shard_map/ppermute | solution.py:39
  46.1 1.9 %finish.1 = f32[4224,128]{1,0:T(8,128)} custom-call(s32[1,2]{1,0:T(1,128)S(1)} %copy-done.1, bf16[2112,1024]{1,0:T(8,128)(2,1)S(1)} %lags.2.refs_6_.lags_ref, bf16[2,128,512]{2,1,0:T(8,128)(2,1)S(1)} %collective-permute-done.15.other_ref, f32[2112,256]{1,0:T(8,128)S(1)} %accumulate.3.acc_ref), custom_call_target="tpu_custom_call" | custom-call | tf_op jit(solution)/shard_map/finish/pallas_call | solution.py:310
  (20 shorter events, 0.7 us)
Async XLA Ops:
  0.8 8.2 %collective-permute-start = (bf16[128,128]{1,0:T(8,128)(2,1)S(1)}, bf16[128,128]{1,0:T(8,128)(2,1)S(1)}, u32[]{:S(2)}, u32[]{:S(2)}) collective-permute-start(bf16[128,128]{1,0:T(8,128)(2,1)S(1)} %slice.3), channel_id=1, source_target_pairs={{0,1},{2,3},{4,5},{6,7},{8,9},{10,11},{12,13},{14,15},{16,17},{18,... | collective-permute-start | bytes 98312 | tf_op jit(solution)/shard_map/ppermute | solution.py:332
  5.6 3.3 %collective-permute-start.1 = (s32[1,2]{1,0:T(1,128)}, s32[1,2]{1,0:T(1,128)S(1)}, u32[]{:S(2)}, u32[]{:S(2)}) collective-permute-start(s32[1,2]{1,0:T(1,128)} %offsets.5), channel_id=1, source_target_pairs={{0,2},{2,0},{4,6},{6,4},{8,10},{10,8},{12,14},{14,12},{16,18},{18,... | collective-permute-start | bytes 32 | tf_op jit(solution)/shard_map/ppermute | solution.py:44
  5.7 1.2 %copy-start = (bf16[128,4096]{1,0:T(8,128)(2,1)S(1)}, bf16[128,4096]{1,0:T(8,128)(2,1)}, u32[]{:S(2)}) copy-start(bf16[128,4096]{1,0:T(8,128)(2,1)} %records_ref.1) | copy-start | bytes 3145732
  6.9 0.7 %copy-start.2 = (f32[64]{0:T(128)S(1)}, f32[64]{0:T(128)}, u32[]{:S(2)}) copy-start(f32[64]{0:T(128)} %param.4) | copy-start | bytes 772
  9.3 7.5 %collective-permute-start.7 = (bf16[128,512]{1,0:T(8,128)(2,1)S(1)}, bf16[128,512]{1,0:T(8,128)(2,1)S(1)}, u32[]{:S(2)}, u32[]{:S(2)}) collective-permute-start(bf16[128,512]{1,0:T(8,128)(2,1)S(1)} %get-tuple-element.29.refs_1_), channel_id=1, source_target_pairs={{0,24},{2,26},{4,28},{6,30},{8,0},{10,2},{12,4},{14,6},{16,8},{18,... | collective-permute-start | bytes 393224 | tf_op jit(solution)/shard_map/ppermute | solution.py:39
  13.0 7.4 %collective-permute-start.6 = (bf16[128,512]{1,0:T(8,128)(2,1)S(1)}, bf16[128,512]{1,0:T(8,128)(2,1)S(1)}, u32[]{:S(2)}, u32[]{:S(2)}) collective-permute-start(bf16[128,512]{1,0:T(8,128)(2,1)S(1)} %get-tuple-element.29.refs_1_), channel_id=1, source_target_pairs={{0,8},{2,10},{4,12},{6,14},{8,16},{10,18},{12,20},{14,22},{16,24},... | collective-permute-start | bytes 393224 | tf_op jit(solution)/shard_map/ppermute | solution.py:39
  13.0 11.0 %collective-permute-start.5 = (bf16[128,1024]{1,0:T(8,128)(2,1)S(1)}, bf16[128,1024]{1,0:T(8,128)(2,1)S(1)}, u32[]{:S(2)}, u32[]{:S(2)}) collective-permute-start(bf16[128,1024]{1,0:T(8,128)(2,1)S(1)} %get-tuple-element.28), channel_id=1, source_target_pairs={{0,4},{2,6},{4,0},{6,2},{8,12},{10,14},{12,8},{14,10},{16,20},{18,... | collective-permute-start | bytes 786440 | tf_op jit(solution)/shard_map/ppermute | solution.py:44
  15.9 9.5 %copy-start.1 = (s32[1,2]{1,0:T(1,128)S(1)}, s32[1,2]{1,0:T(1,128)}, u32[]{:S(2)}) copy-start(s32[1,2]{1,0:T(1,128)} %offsets.5) | copy-start | bytes 28
  20.4 5.0 %collective-permute-start.8 = (bf16[128,512]{1,0:T(8,128)(2,1)S(1)}, bf16[128,512]{1,0:T(8,128)(2,1)S(1)}, u32[]{:S(2)}, u32[]{:S(2)}) collective-permute-start(bf16[128,512]{1,0:T(8,128)(2,1)S(1)} %far.2), channel_id=1, source_target_pairs={{0,4},{2,6},{4,0},{6,2},{8,12},{10,14},{12,8},{14,10},{16,20},{18,... | collective-permute-start | bytes 393224 | tf_op jit(solution)/shard_map/ppermute | solution.py:44
  22.0 5.2 %collective-permute-start.4 = (bf16[128,512]{1,0:T(8,128)(2,1)S(1)}, bf16[128,512]{1,0:T(8,128)(2,1)S(1)}, u32[]{:S(2)}, u32[]{:S(2)}) collective-permute-start(bf16[128,512]{1,0:T(8,128)(2,1)S(1)} %get-tuple-element.27.refs_1_), channel_id=1, source_target_pairs={{0,24},{2,26},{4,28},{6,30},{8,0},{10,2},{12,4},{14,6},{16,8},{18,... | collective-permute-start | bytes 393224 | tf_op jit(solution)/shard_map/ppermute | solution.py:39
  23.5 6.9 %collective-permute-start.3 = (bf16[128,512]{1,0:T(8,128)(2,1)S(1)}, bf16[128,512]{1,0:T(8,128)(2,1)S(1)}, u32[]{:S(2)}, u32[]{:S(2)}) collective-permute-start(bf16[128,512]{1,0:T(8,128)(2,1)S(1)} %get-tuple-element.27.refs_1_), channel_id=1, source_target_pairs={{0,8},{2,10},{4,12},{6,14},{8,16},{10,18},{12,20},{14,22},{16,24},... | collective-permute-start | bytes 393224 | tf_op jit(solution)/shard_map/ppermute | solution.py:39
  25.9 5.1 %collective-permute-start.11 = (bf16[128,512]{1,0:T(8,128)(2,1)S(1)}, bf16[128,512]{1,0:T(8,128)(2,1)S(1)}, u32[]{:S(2)}, u32[]{:S(2)}) collective-permute-start(bf16[128,512]{1,0:T(8,128)(2,1)S(1)} %get-tuple-element.33), channel_id=1, source_target_pairs={{0,2},{2,0},{4,6},{6,4},{8,10},{10,8},{12,14},{14,12},{16,18},{18,... | collective-permute-start | bytes 393224 | tf_op jit(solution)/shard_map/ppermute | solution.py:44
  26.0 5.0 %collective-permute-start.10 = (bf16[128,512]{1,0:T(8,128)(2,1)S(1)}, bf16[128,512]{1,0:T(8,128)(2,1)S(1)}, u32[]{:S(2)}, u32[]{:S(2)}) collective-permute-start(bf16[128,512]{1,0:T(8,128)(2,1)S(1)} %get-tuple-element.31.refs_0_), channel_id=1, source_target_pairs={{0,2},{2,0},{4,6},{6,4},{8,10},{10,8},{12,14},{14,12},{16,18},{18,... | collective-permute-start | bytes 393224 | tf_op jit(solution)/shard_map/ppermute | solution.py:44
  26.5 6.1 %collective-permute-start.2 = (bf16[64,1024]{1,0:T(8,128)(2,1)S(1)}, bf16[64,1024]{1,0:T(8,128)(2,1)S(1)}, u32[]{:S(2)}, u32[]{:S(2)}) collective-permute-start(bf16[64,1024]{1,0:T(8,128)(2,1)S(1)} %get-tuple-element.25), channel_id=1, source_target_pairs={{0,1},{1,0},{2,3},{3,2},{4,5},{5,4},{6,7},{7,6},{8,9},{9,8},{10,11... | collective-permute-start | bytes 393224 | tf_op jit(solution)/shard_map/ppermute | solution.py:39
  30.3 5.0 %collective-permute-start.9 = (bf16[128,512]{1,0:T(8,128)(2,1)S(1)}, bf16[128,512]{1,0:T(8,128)(2,1)S(1)}, u32[]{:S(2)}, u32[]{:S(2)}) collective-permute-start(bf16[128,512]{1,0:T(8,128)(2,1)S(1)} %far.3), channel_id=1, source_target_pairs={{0,4},{2,6},{4,0},{6,2},{8,12},{10,14},{12,8},{14,10},{16,20},{18,... | collective-permute-start | bytes 393224 | tf_op jit(solution)/shard_map/ppermute | solution.py:44
  31.0 6.5 %collective-permute-start.14 = (bf16[2,128,512]{2,1,0:T(8,128)(2,1)S(1)}, bf16[2,128,512]{2,1,0:T(8,128)(2,1)S(1)}, u32[]{:S(2)}, u32[]{:S(2)}) collective-permute-start(bf16[2,128,512]{2,1,0:T(8,128)(2,1)S(1)} %merge.2.refs_5_.refs_0_), channel_id=1, source_target_pairs={{0,1},{1,0},{2,3},{3,2},{4,5},{5,4},{6,7},{7,6},{8,9},{9,8},{10,11... | collective-permute-start | bytes 786440 | tf_op jit(solution)/shard_map/ppermute | solution.py:39
  35.8 1.4 %collective-permute-start.12 = (bf16[128,512]{1,0:T(8,128)(2,1)S(1)}, bf16[128,512]{1,0:T(8,128)(2,1)S(1)}, u32[]{:S(2)}, u32[]{:S(2)}) collective-permute-start(bf16[128,512]{1,0:T(8,128)(2,1)S(1)} %get-tuple-element.35), channel_id=1, source_target_pairs={{0,2},{2,0},{4,6},{6,4},{8,10},{10,8},{12,14},{14,12},{16,18},{18,... | collective-permute-start | bytes 393224 | tf_op jit(solution)/shard_map/ppermute | solution.py:44
  35.9 1.5 %collective-permute-start.13 = (bf16[128,512]{1,0:T(8,128)(2,1)S(1)}, bf16[128,512]{1,0:T(8,128)(2,1)S(1)}, u32[]{:S(2)}, u32[]{:S(2)}) collective-permute-start(bf16[128,512]{1,0:T(8,128)(2,1)S(1)} %get-tuple-element.36), channel_id=1, source_target_pairs={{0,2},{2,0},{4,6},{6,4},{8,10},{10,8},{12,14},{14,12},{16,18},{18,... | collective-permute-start | bytes 393224 | tf_op jit(solution)/shard_map/ppermute | solution.py:44
  37.7 8.4 %collective-permute-start.15 = (bf16[2,128,512]{2,1,0:T(8,128)(2,1)S(1)}, bf16[2,128,512]{2,1,0:T(8,128)(2,1)S(1)}, u32[]{:S(2)}, u32[]{:S(2)}) collective-permute-start(bf16[2,128,512]{2,1,0:T(8,128)(2,1)S(1)} %merge.3.refs_1_), channel_id=1, source_target_pairs={{0,1},{1,0},{2,3},{3,2},{4,5},{5,4},{6,7},{7,6},{8,9},{9,8},{10,11... | collective-permute-start | bytes 786440 | tf_op jit(solution)/shard_map/ppermute | solution.py:39

commit v4 on v3

--- a/solution.py
+++ b/solution.py
@@ -21,6 +21,7 @@
 EDGES = (0, 512, 1024)
 CHUNKS = len(EDGES) - 1
 TEAM = 4
+HEAD_GRANT = 52 << 20
 GROUP = 16
 VMEM = pltpu.VMEM
 F32 = jnp.float32
@@ -42,6 +43,35 @@
 def swap(x, bit):
     n = lax.axis_size("chan")
     return lax.ppermute(x, "chan", [(i, i ^ bit) for i in range(n)])
+
+
+def head_kernel(records_ref, taps_ref, tail_out, records_out, taps_out, sems):
+    last = records_ref.shape[1] - LANES
+    copies = [
+        pltpu.make_async_copy(taps_ref, taps_out, sems.at[0]),
+        pltpu.make_async_copy(records_ref.at[:, pl.ds(last, LANES)], tail_out, sems.at[1]),
+        pltpu.make_async_copy(records_ref, records_out, sems.at[2]),
+    ]
+    for copy in copies:
+        copy.start()
+    for copy in copies:
+        copy.wait()
+
+
+def head(records, fir_taps):
+    return pl.pallas_call(
+        head_kernel,
+        out_shape=[
+            jax.ShapeDtypeStruct((records.shape[0], LANES), BF16),
+            jax.ShapeDtypeStruct(records.shape, BF16),
+            jax.ShapeDtypeStruct((1, TAPS), F32),
+        ],
+        in_specs=[HBM_SPEC] * 2,
+        out_specs=[VMEM_SPEC] * 3,
+        scratch_shapes=[pltpu.SemaphoreType.DMA((3,))],
+        compiler_params=pltpu.CompilerParams(vmem_limit_bytes=HEAD_GRANT),
+        name="head",
+    )(records, fir_taps.reshape(1, TAPS))
 
 
 def filter_kernel(records_ref, taps_ref, filtered, squares_ref, band_ref, line):
@@ -57,21 +87,20 @@
     low = (rest - mid.astype(F32)).astype(BF16)
     weights = jnp.concatenate([high, mid, low], axis=0)
     band_ref[...] = weights[:, :LANES]
+    blocks = [jnp.concatenate([jnp.zeros((channels, LANES), BF16), records_ref[:, :RAW]], axis=1)]
+    blocks += [records_ref[:, tile * RAW - LANES : (tile + 1) * RAW] for tile in range(1, TILES)]
+    out = lax.dot_general(jnp.concatenate(blocks, axis=0), weights, NT, preferred_element_type=F32)
     squares = jnp.zeros((channels, LANES), F32)
     for tile in range(TILES):
-        if tile == 0:
-            block, used = records_ref[:, :RAW], weights[:, LANES:]
-        else:
-            block, used = records_ref[:, tile * RAW - LANES : (tile + 1) * RAW], weights
-        out = lax.dot_general(block, used, NT, preferred_element_type=F32)
-        value = out[:, :LANES] + (out[:, LANES : 2 * LANES] + out[:, 2 * LANES :])
+        rows = slice(tile * channels, (tile + 1) * channels)
+        value = out[rows, :LANES] + (out[rows, LANES : 2 * LANES] + out[rows, 2 * LANES :])
         filtered[:, tile * LANES : (tile + 1) * LANES] = value
         if tile > 0:
             squares = squares + value * value
     squares_ref[...] = squares
 
 
-def bulk_filter(records, fir_taps):
+def bulk_filter(records, taps):
     channels = records.shape[0]
     return pl.pallas_call(
         filter_kernel,
@@ -85,7 +114,7 @@
         scratch_shapes=[VMEM((8, SPAN), F32)],
         compiler_params=grant(4),
         name="bulk_filter",
-    )(records, fir_taps.reshape(1, TAPS))
+    )(records, taps)
 
 
 def whiten_kernel(win, tail_ref, band_ref, filtered, squares_ref, *refs):
@@ -328,10 +357,10 @@
     hops = reach // TEAM
     factor = 1.0 / math.sqrt(T_DEC * win)
 
-    tail = records[:, records.shape[1] - LANES :]
+    tail, records, taps = head(records, fir_taps)
     before = lax.ppermute(tail, "win", [(i, i + 1) for i in range(win - 1)])
     core_offsets = swap(pair_offsets, 1)
-    filtered, squares, band = bulk_filter(records, fir_taps)
+    filtered, squares, band = bulk_filter(records, taps)
     before, core_offsets = lax.optimization_barrier((before, core_offsets))
     outs = whiten(before, band, filtered, squares)
     chunks, row_parts, whole = outs[:CHUNKS], outs[CHUNKS:-1], outs[-1]

time: 48.3 us -> 47.2 us (0.977)
  waiting for transfers between devices: 19.7 us -> 15.1 us
  starting transfers between devices: 16 us -> 20.5 us
  local copies, waits for them, and re-layouts: 2.64 us -> 0.66 us
  Pallas kernels: 9.6 us -> 10.6 us
    ppermute x7, waiting for transfers between devices: 15.8 us -> 11.2 us  [shift(): return lax.ppermute(x, axis, [(i, (i + by) % n) for i in range(n)])]
    ppermute x7, starting transfers between devices: 6.24 us -> 10.4 us  [shift(): return lax.ppermute(x, axis, [(i, (i + by) % n) for i in range(n)])]
    pallas_call x0 -> x1, Pallas kernels: none -> 1.33 us  [head(): pl.pallas_call(head_kernel, out_shape=[jax.ShapeDtypeStruct((records.shap...]
    unnamed x6 -> x4, local copies, waits for them, and re-layouts: 1.88 us -> 0.66 us
    slice x1 -> x0, local copies, waits for them, and re-layouts: 0.76 us -> none  [body(): tail = records[:, records.shape[1] - LANES:]]
  transfers between devices with their start and end apart: 16 -> 16, of which waited for: 11 -> 12; matrix products, arithmetic and copies ran while one was open for 0% -> 0% of each run, Pallas kernels for 15% -> 15%
where the time goes in v4:
time: 47.2 us; the launch traced here: 47 us
  starting transfers between devices  20.5 us (43%)
  waiting for transfers between devices  15.1 us (32%)
  Pallas kernels  10.6 us (22%)
  local copies, waits for them, and re-layouts  0.66 us (1%)
    ppermute x7, waiting for transfers between devices, shift(): return lax.ppermute(x, axis, [(i, (i + by) % n) for i in range(n)])  11.2 us
    ppermute x7, starting transfers between devices, shift(): return lax.ppermute(x, axis, [(i, (i + by) % n) for i in range(n)])  10.4 us
    ppermute x8, starting transfers between devices, swap(): return lax.ppermute(x, 'chan', [(i, i ^ bit) for i in range(n)])  5.2 us
    ppermute x1, starting transfers between devices, body(): before = lax.ppermute(tail, 'win', [(i, i + 1) for i in range(win - 1)])  4.87 us
    ppermute x8, waiting for transfers between devices, swap(): return lax.ppermute(x, 'chan', [(i, i ^ bit) for i in range(n)])  3.7 us
    pallas_call x2, Pallas kernels, lay_out_lags(): pl.pallas_call(lags_kernel, out_shape=jax.ShapeDtypeStruct((rows * LAGS,...  2.84 us
    pallas_call x2, Pallas kernels, accumulate(): pl.pallas_call(functools.partial(accumulate_kernel, firsts, acc is not No...  2.09 us
    pallas_call x1, Pallas kernels, finish(): pl.pallas_call(functools.partial(finish_kernel, reach, factor, first), ou...  1.91 us
  transfers between devices with their start and end apart: 16, of which 12 were waited for; matrix products, arithmetic and copies ran while one was open for 0% of the time, Pallas kernels for 15%

profile of v4, /device:TPU:0, one launch (start us, length us, event | category | flops | bytes accessed | tf_op | source)
XLA Modules:
  0.0 47.0 jit_solution(17054901642191829886)
XLA Ops:
  0.0 0.7 %copy-done.1 = f32[64]{0:T(128)S(1)} copy-done((f32[64]{0:T(128)S(1)}, f32[64]{0:T(128)}, u32[]{:S(2)}) %copy-start.1) | copy-done | bytes 280
  0.7 1.3 %head.1 = (bf16[128,128]{1,0:T(8,128)(2,1)S(1)}, bf16[128,4096]{1,0:T(8,128)(2,1)S(1)}, f32[1,64]{1,0:T(1,128)S(1)}) custom-call(bf16[128,4096]{1,0:T(8,128)(2,1)} %records_ref.1, f32[1,64]{1,0:T(1,128)S(1)} %bitcast.4), custom_call_target="tpu_custom_call" | custom-call | tf_op jit(solution)/shard_map/head/pallas_call | solution.py:62
  2.0 4.9 %collective-permute-start = (bf16[128,128]{1,0:T(8,128)(2,1)S(1)}, bf16[128,128]{1,0:T(8,128)(2,1)S(1)}, u32[]{:S(2)}, u32[]{:S(2)}) collective-permute-start(bf16[128,128]{1,0:T(8,128)(2,1)S(1)} %get-tuple-element.24), channel_id=1, source_target_pairs={{0,1},{2,3},{4,5},{6,7},{8,9},{10,11},{12,13},{14,15},{16,17},{18,... | collective-permute-start | bytes 98312 | tf_op jit(solution)/shard_map/ppermute | solution.py:361
  7.0 1.0 %bulk_filter.1 = (f32[128,1024]{1,0:T(8,128)S(1)}, f32[128,128]{1,0:T(8,128)S(1)}, bf16[384,128]{1,0:T(8,128)(2,1)S(1)}) custom-call(bf16[128,4096]{1,0:T(8,128)(2,1)S(1)} %get-tuple-element.26.records_ref, f32[1,64]{1,0:T(1,128)S(1)} %get-tuple-element.27.taps_ref), custom_call_target="tpu_custom_call" | custom-call | tf_op jit(solution)/shard_map/bulk_filter/pallas_call | solution.py:105
  8.5 0.4 whiten.1
  8.8 3.7 %collective-permute-start.7 = (bf16[128,512]{1,0:T(8,128)(2,1)S(1)}, bf16[128,512]{1,0:T(8,128)(2,1)S(1)}, u32[]{:S(2)}, u32[]{:S(2)}) collective-permute-start(bf16[128,512]{1,0:T(8,128)(2,1)S(1)} %get-tuple-element.35.refs_1_), channel_id=1, source_target_pairs={{0,24},{2,26},{4,28},{6,30},{8,0},{10,2},{12,4},{14,6},{16,8},{18,... | collective-permute-start | bytes 393224 | tf_op jit(solution)/shard_map/ppermute | solution.py:40
  12.5 1.5 %collective-permute-start.5 = (bf16[128,1024]{1,0:T(8,128)(2,1)S(1)}, bf16[128,1024]{1,0:T(8,128)(2,1)S(1)}, u32[]{:S(2)}, u32[]{:S(2)}) collective-permute-start(bf16[128,1024]{1,0:T(8,128)(2,1)S(1)} %get-tuple-element.34), channel_id=1, source_target_pairs={{0,4},{2,6},{4,0},{6,2},{8,12},{10,14},{12,8},{14,10},{16,20},{18,... | collective-permute-start | bytes 786440 | tf_op jit(solution)/shard_map/ppermute | solution.py:45
  14.0 1.4 %lags.3.refs_0_.lags_ref = bf16[2112,1024]{1,0:T(8,128)(2,1)S(1)} custom-call(bf16[64,1024]{1,0:T(8,128)(2,1)S(1)} %get-tuple-element.36.own_ref), custom_call_target="tpu_custom_call" | custom-call | bytes 8388608 | tf_op jit(solution)/shard_map/lags/pallas_call | solution.py:178
  15.4 1.0 %collective-permute-done.7.ahead_ref.refs_2_ = bf16[128,512]{1,0:T(8,128)(2,1)S(1)} collective-permute-done((bf16[128,512]{1,0:T(8,128)(2,1)S(1)}, bf16[128,512]{1,0:T(8,128)(2,1)S(1)}, u32[]{:S(2)}, u32[]{:S(2)}) %collective-permute-start.7) | collective-permute-done | bytes 131104 | tf_op jit(solution)/shard_map/ppermute | solution.py:40
  16.4 3.0 %collective-permute-done.6.behind_ref.refs_0_ = bf16[128,512]{1,0:T(8,128)(2,1)S(1)} collective-permute-done((bf16[128,512]{1,0:T(8,128)(2,1)S(1)}, bf16[128,512]{1,0:T(8,128)(2,1)S(1)}, u32[]{:S(2)}, u32[]{:S(2)}) %collective-permute-start.6) | collective-permute-done | bytes 131104 | tf_op jit(solution)/shard_map/ppermute | solution.py:40
  19.5 1.6 %collective-permute-start.8 = (bf16[128,512]{1,0:T(8,128)(2,1)S(1)}, bf16[128,512]{1,0:T(8,128)(2,1)S(1)}, u32[]{:S(2)}, u32[]{:S(2)}) collective-permute-start(bf16[128,512]{1,0:T(8,128)(2,1)S(1)} %far.2), channel_id=1, source_target_pairs={{0,4},{2,6},{4,0},{6,2},{8,12},{10,14},{12,8},{14,10},{16,20},{18,... | collective-permute-start | bytes 393224 | tf_op jit(solution)/shard_map/ppermute | solution.py:45
  21.0 1.5 %collective-permute-start.4 = (bf16[128,512]{1,0:T(8,128)(2,1)S(1)}, bf16[128,512]{1,0:T(8,128)(2,1)S(1)}, u32[]{:S(2)}, u32[]{:S(2)}) collective-permute-start(bf16[128,512]{1,0:T(8,128)(2,1)S(1)} %get-tuple-element.33.refs_1_), channel_id=1, source_target_pairs={{0,24},{2,26},{4,28},{6,30},{8,0},{10,2},{12,4},{14,6},{16,8},{18,... | collective-permute-start | bytes 393224 | tf_op jit(solution)/shard_map/ppermute | solution.py:40
  22.5 0.6 %collective-permute-start.3 = (bf16[128,512]{1,0:T(8,128)(2,1)S(1)}, bf16[128,512]{1,0:T(8,128)(2,1)S(1)}, u32[]{:S(2)}, u32[]{:S(2)}) collective-permute-start(bf16[128,512]{1,0:T(8,128)(2,1)S(1)} %get-tuple-element.33.refs_1_), channel_id=1, source_target_pairs={{0,8},{2,10},{4,12},{6,14},{8,16},{10,18},{12,20},{14,22},{16,24},... | collective-permute-start | bytes 393224 | tf_op jit(solution)/shard_map/ppermute | solution.py:40
  23.0 1.4 %collective-permute-done.8.refs_4_ = bf16[128,512]{1,0:T(8,128)(2,1)S(1)} collective-permute-done((bf16[128,512]{1,0:T(8,128)(2,1)S(1)}, bf16[128,512]{1,0:T(8,128)(2,1)S(1)}, u32[]{:S(2)}, u32[]{:S(2)}) %collective-permute-start.8) | collective-permute-done | bytes 131104 | tf_op jit(solution)/shard_map/ppermute | solution.py:45
  24.5 0.4 pick.2
  25.0 0.5 %collective-permute-start.10 = (bf16[128,512]{1,0:T(8,128)(2,1)S(1)}, bf16[128,512]{1,0:T(8,128)(2,1)S(1)}, u32[]{:S(2)}, u32[]{:S(2)}) collective-permute-start(bf16[128,512]{1,0:T(8,128)(2,1)S(1)} %get-tuple-element.37.refs_0_), channel_id=1, source_target_pairs={{0,2},{2,0},{4,6},{6,4},{8,10},{10,8},{12,14},{14,12},{16,18},{18,... | collective-permute-start | bytes 393224 | tf_op jit(solution)/shard_map/ppermute | solution.py:45
  25.5 2.6 %collective-permute-start.2 = (bf16[64,1024]{1,0:T(8,128)(2,1)S(1)}, bf16[64,1024]{1,0:T(8,128)(2,1)S(1)}, u32[]{:S(2)}, u32[]{:S(2)}) collective-permute-start(bf16[64,1024]{1,0:T(8,128)(2,1)S(1)} %get-tuple-element.31), channel_id=1, source_target_pairs={{0,1},{1,0},{2,3},{3,2},{4,5},{5,4},{6,7},{7,6},{8,9},{9,8},{10,11... | collective-permute-start | bytes 393224 | tf_op jit(solution)/shard_map/ppermute | solution.py:40
  28.1 1.1 %collective-permute-done.3.behind_ref.refs_0_ = bf16[128,512]{1,0:T(8,128)(2,1)S(1)} collective-permute-done((bf16[128,512]{1,0:T(8,128)(2,1)S(1)}, bf16[128,512]{1,0:T(8,128)(2,1)S(1)}, u32[]{:S(2)}, u32[]{:S(2)}) %collective-permute-start.3) | collective-permute-done | bytes 131104 | tf_op jit(solution)/shard_map/ppermute | solution.py:40
  29.3 0.9 %collective-permute-start.9 = (bf16[128,512]{1,0:T(8,128)(2,1)S(1)}, bf16[128,512]{1,0:T(8,128)(2,1)S(1)}, u32[]{:S(2)}, u32[]{:S(2)}) collective-permute-start(bf16[128,512]{1,0:T(8,128)(2,1)S(1)} %far.3), channel_id=1, source_target_pairs={{0,4},{2,6},{4,0},{6,2},{8,12},{10,14},{12,8},{14,10},{16,20},{18,... | collective-permute-start | bytes 393224 | tf_op jit(solution)/shard_map/ppermute | solution.py:45
  30.3 1.0 %collective-permute-start.14 = (bf16[2,128,512]{2,1,0:T(8,128)(2,1)S(1)}, bf16[2,128,512]{2,1,0:T(8,128)(2,1)S(1)}, u32[]{:S(2)}, u32[]{:S(2)}) collective-permute-start(bf16[2,128,512]{2,1,0:T(8,128)(2,1)S(1)} %merge.2.refs_5_.refs_0_), channel_id=1, source_target_pairs={{0,1},{1,0},{2,3},{3,2},{4,5},{5,4},{6,7},{7,6},{8,9},{9,8},{10,11... | collective-permute-start | bytes 786440 | tf_op jit(solution)/shard_map/ppermute | solution.py:40
  31.3 0.6 %collective-permute-done.2.own_ref = bf16[64,1024]{1,0:T(8,128)(2,1)S(1)} collective-permute-done((bf16[64,1024]{1,0:T(8,128)(2,1)S(1)}, bf16[64,1024]{1,0:T(8,128)(2,1)S(1)}, u32[]{:S(2)}, u32[]{:S(2)}) %collective-permute-start.2) | collective-permute-done | bytes 131104 | tf_op jit(solution)/shard_map/ppermute | solution.py:40
  31.9 1.4 %lags.2.refs_6_.lags_ref = bf16[2112,1024]{1,0:T(8,128)(2,1)S(1)} custom-call(bf16[64,1024]{1,0:T(8,128)(2,1)S(1)} %collective-permute-done.2.own_ref), custom_call_target="tpu_custom_call" | custom-call | bytes 8388608 | tf_op jit(solution)/shard_map/lags/pallas_call | solution.py:178
  33.3 1.0 %collective-permute-done.9.refs_4_ = bf16[128,512]{1,0:T(8,128)(2,1)S(1)} collective-permute-done((bf16[128,512]{1,0:T(8,128)(2,1)S(1)}, bf16[128,512]{1,0:T(8,128)(2,1)S(1)}, u32[]{:S(2)}, u32[]{:S(2)}) %collective-permute-start.9) | collective-permute-done | bytes 131104 | tf_op jit(solution)/shard_map/ppermute | solution.py:45
  34.3 0.4 pick.3
  34.8 0.5 %collective-permute-start.13 = (bf16[128,512]{1,0:T(8,128)(2,1)S(1)}, bf16[128,512]{1,0:T(8,128)(2,1)S(1)}, u32[]{:S(2)}, u32[]{:S(2)}) collective-permute-start(bf16[128,512]{1,0:T(8,128)(2,1)S(1)} %get-tuple-element.42), channel_id=1, source_target_pairs={{0,2},{2,0},{4,6},{6,4},{8,10},{10,8},{12,14},{14,12},{16,18},{18,... | collective-permute-start | bytes 393224 | tf_op jit(solution)/shard_map/ppermute | solution.py:45
  35.3 0.8 %collective-permute-done.12.refs_0_ = bf16[128,512]{1,0:T(8,128)(2,1)S(1)} collective-permute-done((bf16[128,512]{1,0:T(8,128)(2,1)S(1)}, bf16[128,512]{1,0:T(8,128)(2,1)S(1)}, u32[]{:S(2)}, u32[]{:S(2)}) %collective-permute-start.12) | collective-permute-done | bytes 131104 | tf_op jit(solution)/shard_map/ppermute | solution.py:45
  36.3 1.8 %collective-permute-done.14.refs_2_.refs_0_ = bf16[2,128,512]{2,1,0:T(8,128)(2,1)S(1)} collective-permute-done((bf16[2,128,512]{2,1,0:T(8,128)(2,1)S(1)}, bf16[2,128,512]{2,1,0:T(8,128)(2,1)S(1)}, u32[]{:S(2)}, u32[]{:S(2)}) %collective-permute-start.14) | collective-permute-done | bytes 262176 | tf_op jit(solution)/shard_map/ppermute | solution.py:40
  38.2 1.1 %collective-permute-start.15 = (bf16[2,128,512]{2,1,0:T(8,128)(2,1)S(1)}, bf16[2,128,512]{2,1,0:T(8,128)(2,1)S(1)}, u32[]{:S(2)}, u32[]{:S(2)}) collective-permute-start(bf16[2,128,512]{2,1,0:T(8,128)(2,1)S(1)} %merge.3.refs_1_), channel_id=1, source_target_pairs={{0,1},{1,0},{2,3},{3,2},{4,5},{5,4},{6,7},{7,6},{8,9},{9,8},{10,11... | collective-permute-start | bytes 786440 | tf_op jit(solution)/shard_map/ppermute | solution.py:40
  39.4 1.3 %accumulate.2.refs_1_ = f32[2112,256]{1,0:T(8,128)S(1)} custom-call(bf16[2112,1024]{1,0:T(8,128)(2,1)S(1)} %lags.3.refs_0_.lags_ref, bf16[2,128,512]{2,1,0:T(8,128)(2,1)S(1)} %merge.2.refs_5_.refs_0_, bf16[2,128,512]{2,1,0:T(8,128)(2,1)S(1)} %merge.3.refs_1_), custom_call_target="tpu_custom_call" | custom-call | tf_op jit(solution)/shard_map/accumulate/pallas_call | solution.py:300
  40.7 0.8 %accumulate.3.acc_ref = f32[2112,256]{1,0:T(8,128)S(1)} custom-call(bf16[2112,1024]{1,0:T(8,128)(2,1)S(1)} %lags.2.refs_6_.lags_ref, bf16[2,128,512]{2,1,0:T(8,128)(2,1)S(1)} %collective-permute-done.14.refs_2_.refs_0_, f32[2112,256]{1,0:T(8,128)S(1)} %accumulate.2.refs_1_), custom_call_target="tpu_custom_call" | custom-call | tf_op jit(solution)/shard_map/accumulate/pallas_call | solution.py:300
  41.5 3.6 %collective-permute-done.15.other_ref = bf16[2,128,512]{2,1,0:T(8,128)(2,1)S(1)} collective-permute-done((bf16[2,128,512]{2,1,0:T(8,128)(2,1)S(1)}, bf16[2,128,512]{2,1,0:T(8,128)(2,1)S(1)}, u32[]{:S(2)}, u32[]{:S(2)}) %collective-permute-start.15) | collective-permute-done | bytes 262176 | tf_op jit(solution)/shard_map/ppermute | solution.py:40
  45.1 1.9 %finish.1 = f32[4224,128]{1,0:T(8,128)} custom-call(s32[1,2]{1,0:T(1,128)S(1)} %copy-done, bf16[2112,1024]{1,0:T(8,128)(2,1)S(1)} %lags.2.refs_6_.lags_ref, bf16[2,128,512]{2,1,0:T(8,128)(2,1)S(1)} %collective-permute-done.15.other_ref, f32[2112,256]{1,0:T(8,128)S(1)} %accumulate.3.acc_ref), custom_call_target="tpu_custom_call" | custom-call | tf_op jit(solution)/shard_map/finish/pallas_call | solution.py:339
  (18 shorter events, 1.1 us)
Async XLA Ops:
  0.0 0.7 %copy-start.1 = (f32[64]{0:T(128)S(1)}, f32[64]{0:T(128)}, u32[]{:S(2)}) copy-start(f32[64]{0:T(128)} %param.4) | copy-start | bytes 772
  2.0 6.5 %collective-permute-start = (bf16[128,128]{1,0:T(8,128)(2,1)S(1)}, bf16[128,128]{1,0:T(8,128)(2,1)S(1)}, u32[]{:S(2)}, u32[]{:S(2)}) collective-permute-start(bf16[128,128]{1,0:T(8,128)(2,1)S(1)} %get-tuple-element.24), channel_id=1, source_target_pairs={{0,1},{2,3},{4,5},{6,7},{8,9},{10,11},{12,13},{14,15},{16,17},{18,... | collective-permute-start | bytes 98312 | tf_op jit(solution)/shard_map/ppermute | solution.py:361
  6.9 1.3 %collective-permute-start.1 = (s32[1,2]{1,0:T(1,128)}, s32[1,2]{1,0:T(1,128)S(1)}, u32[]{:S(2)}, u32[]{:S(2)}) collective-permute-start(s32[1,2]{1,0:T(1,128)} %offsets.5), channel_id=1, source_target_pairs={{0,2},{2,0},{4,6},{6,4},{8,10},{10,8},{12,14},{14,12},{16,18},{18,... | collective-permute-start | bytes 32 | tf_op jit(solution)/shard_map/ppermute | solution.py:45
  8.8 7.6 %collective-permute-start.7 = (bf16[128,512]{1,0:T(8,128)(2,1)S(1)}, bf16[128,512]{1,0:T(8,128)(2,1)S(1)}, u32[]{:S(2)}, u32[]{:S(2)}) collective-permute-start(bf16[128,512]{1,0:T(8,128)(2,1)S(1)} %get-tuple-element.35.refs_1_), channel_id=1, source_target_pairs={{0,24},{2,26},{4,28},{6,30},{8,0},{10,2},{12,4},{14,6},{16,8},{18,... | collective-permute-start | bytes 393224 | tf_op jit(solution)/shard_map/ppermute | solution.py:40
  12.5 7.0 %collective-permute-start.6 = (bf16[128,512]{1,0:T(8,128)(2,1)S(1)}, bf16[128,512]{1,0:T(8,128)(2,1)S(1)}, u32[]{:S(2)}, u32[]{:S(2)}) collective-permute-start(bf16[128,512]{1,0:T(8,128)(2,1)S(1)} %get-tuple-element.35.refs_1_), channel_id=1, source_target_pairs={{0,8},{2,10},{4,12},{6,14},{8,16},{10,18},{12,20},{14,22},{16,24},... | collective-permute-start | bytes 393224 | tf_op jit(solution)/shard_map/ppermute | solution.py:40
  12.5 10.6 %collective-permute-start.5 = (bf16[128,1024]{1,0:T(8,128)(2,1)S(1)}, bf16[128,1024]{1,0:T(8,128)(2,1)S(1)}, u32[]{:S(2)}, u32[]{:S(2)}) collective-permute-start(bf16[128,1024]{1,0:T(8,128)(2,1)S(1)} %get-tuple-element.34), channel_id=1, source_target_pairs={{0,4},{2,6},{4,0},{6,2},{8,12},{10,14},{12,8},{14,10},{16,20},{18,... | collective-permute-start | bytes 786440 | tf_op jit(solution)/shard_map/ppermute | solution.py:45
  15.4 9.1 %copy-start = (s32[1,2]{1,0:T(1,128)S(1)}, s32[1,2]{1,0:T(1,128)}, u32[]{:S(2)}) copy-start(s32[1,2]{1,0:T(1,128)} %offsets.5) | copy-start | bytes 28
  19.5 5.0 %collective-permute-start.8 = (bf16[128,512]{1,0:T(8,128)(2,1)S(1)}, bf16[128,512]{1,0:T(8,128)(2,1)S(1)}, u32[]{:S(2)}, u32[]{:S(2)}) collective-permute-start(bf16[128,512]{1,0:T(8,128)(2,1)S(1)} %far.2), channel_id=1, source_target_pairs={{0,4},{2,6},{4,0},{6,2},{8,12},{10,14},{12,8},{14,10},{16,20},{18,... | collective-permute-start | bytes 393224 | tf_op jit(solution)/shard_map/ppermute | solution.py:45
  21.0 7.1 %collective-permute-start.4 = (bf16[128,512]{1,0:T(8,128)(2,1)S(1)}, bf16[128,512]{1,0:T(8,128)(2,1)S(1)}, u32[]{:S(2)}, u32[]{:S(2)}) collective-permute-start(bf16[128,512]{1,0:T(8,128)(2,1)S(1)} %get-tuple-element.33.refs_1_), channel_id=1, source_target_pairs={{0,24},{2,26},{4,28},{6,30},{8,0},{10,2},{12,4},{14,6},{16,8},{18,... | collective-permute-start | bytes 393224 | tf_op jit(solution)/shard_map/ppermute | solution.py:40
  22.5 6.8 %collective-permute-start.3 = (bf16[128,512]{1,0:T(8,128)(2,1)S(1)}, bf16[128,512]{1,0:T(8,128)(2,1)S(1)}, u32[]{:S(2)}, u32[]{:S(2)}) collective-permute-start(bf16[128,512]{1,0:T(8,128)(2,1)S(1)} %get-tuple-element.33.refs_1_), channel_id=1, source_target_pairs={{0,8},{2,10},{4,12},{6,14},{8,16},{10,18},{12,20},{14,22},{16,24},... | collective-permute-start | bytes 393224 | tf_op jit(solution)/shard_map/ppermute | solution.py:40
  24.9 5.3 %collective-permute-start.11 = (bf16[128,512]{1,0:T(8,128)(2,1)S(1)}, bf16[128,512]{1,0:T(8,128)(2,1)S(1)}, u32[]{:S(2)}, u32[]{:S(2)}) collective-permute-start(bf16[128,512]{1,0:T(8,128)(2,1)S(1)} %get-tuple-element.39), channel_id=1, source_target_pairs={{0,2},{2,0},{4,6},{6,4},{8,10},{10,8},{12,14},{14,12},{16,18},{18,... | collective-permute-start | bytes 393224 | tf_op jit(solution)/shard_map/ppermute | solution.py:45
  25.0 5.2 %collective-permute-start.10 = (bf16[128,512]{1,0:T(8,128)(2,1)S(1)}, bf16[128,512]{1,0:T(8,128)(2,1)S(1)}, u32[]{:S(2)}, u32[]{:S(2)}) collective-permute-start(bf16[128,512]{1,0:T(8,128)(2,1)S(1)} %get-tuple-element.37.refs_0_), channel_id=1, source_target_pairs={{0,2},{2,0},{4,6},{6,4},{8,10},{10,8},{12,14},{14,12},{16,18},{18,... | collective-permute-start | bytes 393224 | tf_op jit(solution)/shard_map/ppermute | solution.py:45
  25.5 6.4 %collective-permute-start.2 = (bf16[64,1024]{1,0:T(8,128)(2,1)S(1)}, bf16[64,1024]{1,0:T(8,128)(2,1)S(1)}, u32[]{:S(2)}, u32[]{:S(2)}) collective-permute-start(bf16[64,1024]{1,0:T(8,128)(2,1)S(1)} %get-tuple-element.31), channel_id=1, source_target_pairs={{0,1},{1,0},{2,3},{3,2},{4,5},{5,4},{6,7},{7,6},{8,9},{9,8},{10,11... | collective-permute-start | bytes 393224 | tf_op jit(solution)/shard_map/ppermute | solution.py:40
  29.3 5.0 %collective-permute-start.9 = (bf16[128,512]{1,0:T(8,128)(2,1)S(1)}, bf16[128,512]{1,0:T(8,128)(2,1)S(1)}, u32[]{:S(2)}, u32[]{:S(2)}) collective-permute-start(bf16[128,512]{1,0:T(8,128)(2,1)S(1)} %far.3), channel_id=1, source_target_pairs={{0,4},{2,6},{4,0},{6,2},{8,12},{10,14},{12,8},{14,10},{16,20},{18,... | collective-permute-start | bytes 393224 | tf_op jit(solution)/shard_map/ppermute | solution.py:45
  30.3 7.8 %collective-permute-start.14 = (bf16[2,128,512]{2,1,0:T(8,128)(2,1)S(1)}, bf16[2,128,512]{2,1,0:T(8,128)(2,1)S(1)}, u32[]{:S(2)}, u32[]{:S(2)}) collective-permute-start(bf16[2,128,512]{2,1,0:T(8,128)(2,1)S(1)} %merge.2.refs_5_.refs_0_), channel_id=1, source_target_pairs={{0,1},{1,0},{2,3},{3,2},{4,5},{5,4},{6,7},{7,6},{8,9},{9,8},{10,11... | collective-permute-start | bytes 786440 | tf_op jit(solution)/shard_map/ppermute | solution.py:40
  34.7 1.4 %collective-permute-start.12 = (bf16[128,512]{1,0:T(8,128)(2,1)S(1)}, bf16[128,512]{1,0:T(8,128)(2,1)S(1)}, u32[]{:S(2)}, u32[]{:S(2)}) collective-permute-start(bf16[128,512]{1,0:T(8,128)(2,1)S(1)} %get-tuple-element.41), channel_id=1, source_target_pairs={{0,2},{2,0},{4,6},{6,4},{8,10},{10,8},{12,14},{14,12},{16,18},{18,... | collective-permute-start | bytes 393224 | tf_op jit(solution)/shard_map/ppermute | solution.py:45
  34.8 1.5 %collective-permute-start.13 = (bf16[128,512]{1,0:T(8,128)(2,1)S(1)}, bf16[128,512]{1,0:T(8,128)(2,1)S(1)}, u32[]{:S(2)}, u32[]{:S(2)}) collective-permute-start(bf16[128,512]{1,0:T(8,128)(2,1)S(1)} %get-tuple-element.42), channel_id=1, source_target_pairs={{0,2},{2,0},{4,6},{6,4},{8,10},{10,8},{12,14},{14,12},{16,18},{18,... | collective-permute-start | bytes 393224 | tf_op jit(solution)/shard_map/ppermute | solution.py:45
  38.2 6.9 %collective-permute-start.15 = (bf16[2,128,512]{2,1,0:T(8,128)(2,1)S(1)}, bf16[2,128,512]{2,1,0:T(8,128)(2,1)S(1)}, u32[]{:S(2)}, u32[]{:S(2)}) collective-permute-start(bf16[2,128,512]{2,1,0:T(8,128)(2,1)S(1)} %merge.3.refs_1_), channel_id=1, source_target_pairs={{0,1},{1,0},{2,3},{3,2},{4,5},{5,4},{6,7},{7,6},{8,9},{9,8},{10,11... | collective-permute-start | bytes 786440 | tf_op jit(solution)/shard_map/ppermute | solution.py:40

commit v5 on v4

--- a/solution.py
+++ b/solution.py
@@ -387,10 +387,10 @@
     lags = [lay_out_lags(part) for part in own]
 
     pieces = []
-    after_far, after_pick, after_merge = lags[:1], [], []
+    after_far, after_pick, after_merge = [], [], []
     for chunk in range(CHUNKS):
         piece, send = gather(chunk, directs[chunk], after_far, after_pick, after_merge)
-        after_far, after_pick, after_merge = [send[0]], [piece[0]] + lags[1:], piece[1:]
+        after_far, after_pick, after_merge = [], [piece[0]] + lags[1:], piece[1:]
         pieces.append(piece)
     others = [[pieces[chunk][step] for chunk in range(CHUNKS)] for step in range(win)]
     acc = accumulate(None, lags[0], list(zip(EDGES, others[0])))

time: 47.2 us -> 46.7 us (0.989)
  starting transfers between devices: 20.5 us -> 18.8 us
  waiting for transfers between devices: 15.1 us -> 16.3 us
    ppermute x7, waiting for transfers between devices: 11.2 us -> 12.7 us  [shift(): return lax.ppermute(x, axis, [(i, (i + by) % n) for i in range(n)])]
    ppermute x7, starting transfers between devices: 10.4 us -> 9.08 us  [shift(): return lax.ppermute(x, axis, [(i, (i + by) % n) for i in range(n)])]
where the time goes in v5:
time: 46.7 us; the launch traced here: 46.5 us
  starting transfers between devices  18.8 us (40%)
  waiting for transfers between devices  16.3 us (35%)
  Pallas kernels  10.6 us (23%)
  local copies, waits for them, and re-layouts  0.67 us (1%)
    ppermute x7, waiting for transfers between devices, shift(): return lax.ppermute(x, axis, [(i, (i + by) % n) for i in range(n)])  12.7 us
    ppermute x7, starting transfers between devices, shift(): return lax.ppermute(x, axis, [(i, (i + by) % n) for i in range(n)])  9.08 us
    ppermute x8, starting transfers between devices, swap(): return lax.ppermute(x, 'chan', [(i, i ^ bit) for i in range(n)])  4.88 us
    ppermute x1, starting transfers between devices, body(): before = lax.ppermute(tail, 'win', [(i, i + 1) for i in range(win - 1)])  4.87 us
    ppermute x8, waiting for transfers between devices, swap(): return lax.ppermute(x, 'chan', [(i, i ^ bit) for i in range(n)])  3.34 us
    pallas_call x2, Pallas kernels, lay_out_lags(): pl.pallas_call(lags_kernel, out_shape=jax.ShapeDtypeStruct((rows * LAGS,...  2.84 us
    pallas_call x2, Pallas kernels, accumulate(): pl.pallas_call(functools.partial(accumulate_kernel, firsts, acc is not No...  2.09 us
    pallas_call x1, Pallas kernels, finish(): pl.pallas_call(functools.partial(finish_kernel, reach, factor, first), ou...  1.91 us
  transfers between devices with their start and end apart: 16, of which 12 were waited for; matrix products, arithmetic and copies ran while one was open for 0% of the time, Pallas kernels for 15%

profile of v5, /device:TPU:0, one launch (start us, length us, event | category | flops | bytes accessed | tf_op | source)
XLA Modules:
  0.0 46.5 jit_solution(2032038621759676456)
XLA Ops:
  0.0 0.7 %copy-done.1 = f32[64]{0:T(128)S(1)} copy-done((f32[64]{0:T(128)S(1)}, f32[64]{0:T(128)}, u32[]{:S(2)}) %copy-start.1) | copy-done | bytes 280
  0.7 1.3 %head.1 = (bf16[128,128]{1,0:T(8,128)(2,1)S(1)}, bf16[128,4096]{1,0:T(8,128)(2,1)S(1)}, f32[1,64]{1,0:T(1,128)S(1)}) custom-call(bf16[128,4096]{1,0:T(8,128)(2,1)} %records_ref.1, f32[1,64]{1,0:T(1,128)S(1)} %bitcast.4), custom_call_target="tpu_custom_call" | custom-call | tf_op jit(solution)/shard_map/head/pallas_call | solution.py:62
  2.0 4.9 %collective-permute-start = (bf16[128,128]{1,0:T(8,128)(2,1)S(1)}, bf16[128,128]{1,0:T(8,128)(2,1)S(1)}, u32[]{:S(2)}, u32[]{:S(2)}) collective-permute-start(bf16[128,128]{1,0:T(8,128)(2,1)S(1)} %get-tuple-element.24), channel_id=1, source_target_pairs={{0,1},{2,3},{4,5},{6,7},{8,9},{10,11},{12,13},{14,15},{16,17},{18,... | collective-permute-start | bytes 98312 | tf_op jit(solution)/shard_map/ppermute | solution.py:361
  7.0 1.0 %bulk_filter.1 = (f32[128,1024]{1,0:T(8,128)S(1)}, f32[128,128]{1,0:T(8,128)S(1)}, bf16[384,128]{1,0:T(8,128)(2,1)S(1)}) custom-call(bf16[128,4096]{1,0:T(8,128)(2,1)S(1)} %get-tuple-element.26.records_ref, f32[1,64]{1,0:T(1,128)S(1)} %get-tuple-element.27.taps_ref), custom_call_target="tpu_custom_call" | custom-call | tf_op jit(solution)/shard_map/bulk_filter/pallas_call | solution.py:105
  8.5 0.4 whiten.1
  8.8 1.6 %collective-permute-start.7 = (bf16[128,512]{1,0:T(8,128)(2,1)S(1)}, bf16[128,512]{1,0:T(8,128)(2,1)S(1)}, u32[]{:S(2)}, u32[]{:S(2)}) collective-permute-start(bf16[128,512]{1,0:T(8,128)(2,1)S(1)} %get-tuple-element.35.refs_1_), channel_id=1, source_target_pairs={{0,8},{2,10},{4,12},{6,14},{8,16},{10,18},{12,20},{14,22},{16,24},... | collective-permute-start | bytes 393224 | tf_op jit(solution)/shard_map/ppermute | solution.py:40
  10.5 2.2 %collective-permute-start.8 = (bf16[128,512]{1,0:T(8,128)(2,1)S(1)}, bf16[128,512]{1,0:T(8,128)(2,1)S(1)}, u32[]{:S(2)}, u32[]{:S(2)}) collective-permute-start(bf16[128,512]{1,0:T(8,128)(2,1)S(1)} %get-tuple-element.35.refs_1_), channel_id=1, source_target_pairs={{0,24},{2,26},{4,28},{6,30},{8,0},{10,2},{12,4},{14,6},{16,8},{18,... | collective-permute-start | bytes 393224 | tf_op jit(solution)/shard_map/ppermute | solution.py:40
  12.7 1.5 %collective-permute-start.5 = (bf16[128,1024]{1,0:T(8,128)(2,1)S(1)}, bf16[128,1024]{1,0:T(8,128)(2,1)S(1)}, u32[]{:S(2)}, u32[]{:S(2)}) collective-permute-start(bf16[128,1024]{1,0:T(8,128)(2,1)S(1)} %get-tuple-element.34), channel_id=1, source_target_pairs={{0,4},{2,6},{4,0},{6,2},{8,12},{10,14},{12,8},{14,10},{16,20},{18,... | collective-permute-start | bytes 786440 | tf_op jit(solution)/shard_map/ppermute | solution.py:45
  14.2 2.8 %collective-permute-done.7.behind_ref.refs_0_ = bf16[128,512]{1,0:T(8,128)(2,1)S(1)} collective-permute-done((bf16[128,512]{1,0:T(8,128)(2,1)S(1)}, bf16[128,512]{1,0:T(8,128)(2,1)S(1)}, u32[]{:S(2)}, u32[]{:S(2)}) %collective-permute-start.7) | collective-permute-done | bytes 131104 | tf_op jit(solution)/shard_map/ppermute | solution.py:40
  17.0 1.4 %collective-permute-done.8.ahead_ref.refs_2_ = bf16[128,512]{1,0:T(8,128)(2,1)S(1)} collective-permute-done((bf16[128,512]{1,0:T(8,128)(2,1)S(1)}, bf16[128,512]{1,0:T(8,128)(2,1)S(1)}, u32[]{:S(2)}, u32[]{:S(2)}) %collective-permute-start.8) | collective-permute-done | bytes 131104 | tf_op jit(solution)/shard_map/ppermute | solution.py:40
  18.5 1.6 %collective-permute-start.9 = (bf16[128,512]{1,0:T(8,128)(2,1)S(1)}, bf16[128,512]{1,0:T(8,128)(2,1)S(1)}, u32[]{:S(2)}, u32[]{:S(2)}) collective-permute-start(bf16[128,512]{1,0:T(8,128)(2,1)S(1)} %far.3), channel_id=1, source_target_pairs={{0,4},{2,6},{4,0},{6,2},{8,12},{10,14},{12,8},{14,10},{16,20},{18,... | collective-permute-start | bytes 393224 | tf_op jit(solution)/shard_map/ppermute | solution.py:45
  20.0 1.1 %collective-permute-start.3 = (bf16[128,512]{1,0:T(8,128)(2,1)S(1)}, bf16[128,512]{1,0:T(8,128)(2,1)S(1)}, u32[]{:S(2)}, u32[]{:S(2)}) collective-permute-start(bf16[128,512]{1,0:T(8,128)(2,1)S(1)} %get-tuple-element.33.refs_1_), channel_id=1, source_target_pairs={{0,8},{2,10},{4,12},{6,14},{8,16},{10,18},{12,20},{14,22},{16,24},... | collective-permute-start | bytes 393224 | tf_op jit(solution)/shard_map/ppermute | solution.py:40
  21.1 2.7 %collective-permute-start.4 = (bf16[128,512]{1,0:T(8,128)(2,1)S(1)}, bf16[128,512]{1,0:T(8,128)(2,1)S(1)}, u32[]{:S(2)}, u32[]{:S(2)}) collective-permute-start(bf16[128,512]{1,0:T(8,128)(2,1)S(1)} %get-tuple-element.33.refs_1_), channel_id=1, source_target_pairs={{0,24},{2,26},{4,28},{6,30},{8,0},{10,2},{12,4},{14,6},{16,8},{18,... | collective-permute-start | bytes 393224 | tf_op jit(solution)/shard_map/ppermute | solution.py:40
  23.9 0.4 pick.2
  24.4 0.5 %collective-permute-start.11 = (bf16[128,512]{1,0:T(8,128)(2,1)S(1)}, bf16[128,512]{1,0:T(8,128)(2,1)S(1)}, u32[]{:S(2)}, u32[]{:S(2)}) collective-permute-start(bf16[128,512]{1,0:T(8,128)(2,1)S(1)} %get-tuple-element.38), channel_id=1, source_target_pairs={{0,2},{2,0},{4,6},{6,4},{8,10},{10,8},{12,14},{14,12},{16,18},{18,... | collective-permute-start | bytes 393224 | tf_op jit(solution)/shard_map/ppermute | solution.py:45
  24.9 1.0 %collective-permute-start.2 = (bf16[64,1024]{1,0:T(8,128)(2,1)S(1)}, bf16[64,1024]{1,0:T(8,128)(2,1)S(1)}, u32[]{:S(2)}, u32[]{:S(2)}) collective-permute-start(bf16[64,1024]{1,0:T(8,128)(2,1)S(1)} %get-tuple-element.31), channel_id=1, source_target_pairs={{0,1},{1,0},{2,3},{3,2},{4,5},{5,4},{6,7},{7,6},{8,9},{9,8},{10,11... | collective-permute-start | bytes 393224 | tf_op jit(solution)/shard_map/ppermute | solution.py:40
  25.8 2.0 %collective-permute-done.3.behind_ref.refs_0_ = bf16[128,512]{1,0:T(8,128)(2,1)S(1)} collective-permute-done((bf16[128,512]{1,0:T(8,128)(2,1)S(1)}, bf16[128,512]{1,0:T(8,128)(2,1)S(1)}, u32[]{:S(2)}, u32[]{:S(2)}) %collective-permute-start.3) | collective-permute-done | bytes 131104 | tf_op jit(solution)/shard_map/ppermute | solution.py:40
  27.9 0.9 %collective-permute-done.4.ahead_ref.refs_2_ = bf16[128,512]{1,0:T(8,128)(2,1)S(1)} collective-permute-done((bf16[128,512]{1,0:T(8,128)(2,1)S(1)}, bf16[128,512]{1,0:T(8,128)(2,1)S(1)}, u32[]{:S(2)}, u32[]{:S(2)}) %collective-permute-start.4) | collective-permute-done | bytes 131104 | tf_op jit(solution)/shard_map/ppermute | solution.py:40
  28.8 0.6 %collective-permute-start.6 = (bf16[128,512]{1,0:T(8,128)(2,1)S(1)}, bf16[128,512]{1,0:T(8,128)(2,1)S(1)}, u32[]{:S(2)}, u32[]{:S(2)}) collective-permute-start(bf16[128,512]{1,0:T(8,128)(2,1)S(1)} %far.2), channel_id=1, source_target_pairs={{0,4},{2,6},{4,0},{6,2},{8,12},{10,14},{12,8},{14,10},{16,20},{18,... | collective-permute-start | bytes 393224 | tf_op jit(solution)/shard_map/ppermute | solution.py:45
  29.6 0.7 %collective-permute-done.2.own_ref = bf16[64,1024]{1,0:T(8,128)(2,1)S(1)} collective-permute-done((bf16[64,1024]{1,0:T(8,128)(2,1)S(1)}, bf16[64,1024]{1,0:T(8,128)(2,1)S(1)}, u32[]{:S(2)}, u32[]{:S(2)}) %collective-permute-start.2) | collective-permute-done | bytes 131104 | tf_op jit(solution)/shard_map/ppermute | solution.py:40
  30.3 1.4 %lags.2.refs_6_.lags_ref = bf16[2112,1024]{1,0:T(8,128)(2,1)S(1)} custom-call(bf16[64,1024]{1,0:T(8,128)(2,1)S(1)} %collective-permute-done.2.own_ref), custom_call_target="tpu_custom_call" | custom-call | bytes 8388608 | tf_op jit(solution)/shard_map/lags/pallas_call | solution.py:178
  31.8 2.1 %collective-permute-done.6.refs_4_ = bf16[128,512]{1,0:T(8,128)(2,1)S(1)} collective-permute-done((bf16[128,512]{1,0:T(8,128)(2,1)S(1)}, bf16[128,512]{1,0:T(8,128)(2,1)S(1)}, u32[]{:S(2)}, u32[]{:S(2)}) %collective-permute-start.6) | collective-permute-done | bytes 131104 | tf_op jit(solution)/shard_map/ppermute | solution.py:45
  33.9 0.4 pick.3
  34.4 0.5 %collective-permute-start.13 = (bf16[128,512]{1,0:T(8,128)(2,1)S(1)}, bf16[128,512]{1,0:T(8,128)(2,1)S(1)}, u32[]{:S(2)}, u32[]{:S(2)}) collective-permute-start(bf16[128,512]{1,0:T(8,128)(2,1)S(1)} %get-tuple-element.41), channel_id=1, source_target_pairs={{0,2},{2,0},{4,6},{6,4},{8,10},{10,8},{12,14},{14,12},{16,18},{18,... | collective-permute-start | bytes 393224 | tf_op jit(solution)/shard_map/ppermute | solution.py:45
  34.9 0.8 %collective-permute-done.12.refs_0_ = bf16[128,512]{1,0:T(8,128)(2,1)S(1)} collective-permute-done((bf16[128,512]{1,0:T(8,128)(2,1)S(1)}, bf16[128,512]{1,0:T(8,128)(2,1)S(1)}, u32[]{:S(2)}, u32[]{:S(2)}) %collective-permute-start.12) | collective-permute-done | bytes 131104 | tf_op jit(solution)/shard_map/ppermute | solution.py:45
  35.9 1.2 %collective-permute-done.14.refs_2_.refs_0_ = bf16[2,128,512]{2,1,0:T(8,128)(2,1)S(1)} collective-permute-done((bf16[2,128,512]{2,1,0:T(8,128)(2,1)S(1)}, bf16[2,128,512]{2,1,0:T(8,128)(2,1)S(1)}, u32[]{:S(2)}, u32[]{:S(2)}) %collective-permute-start.14) | collective-permute-done | bytes 262176 | tf_op jit(solution)/shard_map/ppermute | solution.py:40
  37.2 0.4 collective-permute-start.15
  37.5 1.4 %lags.3.lags_ref = bf16[2112,1024]{1,0:T(8,128)(2,1)S(1)} custom-call(bf16[64,1024]{1,0:T(8,128)(2,1)S(1)} %get-tuple-element.42.own_ref), custom_call_target="tpu_custom_call" | custom-call | bytes 8388608 | tf_op jit(solution)/shard_map/lags/pallas_call | solution.py:178
  39.0 1.3 %accumulate.2.refs_1_ = f32[2112,256]{1,0:T(8,128)S(1)} custom-call(bf16[2112,1024]{1,0:T(8,128)(2,1)S(1)} %lags.3.lags_ref, bf16[2,128,512]{2,1,0:T(8,128)(2,1)S(1)} %merge.2.refs_5_.refs_0_, bf16[2,128,512]{2,1,0:T(8,128)(2,1)S(1)} %merge.3.refs_1_), custom_call_target="tpu_custom_call" | custom-call | tf_op jit(solution)/shard_map/accumulate/pallas_call | solution.py:300
  40.3 0.8 %accumulate.3.acc_ref = f32[2112,256]{1,0:T(8,128)S(1)} custom-call(bf16[2112,1024]{1,0:T(8,128)(2,1)S(1)} %lags.2.refs_6_.lags_ref, bf16[2,128,512]{2,1,0:T(8,128)(2,1)S(1)} %collective-permute-done.14.refs_2_.refs_0_, f32[2112,256]{1,0:T(8,128)S(1)} %accumulate.2.refs_1_), custom_call_target="tpu_custom_call" | custom-call | tf_op jit(solution)/shard_map/accumulate/pallas_call | solution.py:300
  41.1 3.5 %collective-permute-done.15.other_ref = bf16[2,128,512]{2,1,0:T(8,128)(2,1)S(1)} collective-permute-done((bf16[2,128,512]{2,1,0:T(8,128)(2,1)S(1)}, bf16[2,128,512]{2,1,0:T(8,128)(2,1)S(1)}, u32[]{:S(2)}, u32[]{:S(2)}) %collective-permute-start.15) | collective-permute-done | bytes 262176 | tf_op jit(solution)/shard_map/ppermute | solution.py:40
  44.6 1.9 %finish.1 = f32[4224,128]{1,0:T(8,128)} custom-call(s32[1,2]{1,0:T(1,128)S(1)} %copy-done, bf16[2112,1024]{1,0:T(8,128)(2,1)S(1)} %lags.2.refs_6_.lags_ref, bf16[2,128,512]{2,1,0:T(8,128)(2,1)S(1)} %collective-permute-done.15.other_ref, f32[2112,256]{1,0:T(8,128)S(1)} %accumulate.3.acc_ref), custom_call_target="tpu_custom_call" | custom-call | tf_op jit(solution)/shard_map/finish/pallas_call | solution.py:339
  (18 shorter events, 1.2 us)
Async XLA Ops:
  0.0 23.9 %copy-start = (s32[1,2]{1,0:T(1,128)S(1)}, s32[1,2]{1,0:T(1,128)}, u32[]{:S(2)}) copy-start(s32[1,2]{1,0:T(1,128)} %offsets.5) | copy-start | bytes 28
  0.0 0.7 %copy-start.1 = (f32[64]{0:T(128)S(1)}, f32[64]{0:T(128)}, u32[]{:S(2)}) copy-start(f32[64]{0:T(128)} %param.4) | copy-start | bytes 772
  2.0 6.5 %collective-permute-start = (bf16[128,128]{1,0:T(8,128)(2,1)S(1)}, bf16[128,128]{1,0:T(8,128)(2,1)S(1)}, u32[]{:S(2)}, u32[]{:S(2)}) collective-permute-start(bf16[128,128]{1,0:T(8,128)(2,1)S(1)} %get-tuple-element.24), channel_id=1, source_target_pairs={{0,1},{2,3},{4,5},{6,7},{8,9},{10,11},{12,13},{14,15},{16,17},{18,... | collective-permute-start | bytes 98312 | tf_op jit(solution)/shard_map/ppermute | solution.py:361
  6.9 1.3 %collective-permute-start.1 = (s32[1,2]{1,0:T(1,128)}, s32[1,2]{1,0:T(1,128)S(1)}, u32[]{:S(2)}, u32[]{:S(2)}) collective-permute-start(s32[1,2]{1,0:T(1,128)} %offsets.5), channel_id=1, source_target_pairs={{0,2},{2,0},{4,6},{6,4},{8,10},{10,8},{12,14},{14,12},{16,18},{18,... | collective-permute-start | bytes 32 | tf_op jit(solution)/shard_map/ppermute | solution.py:45
  8.8 8.2 %collective-permute-start.7 = (bf16[128,512]{1,0:T(8,128)(2,1)S(1)}, bf16[128,512]{1,0:T(8,128)(2,1)S(1)}, u32[]{:S(2)}, u32[]{:S(2)}) collective-permute-start(bf16[128,512]{1,0:T(8,128)(2,1)S(1)} %get-tuple-element.35.refs_1_), channel_id=1, source_target_pairs={{0,8},{2,10},{4,12},{6,14},{8,16},{10,18},{12,20},{14,22},{16,24},... | collective-permute-start | bytes 393224 | tf_op jit(solution)/shard_map/ppermute | solution.py:40
  10.5 8.0 %collective-permute-start.8 = (bf16[128,512]{1,0:T(8,128)(2,1)S(1)}, bf16[128,512]{1,0:T(8,128)(2,1)S(1)}, u32[]{:S(2)}, u32[]{:S(2)}) collective-permute-start(bf16[128,512]{1,0:T(8,128)(2,1)S(1)} %get-tuple-element.35.refs_1_), channel_id=1, source_target_pairs={{0,24},{2,26},{4,28},{6,30},{8,0},{10,2},{12,4},{14,6},{16,8},{18,... | collective-permute-start | bytes 393224 | tf_op jit(solution)/shard_map/ppermute | solution.py:40
  12.7 11.1 %collective-permute-start.5 = (bf16[128,1024]{1,0:T(8,128)(2,1)S(1)}, bf16[128,1024]{1,0:T(8,128)(2,1)S(1)}, u32[]{:S(2)}, u32[]{:S(2)}) collective-permute-start(bf16[128,1024]{1,0:T(8,128)(2,1)S(1)} %get-tuple-element.34), channel_id=1, source_target_pairs={{0,4},{2,6},{4,0},{6,2},{8,12},{10,14},{12,8},{14,10},{16,20},{18,... | collective-permute-start | bytes 786440 | tf_op jit(solution)/shard_map/ppermute | solution.py:45
  18.5 5.4 %collective-permute-start.9 = (bf16[128,512]{1,0:T(8,128)(2,1)S(1)}, bf16[128,512]{1,0:T(8,128)(2,1)S(1)}, u32[]{:S(2)}, u32[]{:S(2)}) collective-permute-start(bf16[128,512]{1,0:T(8,128)(2,1)S(1)} %far.3), channel_id=1, source_target_pairs={{0,4},{2,6},{4,0},{6,2},{8,12},{10,14},{12,8},{14,10},{16,20},{18,... | collective-permute-start | bytes 393224 | tf_op jit(solution)/shard_map/ppermute | solution.py:45
  20.0 7.8 %collective-permute-start.3 = (bf16[128,512]{1,0:T(8,128)(2,1)S(1)}, bf16[128,512]{1,0:T(8,128)(2,1)S(1)}, u32[]{:S(2)}, u32[]{:S(2)}) collective-permute-start(bf16[128,512]{1,0:T(8,128)(2,1)S(1)} %get-tuple-element.33.refs_1_), channel_id=1, source_target_pairs={{0,8},{2,10},{4,12},{6,14},{8,16},{10,18},{12,20},{14,22},{16,24},... | collective-permute-start | bytes 393224 | tf_op jit(solution)/shard_map/ppermute | solution.py:40
  21.1 7.7 %collective-permute-start.4 = (bf16[128,512]{1,0:T(8,128)(2,1)S(1)}, bf16[128,512]{1,0:T(8,128)(2,1)S(1)}, u32[]{:S(2)}, u32[]{:S(2)}) collective-permute-start(bf16[128,512]{1,0:T(8,128)(2,1)S(1)} %get-tuple-element.33.refs_1_), channel_id=1, source_target_pairs={{0,24},{2,26},{4,28},{6,30},{8,0},{10,2},{12,4},{14,6},{16,8},{18,... | collective-permute-start | bytes 393224 | tf_op jit(solution)/shard_map/ppermute | solution.py:40
  24.3 5.2 %collective-permute-start.10 = (bf16[128,512]{1,0:T(8,128)(2,1)S(1)}, bf16[128,512]{1,0:T(8,128)(2,1)S(1)}, u32[]{:S(2)}, u32[]{:S(2)}) collective-permute-start(bf16[128,512]{1,0:T(8,128)(2,1)S(1)} %get-tuple-element.37), channel_id=1, source_target_pairs={{0,2},{2,0},{4,6},{6,4},{8,10},{10,8},{12,14},{14,12},{16,18},{18,... | collective-permute-start | bytes 393224 | tf_op jit(solution)/shard_map/ppermute | solution.py:45
  24.4 5.1 %collective-permute-start.11 = (bf16[128,512]{1,0:T(8,128)(2,1)S(1)}, bf16[128,512]{1,0:T(8,128)(2,1)S(1)}, u32[]{:S(2)}, u32[]{:S(2)}) collective-permute-start(bf16[128,512]{1,0:T(8,128)(2,1)S(1)} %get-tuple-element.38), channel_id=1, source_target_pairs={{0,2},{2,0},{4,6},{6,4},{8,10},{10,8},{12,14},{14,12},{16,18},{18,... | collective-permute-start | bytes 393224 | tf_op jit(solution)/shard_map/ppermute | solution.py:45
  24.9 5.5 %collective-permute-start.2 = (bf16[64,1024]{1,0:T(8,128)(2,1)S(1)}, bf16[64,1024]{1,0:T(8,128)(2,1)S(1)}, u32[]{:S(2)}, u32[]{:S(2)}) collective-permute-start(bf16[64,1024]{1,0:T(8,128)(2,1)S(1)} %get-tuple-element.31), channel_id=1, source_target_pairs={{0,1},{1,0},{2,3},{3,2},{4,5},{5,4},{6,7},{7,6},{8,9},{9,8},{10,11... | collective-permute-start | bytes 393224 | tf_op jit(solution)/shard_map/ppermute | solution.py:40
  28.8 5.0 %collective-permute-start.6 = (bf16[128,512]{1,0:T(8,128)(2,1)S(1)}, bf16[128,512]{1,0:T(8,128)(2,1)S(1)}, u32[]{:S(2)}, u32[]{:S(2)}) collective-permute-start(bf16[128,512]{1,0:T(8,128)(2,1)S(1)} %far.2), channel_id=1, source_target_pairs={{0,4},{2,6},{4,0},{6,2},{8,12},{10,14},{12,8},{14,10},{16,20},{18,... | collective-permute-start | bytes 393224 | tf_op jit(solution)/shard_map/ppermute | solution.py:45
  29.5 7.5 %collective-permute-start.14 = (bf16[2,128,512]{2,1,0:T(8,128)(2,1)S(1)}, bf16[2,128,512]{2,1,0:T(8,128)(2,1)S(1)}, u32[]{:S(2)}, u32[]{:S(2)}) collective-permute-start(bf16[2,128,512]{2,1,0:T(8,128)(2,1)S(1)} %merge.2.refs_5_.refs_0_), channel_id=1, source_target_pairs={{0,1},{1,0},{2,3},{3,2},{4,5},{5,4},{6,7},{7,6},{8,9},{9,8},{10,11... | collective-permute-start | bytes 786440 | tf_op jit(solution)/shard_map/ppermute | solution.py:40
  34.3 1.4 %collective-permute-start.12 = (bf16[128,512]{1,0:T(8,128)(2,1)S(1)}, bf16[128,512]{1,0:T(8,128)(2,1)S(1)}, u32[]{:S(2)}, u32[]{:S(2)}) collective-permute-start(bf16[128,512]{1,0:T(8,128)(2,1)S(1)} %get-tuple-element.40), channel_id=1, source_target_pairs={{0,2},{2,0},{4,6},{6,4},{8,10},{10,8},{12,14},{14,12},{16,18},{18,... | collective-permute-start | bytes 393224 | tf_op jit(solution)/shard_map/ppermute | solution.py:45
  34.4 1.5 %collective-permute-start.13 = (bf16[128,512]{1,0:T(8,128)(2,1)S(1)}, bf16[128,512]{1,0:T(8,128)(2,1)S(1)}, u32[]{:S(2)}, u32[]{:S(2)}) collective-permute-start(bf16[128,512]{1,0:T(8,128)(2,1)S(1)} %get-tuple-element.41), channel_id=1, source_target_pairs={{0,2},{2,0},{4,6},{6,4},{8,10},{10,8},{12,14},{14,12},{16,18},{18,... | collective-permute-start | bytes 393224 | tf_op jit(solution)/shard_map/ppermute | solution.py:45
  37.2 7.4 %collective-permute-start.15 = (bf16[2,128,512]{2,1,0:T(8,128)(2,1)S(1)}, bf16[2,128,512]{2,1,0:T(8,128)(2,1)S(1)}, u32[]{:S(2)}, u32[]{:S(2)}) collective-permute-start(bf16[2,128,512]{2,1,0:T(8,128)(2,1)S(1)} %merge.3.refs_1_), channel_id=1, source_target_pairs={{0,1},{1,0},{2,3},{3,2},{4,5},{5,4},{6,7},{7,6},{8,9},{9,8},{10,11... | collective-permute-start | bytes 786440 | tf_op jit(solution)/shard_map/ppermute | solution.py:40

commit v6 on v5

--- a/solution.py
+++ b/solution.py
@@ -361,7 +361,6 @@
     before = lax.ppermute(tail, "win", [(i, i + 1) for i in range(win - 1)])
     core_offsets = swap(pair_offsets, 1)
     filtered, squares, band = bulk_filter(records, taps)
-    before, core_offsets = lax.optimization_barrier((before, core_offsets))
     outs = whiten(before, band, filtered, squares)
     chunks, row_parts, whole = outs[:CHUNKS], outs[CHUNKS:-1], outs[-1]
 
@@ -387,7 +386,7 @@
     lags = [lay_out_lags(part) for part in own]
 
     pieces = []
-    after_far, after_pick, after_merge = [], [], []
+    after_far, after_pick, after_merge = [core_offsets], [], []
     for chunk in range(CHUNKS):
         piece, send = gather(chunk, directs[chunk], after_far, after_pick, after_merge)
         after_far, after_pick, after_merge = [], [piece[0]] + lags[1:], piece[1:]

time: 46.7 us -> 44.8 us (0.959)
  waiting for transfers between devices: 16.3 us -> 10.4 us
  starting transfers between devices: 18.8 us -> 22.9 us
    ppermute x7, waiting for transfers between devices: 12.7 us -> 6.8 us  [shift(): return lax.ppermute(x, axis, [(i, (i + by) % n) for i in range(n)])]
    ppermute x7, starting transfers between devices: 9.08 us -> 13.2 us  [shift(): return lax.ppermute(x, axis, [(i, (i + by) % n) for i in range(n)])]
where the time goes in v6:
time: 44.8 us; the launch traced here: 44.7 us
  starting transfers between devices  22.9 us (51%)
  Pallas kernels  10.6 us (24%)
  waiting for transfers between devices  10.4 us (23%)
  local copies, waits for them, and re-layouts  0.67 us (1%)
    ppermute x7, starting transfers between devices, shift(): return lax.ppermute(x, axis, [(i, (i + by) % n) for i in range(n)])  13.2 us
    ppermute x7, waiting for transfers between devices, shift(): return lax.ppermute(x, axis, [(i, (i + by) % n) for i in range(n)])  6.8 us
    ppermute x1, starting transfers between devices, body(): before = lax.ppermute(tail, 'win', [(i, i + 1) for i in range(win - 1)])  4.87 us
    ppermute x8, starting transfers between devices, swap(): return lax.ppermute(x, 'chan', [(i, i ^ bit) for i in range(n)])  4.8 us
    ppermute x8, waiting for transfers between devices, swap(): return lax.ppermute(x, 'chan', [(i, i ^ bit) for i in range(n)])  3.04 us
    pallas_call x2, Pallas kernels, lay_out_lags(): pl.pallas_call(lags_kernel, out_shape=jax.ShapeDtypeStruct((rows * LAGS,...  2.84 us
    pallas_call x2, Pallas kernels, accumulate(): pl.pallas_call(functools.partial(accumulate_kernel, firsts, acc is not No...  2.09 us
    pallas_call x1, Pallas kernels, finish(): pl.pallas_call(functools.partial(finish_kernel, reach, factor, first), ou...  1.92 us
  transfers between devices with their start and end apart: 16, of which 12 were waited for; matrix products, arithmetic and copies ran while one was open for 0% of the time, Pallas kernels for 15%

profile of v6, /device:TPU:0, one launch (start us, length us, event | category | flops | bytes accessed | tf_op | source)
XLA Modules:
  0.0 44.7 jit_solution(9325090067431250589)
XLA Ops:
  0.0 0.7 %copy-done.1 = f32[64]{0:T(128)S(1)} copy-done((f32[64]{0:T(128)S(1)}, f32[64]{0:T(128)}, u32[]{:S(2)}) %copy-start.1) | copy-done | bytes 280
  0.7 1.3 %head.1 = (bf16[128,128]{1,0:T(8,128)(2,1)S(1)}, bf16[128,4096]{1,0:T(8,128)(2,1)S(1)}, f32[1,64]{1,0:T(1,128)S(1)}) custom-call(bf16[128,4096]{1,0:T(8,128)(2,1)} %records_ref.1, f32[1,64]{1,0:T(1,128)S(1)} %bitcast.4), custom_call_target="tpu_custom_call" | custom-call | tf_op jit(solution)/shard_map/head/pallas_call | solution.py:62
  2.0 4.9 %collective-permute-start = (bf16[128,128]{1,0:T(8,128)(2,1)S(1)}, bf16[128,128]{1,0:T(8,128)(2,1)S(1)}, u32[]{:S(2)}, u32[]{:S(2)}) collective-permute-start(bf16[128,128]{1,0:T(8,128)(2,1)S(1)} %get-tuple-element.22), channel_id=1, source_target_pairs={{0,1},{2,3},{4,5},{6,7},{8,9},{10,11},{12,13},{14,15},{16,17},{18,... | collective-permute-start | bytes 98312 | tf_op jit(solution)/shard_map/ppermute | solution.py:361
  6.9 1.0 %bulk_filter.1 = (f32[128,1024]{1,0:T(8,128)S(1)}, f32[128,128]{1,0:T(8,128)S(1)}, bf16[384,128]{1,0:T(8,128)(2,1)S(1)}) custom-call(bf16[128,4096]{1,0:T(8,128)(2,1)S(1)} %get-tuple-element.23.records_ref, f32[1,64]{1,0:T(1,128)S(1)} %get-tuple-element.24.taps_ref), custom_call_target="tpu_custom_call" | custom-call | tf_op jit(solution)/shard_map/bulk_filter/pallas_call | solution.py:105
  7.9 0.6 %collective-permute-done.tail_ref = bf16[128,128]{1,0:T(8,128)(2,1)S(1)} collective-permute-done((bf16[128,128]{1,0:T(8,128)(2,1)S(1)}, bf16[128,128]{1,0:T(8,128)(2,1)S(1)}, u32[]{:S(2)}, u32[]{:S(2)}) %collective-permute-start) | collective-permute-done | bytes 32800 | tf_op jit(solution)/shard_map/ppermute | solution.py:361
  8.8 1.6 %collective-permute-start.7 = (bf16[128,512]{1,0:T(8,128)(2,1)S(1)}, bf16[128,512]{1,0:T(8,128)(2,1)S(1)}, u32[]{:S(2)}, u32[]{:S(2)}) collective-permute-start(bf16[128,512]{1,0:T(8,128)(2,1)S(1)} %get-tuple-element.31.refs_1_), channel_id=1, source_target_pairs={{0,8},{2,10},{4,12},{6,14},{8,16},{10,18},{12,20},{14,22},{16,24},... | collective-permute-start | bytes 393224 | tf_op jit(solution)/shard_map/ppermute | solution.py:40
  10.5 2.2 %collective-permute-start.8 = (bf16[128,512]{1,0:T(8,128)(2,1)S(1)}, bf16[128,512]{1,0:T(8,128)(2,1)S(1)}, u32[]{:S(2)}, u32[]{:S(2)}) collective-permute-start(bf16[128,512]{1,0:T(8,128)(2,1)S(1)} %get-tuple-element.31.refs_1_), channel_id=1, source_target_pairs={{0,24},{2,26},{4,28},{6,30},{8,0},{10,2},{12,4},{14,6},{16,8},{18,... | collective-permute-start | bytes 393224 | tf_op jit(solution)/shard_map/ppermute | solution.py:40
  12.7 1.5 %collective-permute-start.5 = (bf16[128,1024]{1,0:T(8,128)(2,1)S(1)}, bf16[128,1024]{1,0:T(8,128)(2,1)S(1)}, u32[]{:S(2)}, u32[]{:S(2)}) collective-permute-start(bf16[128,1024]{1,0:T(8,128)(2,1)S(1)} %get-tuple-element.30), channel_id=1, source_target_pairs={{0,4},{2,6},{4,0},{6,2},{8,12},{10,14},{12,8},{14,10},{16,20},{18,... | collective-permute-start | bytes 786440 | tf_op jit(solution)/shard_map/ppermute | solution.py:45
  14.2 1.1 %collective-permute-done.2.refs_0_.core_offsets = s32[1,2]{1,0:T(1,128)S(1)} collective-permute-done((s32[1,2]{1,0:T(1,128)S(1)}, s32[1,2]{1,0:T(1,128)S(1)}, u32[]{:S(2)}, u32[]{:S(2)}) %collective-permute-start.2) | collective-permute-done | bytes 40 | tf_op jit(solution)/shard_map/ppermute | solution.py:45
  15.3 1.3 %collective-permute-done.7.behind_ref.refs_0_ = bf16[128,512]{1,0:T(8,128)(2,1)S(1)} collective-permute-done((bf16[128,512]{1,0:T(8,128)(2,1)S(1)}, bf16[128,512]{1,0:T(8,128)(2,1)S(1)}, u32[]{:S(2)}, u32[]{:S(2)}) %collective-permute-start.7) | collective-permute-done | bytes 131104 | tf_op jit(solution)/shard_map/ppermute | solution.py:40
  16.7 0.7 %collective-permute-done.8.ahead_ref.refs_2_ = bf16[128,512]{1,0:T(8,128)(2,1)S(1)} collective-permute-done((bf16[128,512]{1,0:T(8,128)(2,1)S(1)}, bf16[128,512]{1,0:T(8,128)(2,1)S(1)}, u32[]{:S(2)}, u32[]{:S(2)}) %collective-permute-start.8) | collective-permute-done | bytes 131104 | tf_op jit(solution)/shard_map/ppermute | solution.py:40
  17.4 1.6 %collective-permute-start.9 = (bf16[128,512]{1,0:T(8,128)(2,1)S(1)}, bf16[128,512]{1,0:T(8,128)(2,1)S(1)}, u32[]{:S(2)}, u32[]{:S(2)}) collective-permute-start(bf16[128,512]{1,0:T(8,128)(2,1)S(1)} %far.3), channel_id=1, source_target_pairs={{0,4},{2,6},{4,0},{6,2},{8,12},{10,14},{12,8},{14,10},{16,20},{18,... | collective-permute-start | bytes 393224 | tf_op jit(solution)/shard_map/ppermute | solution.py:45
  19.0 1.1 %collective-permute-start.3 = (bf16[128,512]{1,0:T(8,128)(2,1)S(1)}, bf16[128,512]{1,0:T(8,128)(2,1)S(1)}, u32[]{:S(2)}, u32[]{:S(2)}) collective-permute-start(bf16[128,512]{1,0:T(8,128)(2,1)S(1)} %get-tuple-element.29.refs_1_), channel_id=1, source_target_pairs={{0,8},{2,10},{4,12},{6,14},{8,16},{10,18},{12,20},{14,22},{16,24},... | collective-permute-start | bytes 393224 | tf_op jit(solution)/shard_map/ppermute | solution.py:40
  20.1 2.7 %collective-permute-start.4 = (bf16[128,512]{1,0:T(8,128)(2,1)S(1)}, bf16[128,512]{1,0:T(8,128)(2,1)S(1)}, u32[]{:S(2)}, u32[]{:S(2)}) collective-permute-start(bf16[128,512]{1,0:T(8,128)(2,1)S(1)} %get-tuple-element.29.refs_1_), channel_id=1, source_target_pairs={{0,24},{2,26},{4,28},{6,30},{8,0},{10,2},{12,4},{14,6},{16,8},{18,... | collective-permute-start | bytes 393224 | tf_op jit(solution)/shard_map/ppermute | solution.py:40
  22.8 0.4 pick.2
  23.3 0.5 %collective-permute-start.11 = (bf16[128,512]{1,0:T(8,128)(2,1)S(1)}, bf16[128,512]{1,0:T(8,128)(2,1)S(1)}, u32[]{:S(2)}, u32[]{:S(2)}) collective-permute-start(bf16[128,512]{1,0:T(8,128)(2,1)S(1)} %get-tuple-element.34), channel_id=1, source_target_pairs={{0,2},{2,0},{4,6},{6,4},{8,10},{10,8},{12,14},{14,12},{16,18},{18,... | collective-permute-start | bytes 393224 | tf_op jit(solution)/shard_map/ppermute | solution.py:45
  23.8 2.0 %collective-permute-start.1 = (bf16[64,1024]{1,0:T(8,128)(2,1)S(1)}, bf16[64,1024]{1,0:T(8,128)(2,1)S(1)}, u32[]{:S(2)}, u32[]{:S(2)}) collective-permute-start(bf16[64,1024]{1,0:T(8,128)(2,1)S(1)} %get-tuple-element.28), channel_id=1, source_target_pairs={{0,1},{1,0},{2,3},{3,2},{4,5},{5,4},{6,7},{7,6},{8,9},{9,8},{10,11... | collective-permute-start | bytes 393224 | tf_op jit(solution)/shard_map/ppermute | solution.py:40
  25.8 0.5 %collective-permute-done.3.behind_ref.refs_0_ = bf16[128,512]{1,0:T(8,128)(2,1)S(1)} collective-permute-done((bf16[128,512]{1,0:T(8,128)(2,1)S(1)}, bf16[128,512]{1,0:T(8,128)(2,1)S(1)}, u32[]{:S(2)}, u32[]{:S(2)}) %collective-permute-start.3) | collective-permute-done | bytes 131104 | tf_op jit(solution)/shard_map/ppermute | solution.py:40
  26.3 0.7 %collective-permute-done.4.ahead_ref.refs_2_ = bf16[128,512]{1,0:T(8,128)(2,1)S(1)} collective-permute-done((bf16[128,512]{1,0:T(8,128)(2,1)S(1)}, bf16[128,512]{1,0:T(8,128)(2,1)S(1)}, u32[]{:S(2)}, u32[]{:S(2)}) %collective-permute-start.4) | collective-permute-done | bytes 131104 | tf_op jit(solution)/shard_map/ppermute | solution.py:40
  27.0 0.6 %collective-permute-start.6 = (bf16[128,512]{1,0:T(8,128)(2,1)S(1)}, bf16[128,512]{1,0:T(8,128)(2,1)S(1)}, u32[]{:S(2)}, u32[]{:S(2)}) collective-permute-start(bf16[128,512]{1,0:T(8,128)(2,1)S(1)} %far.2), channel_id=1, source_target_pairs={{0,4},{2,6},{4,0},{6,2},{8,12},{10,14},{12,8},{14,10},{16,20},{18,... | collective-permute-start | bytes 393224 | tf_op jit(solution)/shard_map/ppermute | solution.py:45
  27.7 1.7 %collective-permute-start.14 = (bf16[2,128,512]{2,1,0:T(8,128)(2,1)S(1)}, bf16[2,128,512]{2,1,0:T(8,128)(2,1)S(1)}, u32[]{:S(2)}, u32[]{:S(2)}) collective-permute-start(bf16[2,128,512]{2,1,0:T(8,128)(2,1)S(1)} %merge.2.refs_5_.refs_0_), channel_id=1, source_target_pairs={{0,1},{1,0},{2,3},{3,2},{4,5},{5,4},{6,7},{7,6},{8,9},{9,8},{10,11... | collective-permute-start | bytes 786440 | tf_op jit(solution)/shard_map/ppermute | solution.py:40
  29.7 1.4 %lags.2.refs_6_.lags_ref = bf16[2112,1024]{1,0:T(8,128)(2,1)S(1)} custom-call(bf16[64,1024]{1,0:T(8,128)(2,1)S(1)} %collective-permute-done.1.own_ref), custom_call_target="tpu_custom_call" | custom-call | bytes 8388608 | tf_op jit(solution)/shard_map/lags/pallas_call | solution.py:178
  31.1 0.9 %collective-permute-done.6.refs_4_ = bf16[128,512]{1,0:T(8,128)(2,1)S(1)} collective-permute-done((bf16[128,512]{1,0:T(8,128)(2,1)S(1)}, bf16[128,512]{1,0:T(8,128)(2,1)S(1)}, u32[]{:S(2)}, u32[]{:S(2)}) %collective-permute-start.6) | collective-permute-done | bytes 131104 | tf_op jit(solution)/shard_map/ppermute | solution.py:45
  32.5 0.5 %collective-permute-start.13 = (bf16[128,512]{1,0:T(8,128)(2,1)S(1)}, bf16[128,512]{1,0:T(8,128)(2,1)S(1)}, u32[]{:S(2)}, u32[]{:S(2)}) collective-permute-start(bf16[128,512]{1,0:T(8,128)(2,1)S(1)} %get-tuple-element.37), channel_id=1, source_target_pairs={{0,2},{2,0},{4,6},{6,4},{8,10},{10,8},{12,14},{14,12},{16,18},{18,... | collective-permute-start | bytes 393224 | tf_op jit(solution)/shard_map/ppermute | solution.py:45
  33.0 0.8 %collective-permute-done.12.refs_0_ = bf16[128,512]{1,0:T(8,128)(2,1)S(1)} collective-permute-done((bf16[128,512]{1,0:T(8,128)(2,1)S(1)}, bf16[128,512]{1,0:T(8,128)(2,1)S(1)}, u32[]{:S(2)}, u32[]{:S(2)}) %collective-permute-start.12) | collective-permute-done | bytes 131104 | tf_op jit(solution)/shard_map/ppermute | solution.py:45
  34.0 1.1 %collective-permute-done.14.refs_2_.refs_0_ = bf16[2,128,512]{2,1,0:T(8,128)(2,1)S(1)} collective-permute-done((bf16[2,128,512]{2,1,0:T(8,128)(2,1)S(1)}, bf16[2,128,512]{2,1,0:T(8,128)(2,1)S(1)}, u32[]{:S(2)}, u32[]{:S(2)}) %collective-permute-start.14) | collective-permute-done | bytes 262176 | tf_op jit(solution)/shard_map/ppermute | solution.py:40
  35.3 1.8 %collective-permute-start.15 = (bf16[2,128,512]{2,1,0:T(8,128)(2,1)S(1)}, bf16[2,128,512]{2,1,0:T(8,128)(2,1)S(1)}, u32[]{:S(2)}, u32[]{:S(2)}) collective-permute-start(bf16[2,128,512]{2,1,0:T(8,128)(2,1)S(1)} %merge.3.refs_1_), channel_id=1, source_target_pairs={{0,1},{1,0},{2,3},{3,2},{4,5},{5,4},{6,7},{7,6},{8,9},{9,8},{10,11... | collective-permute-start | bytes 786440 | tf_op jit(solution)/shard_map/ppermute | solution.py:40
  37.1 1.4 %lags.3.lags_ref = bf16[2112,1024]{1,0:T(8,128)(2,1)S(1)} custom-call(bf16[64,1024]{1,0:T(8,128)(2,1)S(1)} %get-tuple-element.38.own_ref), custom_call_target="tpu_custom_call" | custom-call | bytes 8388608 | tf_op jit(solution)/shard_map/lags/pallas_call | solution.py:178
  38.5 1.3 %accumulate.2.refs_1_ = f32[2112,256]{1,0:T(8,128)S(1)} custom-call(bf16[2112,1024]{1,0:T(8,128)(2,1)S(1)} %lags.3.lags_ref, bf16[2,128,512]{2,1,0:T(8,128)(2,1)S(1)} %merge.2.refs_5_.refs_0_, bf16[2,128,512]{2,1,0:T(8,128)(2,1)S(1)} %merge.3.refs_1_), custom_call_target="tpu_custom_call" | custom-call | tf_op jit(solution)/shard_map/accumulate/pallas_call | solution.py:300
  39.8 0.8 %accumulate.3.acc_ref = f32[2112,256]{1,0:T(8,128)S(1)} custom-call(bf16[2112,1024]{1,0:T(8,128)(2,1)S(1)} %lags.2.refs_6_.lags_ref, bf16[2,128,512]{2,1,0:T(8,128)(2,1)S(1)} %collective-permute-done.14.refs_2_.refs_0_, f32[2112,256]{1,0:T(8,128)S(1)} %accumulate.2.refs_1_), custom_call_target="tpu_custom_call" | custom-call | tf_op jit(solution)/shard_map/accumulate/pallas_call | solution.py:300
  40.6 2.1 %collective-permute-done.15.other_ref = bf16[2,128,512]{2,1,0:T(8,128)(2,1)S(1)} collective-permute-done((bf16[2,128,512]{2,1,0:T(8,128)(2,1)S(1)}, bf16[2,128,512]{2,1,0:T(8,128)(2,1)S(1)}, u32[]{:S(2)}, u32[]{:S(2)}) %collective-permute-start.15) | collective-permute-done | bytes 262176 | tf_op jit(solution)/shard_map/ppermute | solution.py:40
  42.7 1.9 %finish.1 = f32[4224,128]{1,0:T(8,128)} custom-call(s32[1,2]{1,0:T(1,128)S(1)} %copy-done, bf16[2112,1024]{1,0:T(8,128)(2,1)S(1)} %lags.2.refs_6_.lags_ref, bf16[2,128,512]{2,1,0:T(8,128)(2,1)S(1)} %collective-permute-done.15.other_ref, f32[2112,256]{1,0:T(8,128)S(1)} %accumulate.3.acc_ref), custom_call_target="tpu_custom_call" | custom-call | tf_op jit(solution)/shard_map/finish/pallas_call | solution.py:339
  (18 shorter events, 1.6 us)
Async XLA Ops:
  0.0 14.2 %copy-start = (s32[1,2]{1,0:T(1,128)S(1)}, s32[1,2]{1,0:T(1,128)}, u32[]{:S(2)}) copy-start(s32[1,2]{1,0:T(1,128)} %offsets.5) | copy-start | bytes 28
  0.0 0.7 %copy-start.1 = (f32[64]{0:T(128)S(1)}, f32[64]{0:T(128)}, u32[]{:S(2)}) copy-start(f32[64]{0:T(128)} %param.4) | copy-start | bytes 772
  2.0 6.5 %collective-permute-start = (bf16[128,128]{1,0:T(8,128)(2,1)S(1)}, bf16[128,128]{1,0:T(8,128)(2,1)S(1)}, u32[]{:S(2)}, u32[]{:S(2)}) collective-permute-start(bf16[128,128]{1,0:T(8,128)(2,1)S(1)} %get-tuple-element.22), channel_id=1, source_target_pairs={{0,1},{2,3},{4,5},{6,7},{8,9},{10,11},{12,13},{14,15},{16,17},{18,... | collective-permute-start | bytes 98312 | tf_op jit(solution)/shard_map/ppermute | solution.py:361
  8.8 7.8 %collective-permute-start.7 = (bf16[128,512]{1,0:T(8,128)(2,1)S(1)}, bf16[128,512]{1,0:T(8,128)(2,1)S(1)}, u32[]{:S(2)}, u32[]{:S(2)}) collective-permute-start(bf16[128,512]{1,0:T(8,128)(2,1)S(1)} %get-tuple-element.31.refs_1_), channel_id=1, source_target_pairs={{0,8},{2,10},{4,12},{6,14},{8,16},{10,18},{12,20},{14,22},{16,24},... | collective-permute-start | bytes 393224 | tf_op jit(solution)/shard_map/ppermute | solution.py:40
  10.5 6.9 %collective-permute-start.8 = (bf16[128,512]{1,0:T(8,128)(2,1)S(1)}, bf16[128,512]{1,0:T(8,128)(2,1)S(1)}, u32[]{:S(2)}, u32[]{:S(2)}) collective-permute-start(bf16[128,512]{1,0:T(8,128)(2,1)S(1)} %get-tuple-element.31.refs_1_), channel_id=1, source_target_pairs={{0,24},{2,26},{4,28},{6,30},{8,0},{10,2},{12,4},{14,6},{16,8},{18,... | collective-permute-start | bytes 393224 | tf_op jit(solution)/shard_map/ppermute | solution.py:40
  12.7 10.1 %collective-permute-start.5 = (bf16[128,1024]{1,0:T(8,128)(2,1)S(1)}, bf16[128,1024]{1,0:T(8,128)(2,1)S(1)}, u32[]{:S(2)}, u32[]{:S(2)}) collective-permute-start(bf16[128,1024]{1,0:T(8,128)(2,1)S(1)} %get-tuple-element.30), channel_id=1, source_target_pairs={{0,4},{2,6},{4,0},{6,2},{8,12},{10,14},{12,8},{14,10},{16,20},{18,... | collective-permute-start | bytes 786440 | tf_op jit(solution)/shard_map/ppermute | solution.py:45
  14.2 1.1 %collective-permute-start.2 = (s32[1,2]{1,0:T(1,128)S(1)}, s32[1,2]{1,0:T(1,128)S(1)}, u32[]{:S(2)}, u32[]{:S(2)}) collective-permute-start(s32[1,2]{1,0:T(1,128)S(1)} %copy-done), channel_id=1, source_target_pairs={{0,2},{2,0},{4,6},{6,4},{8,10},{10,8},{12,14},{14,12},{16,18},{18,... | collective-permute-start | bytes 32 | tf_op jit(solution)/shard_map/ppermute | solution.py:45
  17.4 5.4 %collective-permute-start.9 = (bf16[128,512]{1,0:T(8,128)(2,1)S(1)}, bf16[128,512]{1,0:T(8,128)(2,1)S(1)}, u32[]{:S(2)}, u32[]{:S(2)}) collective-permute-start(bf16[128,512]{1,0:T(8,128)(2,1)S(1)} %far.3), channel_id=1, source_target_pairs={{0,4},{2,6},{4,0},{6,2},{8,12},{10,14},{12,8},{14,10},{16,20},{18,... | collective-permute-start | bytes 393224 | tf_op jit(solution)/shard_map/ppermute | solution.py:45
  19.0 7.3 %collective-permute-start.3 = (bf16[128,512]{1,0:T(8,128)(2,1)S(1)}, bf16[128,512]{1,0:T(8,128)(2,1)S(1)}, u32[]{:S(2)}, u32[]{:S(2)}) collective-permute-start(bf16[128,512]{1,0:T(8,128)(2,1)S(1)} %get-tuple-element.29.refs_1_), channel_id=1, source_target_pairs={{0,8},{2,10},{4,12},{6,14},{8,16},{10,18},{12,20},{14,22},{16,24},... | collective-permute-start | bytes 393224 | tf_op jit(solution)/shard_map/ppermute | solution.py:40
  20.1 6.8 %collective-permute-start.4 = (bf16[128,512]{1,0:T(8,128)(2,1)S(1)}, bf16[128,512]{1,0:T(8,128)(2,1)S(1)}, u32[]{:S(2)}, u32[]{:S(2)}) collective-permute-start(bf16[128,512]{1,0:T(8,128)(2,1)S(1)} %get-tuple-element.29.refs_1_), channel_id=1, source_target_pairs={{0,24},{2,26},{4,28},{6,30},{8,0},{10,2},{12,4},{14,6},{16,8},{18,... | collective-permute-start | bytes 393224 | tf_op jit(solution)/shard_map/ppermute | solution.py:40
  23.2 4.3 %collective-permute-start.10 = (bf16[128,512]{1,0:T(8,128)(2,1)S(1)}, bf16[128,512]{1,0:T(8,128)(2,1)S(1)}, u32[]{:S(2)}, u32[]{:S(2)}) collective-permute-start(bf16[128,512]{1,0:T(8,128)(2,1)S(1)} %get-tuple-element.33), channel_id=1, source_target_pairs={{0,2},{2,0},{4,6},{6,4},{8,10},{10,8},{12,14},{14,12},{16,18},{18,... | collective-permute-start | bytes 393224 | tf_op jit(solution)/shard_map/ppermute | solution.py:45
  23.3 4.3 %collective-permute-start.11 = (bf16[128,512]{1,0:T(8,128)(2,1)S(1)}, bf16[128,512]{1,0:T(8,128)(2,1)S(1)}, u32[]{:S(2)}, u32[]{:S(2)}) collective-permute-start(bf16[128,512]{1,0:T(8,128)(2,1)S(1)} %get-tuple-element.34), channel_id=1, source_target_pairs={{0,2},{2,0},{4,6},{6,4},{8,10},{10,8},{12,14},{14,12},{16,18},{18,... | collective-permute-start | bytes 393224 | tf_op jit(solution)/shard_map/ppermute | solution.py:45
  23.8 5.9 %collective-permute-start.1 = (bf16[64,1024]{1,0:T(8,128)(2,1)S(1)}, bf16[64,1024]{1,0:T(8,128)(2,1)S(1)}, u32[]{:S(2)}, u32[]{:S(2)}) collective-permute-start(bf16[64,1024]{1,0:T(8,128)(2,1)S(1)} %get-tuple-element.28), channel_id=1, source_target_pairs={{0,1},{1,0},{2,3},{3,2},{4,5},{5,4},{6,7},{7,6},{8,9},{9,8},{10,11... | collective-permute-start | bytes 393224 | tf_op jit(solution)/shard_map/ppermute | solution.py:40
  27.0 5.0 %collective-permute-start.6 = (bf16[128,512]{1,0:T(8,128)(2,1)S(1)}, bf16[128,512]{1,0:T(8,128)(2,1)S(1)}, u32[]{:S(2)}, u32[]{:S(2)}) collective-permute-start(bf16[128,512]{1,0:T(8,128)(2,1)S(1)} %far.2), channel_id=1, source_target_pairs={{0,4},{2,6},{4,0},{6,2},{8,12},{10,14},{12,8},{14,10},{16,20},{18,... | collective-permute-start | bytes 393224 | tf_op jit(solution)/shard_map/ppermute | solution.py:45
  27.7 7.5 %collective-permute-start.14 = (bf16[2,128,512]{2,1,0:T(8,128)(2,1)S(1)}, bf16[2,128,512]{2,1,0:T(8,128)(2,1)S(1)}, u32[]{:S(2)}, u32[]{:S(2)}) collective-permute-start(bf16[2,128,512]{2,1,0:T(8,128)(2,1)S(1)} %merge.2.refs_5_.refs_0_), channel_id=1, source_target_pairs={{0,1},{1,0},{2,3},{3,2},{4,5},{5,4},{6,7},{7,6},{8,9},{9,8},{10,11... | collective-permute-start | bytes 786440 | tf_op jit(solution)/shard_map/ppermute | solution.py:40
  32.4 1.4 %collective-permute-start.12 = (bf16[128,512]{1,0:T(8,128)(2,1)S(1)}, bf16[128,512]{1,0:T(8,128)(2,1)S(1)}, u32[]{:S(2)}, u32[]{:S(2)}) collective-permute-start(bf16[128,512]{1,0:T(8,128)(2,1)S(1)} %get-tuple-element.36), channel_id=1, source_target_pairs={{0,2},{2,0},{4,6},{6,4},{8,10},{10,8},{12,14},{14,12},{16,18},{18,... | collective-permute-start | bytes 393224 | tf_op jit(solution)/shard_map/ppermute | solution.py:45
  32.5 1.5 %collective-permute-start.13 = (bf16[128,512]{1,0:T(8,128)(2,1)S(1)}, bf16[128,512]{1,0:T(8,128)(2,1)S(1)}, u32[]{:S(2)}, u32[]{:S(2)}) collective-permute-start(bf16[128,512]{1,0:T(8,128)(2,1)S(1)} %get-tuple-element.37), channel_id=1, source_target_pairs={{0,2},{2,0},{4,6},{6,4},{8,10},{10,8},{12,14},{14,12},{16,18},{18,... | collective-permute-start | bytes 393224 | tf_op jit(solution)/shard_map/ppermute | solution.py:45
  35.3 7.5 %collective-permute-start.15 = (bf16[2,128,512]{2,1,0:T(8,128)(2,1)S(1)}, bf16[2,128,512]{2,1,0:T(8,128)(2,1)S(1)}, u32[]{:S(2)}, u32[]{:S(2)}) collective-permute-start(bf16[2,128,512]{2,1,0:T(8,128)(2,1)S(1)} %merge.3.refs_1_), channel_id=1, source_target_pairs={{0,1},{1,0},{2,3},{3,2},{4,5},{5,4},{6,7},{7,6},{8,9},{9,8},{10,11... | collective-permute-start | bytes 786440 | tf_op jit(solution)/shard_map/ppermute | solution.py:40

commit v7 on v6

--- a/solution.py
+++ b/solution.py
@@ -342,7 +342,7 @@
         in_specs=[VMEM_SPEC] * 4,
         out_specs=HBM_SPEC,
         scratch_shapes=[
-            VMEM((total * slots, LANES), F32),
+            VMEM((total * slots + 8 * LAGS * slots, LANES), F32),
             pltpu.SemaphoreType.DMA((total // (GROUP * LAGS),)),
         ],
         compiler_params=grant(12),

time: 44.8 us -> 44.8 us (level)
  no operation moved by 1% of the time
where the time goes in v7:
time: 44.8 us; the launch traced here: 44.7 us
  starting transfers between devices  22.9 us (51%)
  Pallas kernels  10.6 us (24%)
  waiting for transfers between devices  10.4 us (23%)
  local copies, waits for them, and re-layouts  0.67 us (1%)
    ppermute x7, starting transfers between devices, shift(): return lax.ppermute(x, axis, [(i, (i + by) % n) for i in range(n)])  13.2 us
    ppermute x7, waiting for transfers between devices, shift(): return lax.ppermute(x, axis, [(i, (i + by) % n) for i in range(n)])  6.8 us
    ppermute x1, starting transfers between devices, body(): before = lax.ppermute(tail, 'win', [(i, i + 1) for i in range(win - 1)])  4.87 us
    ppermute x8, starting transfers between devices, swap(): return lax.ppermute(x, 'chan', [(i, i ^ bit) for i in range(n)])  4.8 us
    ppermute x8, waiting for transfers between devices, swap(): return lax.ppermute(x, 'chan', [(i, i ^ bit) for i in range(n)])  3.04 us
    pallas_call x2, Pallas kernels, lay_out_lags(): pl.pallas_call(lags_kernel, out_shape=jax.ShapeDtypeStruct((rows * LAGS,...  2.84 us
    pallas_call x2, Pallas kernels, accumulate(): pl.pallas_call(functools.partial(accumulate_kernel, firsts, acc is not No...  2.09 us
    pallas_call x1, Pallas kernels, finish(): pl.pallas_call(functools.partial(finish_kernel, reach, factor, first), ou...  1.91 us
  transfers between devices with their start and end apart: 16, of which 12 were waited for; matrix products, arithmetic and copies ran while one was open for 0% of the time, Pallas kernels for 15%

profile of v7, /device:TPU:0, one launch (start us, length us, event | category | flops | bytes accessed | tf_op | source)
XLA Modules:
  0.0 44.7 jit_solution(17278179137717078241)
XLA Ops:
  0.0 0.7 %copy-done.1 = f32[64]{0:T(128)S(1)} copy-done((f32[64]{0:T(128)S(1)}, f32[64]{0:T(128)}, u32[]{:S(2)}) %copy-start.1) | copy-done | bytes 280
  0.7 1.3 %head.1 = (bf16[128,128]{1,0:T(8,128)(2,1)S(1)}, bf16[128,4096]{1,0:T(8,128)(2,1)S(1)}, f32[1,64]{1,0:T(1,128)S(1)}) custom-call(bf16[128,4096]{1,0:T(8,128)(2,1)} %records_ref.1, f32[1,64]{1,0:T(1,128)S(1)} %bitcast.4), custom_call_target="tpu_custom_call" | custom-call | tf_op jit(solution)/shard_map/head/pallas_call | solution.py:62
  2.0 4.9 %collective-permute-start = (bf16[128,128]{1,0:T(8,128)(2,1)S(1)}, bf16[128,128]{1,0:T(8,128)(2,1)S(1)}, u32[]{:S(2)}, u32[]{:S(2)}) collective-permute-start(bf16[128,128]{1,0:T(8,128)(2,1)S(1)} %get-tuple-element.22), channel_id=1, source_target_pairs={{0,1},{2,3},{4,5},{6,7},{8,9},{10,11},{12,13},{14,15},{16,17},{18,... | collective-permute-start | bytes 98312 | tf_op jit(solution)/shard_map/ppermute | solution.py:361
  6.9 1.0 %bulk_filter.1 = (f32[128,1024]{1,0:T(8,128)S(1)}, f32[128,128]{1,0:T(8,128)S(1)}, bf16[384,128]{1,0:T(8,128)(2,1)S(1)}) custom-call(bf16[128,4096]{1,0:T(8,128)(2,1)S(1)} %get-tuple-element.23.records_ref, f32[1,64]{1,0:T(1,128)S(1)} %get-tuple-element.24.taps_ref), custom_call_target="tpu_custom_call" | custom-call | tf_op jit(solution)/shard_map/bulk_filter/pallas_call | solution.py:105
  7.9 0.6 %collective-permute-done.tail_ref = bf16[128,128]{1,0:T(8,128)(2,1)S(1)} collective-permute-done((bf16[128,128]{1,0:T(8,128)(2,1)S(1)}, bf16[128,128]{1,0:T(8,128)(2,1)S(1)}, u32[]{:S(2)}, u32[]{:S(2)}) %collective-permute-start) | collective-permute-done | bytes 32800 | tf_op jit(solution)/shard_map/ppermute | solution.py:361
  8.8 1.6 %collective-permute-start.7 = (bf16[128,512]{1,0:T(8,128)(2,1)S(1)}, bf16[128,512]{1,0:T(8,128)(2,1)S(1)}, u32[]{:S(2)}, u32[]{:S(2)}) collective-permute-start(bf16[128,512]{1,0:T(8,128)(2,1)S(1)} %get-tuple-element.31.refs_1_), channel_id=1, source_target_pairs={{0,8},{2,10},{4,12},{6,14},{8,16},{10,18},{12,20},{14,22},{16,24},... | collective-permute-start | bytes 393224 | tf_op jit(solution)/shard_map/ppermute | solution.py:40
  10.5 2.2 %collective-permute-start.8 = (bf16[128,512]{1,0:T(8,128)(2,1)S(1)}, bf16[128,512]{1,0:T(8,128)(2,1)S(1)}, u32[]{:S(2)}, u32[]{:S(2)}) collective-permute-start(bf16[128,512]{1,0:T(8,128)(2,1)S(1)} %get-tuple-element.31.refs_1_), channel_id=1, source_target_pairs={{0,24},{2,26},{4,28},{6,30},{8,0},{10,2},{12,4},{14,6},{16,8},{18,... | collective-permute-start | bytes 393224 | tf_op jit(solution)/shard_map/ppermute | solution.py:40
  12.7 1.5 %collective-permute-start.5 = (bf16[128,1024]{1,0:T(8,128)(2,1)S(1)}, bf16[128,1024]{1,0:T(8,128)(2,1)S(1)}, u32[]{:S(2)}, u32[]{:S(2)}) collective-permute-start(bf16[128,1024]{1,0:T(8,128)(2,1)S(1)} %get-tuple-element.30), channel_id=1, source_target_pairs={{0,4},{2,6},{4,0},{6,2},{8,12},{10,14},{12,8},{14,10},{16,20},{18,... | collective-permute-start | bytes 786440 | tf_op jit(solution)/shard_map/ppermute | solution.py:45
  14.2 1.1 %collective-permute-done.2.refs_0_.core_offsets = s32[1,2]{1,0:T(1,128)S(1)} collective-permute-done((s32[1,2]{1,0:T(1,128)S(1)}, s32[1,2]{1,0:T(1,128)S(1)}, u32[]{:S(2)}, u32[]{:S(2)}) %collective-permute-start.2) | collective-permute-done | bytes 40 | tf_op jit(solution)/shard_map/ppermute | solution.py:45
  15.3 1.3 %collective-permute-done.7.behind_ref.refs_0_ = bf16[128,512]{1,0:T(8,128)(2,1)S(1)} collective-permute-done((bf16[128,512]{1,0:T(8,128)(2,1)S(1)}, bf16[128,512]{1,0:T(8,128)(2,1)S(1)}, u32[]{:S(2)}, u32[]{:S(2)}) %collective-permute-start.7) | collective-permute-done | bytes 131104 | tf_op jit(solution)/shard_map/ppermute | solution.py:40
  16.7 0.7 %collective-permute-done.8.ahead_ref.refs_2_ = bf16[128,512]{1,0:T(8,128)(2,1)S(1)} collective-permute-done((bf16[128,512]{1,0:T(8,128)(2,1)S(1)}, bf16[128,512]{1,0:T(8,128)(2,1)S(1)}, u32[]{:S(2)}, u32[]{:S(2)}) %collective-permute-start.8) | collective-permute-done | bytes 131104 | tf_op jit(solution)/shard_map/ppermute | solution.py:40
  17.4 1.6 %collective-permute-start.9 = (bf16[128,512]{1,0:T(8,128)(2,1)S(1)}, bf16[128,512]{1,0:T(8,128)(2,1)S(1)}, u32[]{:S(2)}, u32[]{:S(2)}) collective-permute-start(bf16[128,512]{1,0:T(8,128)(2,1)S(1)} %far.3), channel_id=1, source_target_pairs={{0,4},{2,6},{4,0},{6,2},{8,12},{10,14},{12,8},{14,10},{16,20},{18,... | collective-permute-start | bytes 393224 | tf_op jit(solution)/shard_map/ppermute | solution.py:45
  19.0 1.1 %collective-permute-start.3 = (bf16[128,512]{1,0:T(8,128)(2,1)S(1)}, bf16[128,512]{1,0:T(8,128)(2,1)S(1)}, u32[]{:S(2)}, u32[]{:S(2)}) collective-permute-start(bf16[128,512]{1,0:T(8,128)(2,1)S(1)} %get-tuple-element.29.refs_1_), channel_id=1, source_target_pairs={{0,8},{2,10},{4,12},{6,14},{8,16},{10,18},{12,20},{14,22},{16,24},... | collective-permute-start | bytes 393224 | tf_op jit(solution)/shard_map/ppermute | solution.py:40
  20.1 2.7 %collective-permute-start.4 = (bf16[128,512]{1,0:T(8,128)(2,1)S(1)}, bf16[128,512]{1,0:T(8,128)(2,1)S(1)}, u32[]{:S(2)}, u32[]{:S(2)}) collective-permute-start(bf16[128,512]{1,0:T(8,128)(2,1)S(1)} %get-tuple-element.29.refs_1_), channel_id=1, source_target_pairs={{0,24},{2,26},{4,28},{6,30},{8,0},{10,2},{12,4},{14,6},{16,8},{18,... | collective-permute-start | bytes 393224 | tf_op jit(solution)/shard_map/ppermute | solution.py:40
  22.8 0.4 pick.2
  23.3 0.5 %collective-permute-start.11 = (bf16[128,512]{1,0:T(8,128)(2,1)S(1)}, bf16[128,512]{1,0:T(8,128)(2,1)S(1)}, u32[]{:S(2)}, u32[]{:S(2)}) collective-permute-start(bf16[128,512]{1,0:T(8,128)(2,1)S(1)} %get-tuple-element.34), channel_id=1, source_target_pairs={{0,2},{2,0},{4,6},{6,4},{8,10},{10,8},{12,14},{14,12},{16,18},{18,... | collective-permute-start | bytes 393224 | tf_op jit(solution)/shard_map/ppermute | solution.py:45
  23.8 2.0 %collective-permute-start.1 = (bf16[64,1024]{1,0:T(8,128)(2,1)S(1)}, bf16[64,1024]{1,0:T(8,128)(2,1)S(1)}, u32[]{:S(2)}, u32[]{:S(2)}) collective-permute-start(bf16[64,1024]{1,0:T(8,128)(2,1)S(1)} %get-tuple-element.28), channel_id=1, source_target_pairs={{0,1},{1,0},{2,3},{3,2},{4,5},{5,4},{6,7},{7,6},{8,9},{9,8},{10,11... | collective-permute-start | bytes 393224 | tf_op jit(solution)/shard_map/ppermute | solution.py:40
  25.8 0.5 %collective-permute-done.3.behind_ref.refs_0_ = bf16[128,512]{1,0:T(8,128)(2,1)S(1)} collective-permute-done((bf16[128,512]{1,0:T(8,128)(2,1)S(1)}, bf16[128,512]{1,0:T(8,128)(2,1)S(1)}, u32[]{:S(2)}, u32[]{:S(2)}) %collective-permute-start.3) | collective-permute-done | bytes 131104 | tf_op jit(solution)/shard_map/ppermute | solution.py:40
  26.3 0.7 %collective-permute-done.4.ahead_ref.refs_2_ = bf16[128,512]{1,0:T(8,128)(2,1)S(1)} collective-permute-done((bf16[128,512]{1,0:T(8,128)(2,1)S(1)}, bf16[128,512]{1,0:T(8,128)(2,1)S(1)}, u32[]{:S(2)}, u32[]{:S(2)}) %collective-permute-start.4) | collective-permute-done | bytes 131104 | tf_op jit(solution)/shard_map/ppermute | solution.py:40
  27.0 0.6 %collective-permute-start.6 = (bf16[128,512]{1,0:T(8,128)(2,1)S(1)}, bf16[128,512]{1,0:T(8,128)(2,1)S(1)}, u32[]{:S(2)}, u32[]{:S(2)}) collective-permute-start(bf16[128,512]{1,0:T(8,128)(2,1)S(1)} %far.2), channel_id=1, source_target_pairs={{0,4},{2,6},{4,0},{6,2},{8,12},{10,14},{12,8},{14,10},{16,20},{18,... | collective-permute-start | bytes 393224 | tf_op jit(solution)/shard_map/ppermute | solution.py:45
  27.7 1.7 %collective-permute-start.14 = (bf16[2,128,512]{2,1,0:T(8,128)(2,1)S(1)}, bf16[2,128,512]{2,1,0:T(8,128)(2,1)S(1)}, u32[]{:S(2)}, u32[]{:S(2)}) collective-permute-start(bf16[2,128,512]{2,1,0:T(8,128)(2,1)S(1)} %merge.2.refs_5_.refs_0_), channel_id=1, source_target_pairs={{0,1},{1,0},{2,3},{3,2},{4,5},{5,4},{6,7},{7,6},{8,9},{9,8},{10,11... | collective-permute-start | bytes 786440 | tf_op jit(solution)/shard_map/ppermute | solution.py:40
  29.7 1.4 %lags.2.refs_6_.lags_ref = bf16[2112,1024]{1,0:T(8,128)(2,1)S(1)} custom-call(bf16[64,1024]{1,0:T(8,128)(2,1)S(1)} %collective-permute-done.1.own_ref), custom_call_target="tpu_custom_call" | custom-call | bytes 8388608 | tf_op jit(solution)/shard_map/lags/pallas_call | solution.py:178
  31.1 0.9 %collective-permute-done.6.refs_4_ = bf16[128,512]{1,0:T(8,128)(2,1)S(1)} collective-permute-done((bf16[128,512]{1,0:T(8,128)(2,1)S(1)}, bf16[128,512]{1,0:T(8,128)(2,1)S(1)}, u32[]{:S(2)}, u32[]{:S(2)}) %collective-permute-start.6) | collective-permute-done | bytes 131104 | tf_op jit(solution)/shard_map/ppermute | solution.py:45
  32.5 0.5 %collective-permute-start.13 = (bf16[128,512]{1,0:T(8,128)(2,1)S(1)}, bf16[128,512]{1,0:T(8,128)(2,1)S(1)}, u32[]{:S(2)}, u32[]{:S(2)}) collective-permute-start(bf16[128,512]{1,0:T(8,128)(2,1)S(1)} %get-tuple-element.37), channel_id=1, source_target_pairs={{0,2},{2,0},{4,6},{6,4},{8,10},{10,8},{12,14},{14,12},{16,18},{18,... | collective-permute-start | bytes 393224 | tf_op jit(solution)/shard_map/ppermute | solution.py:45
  33.0 0.8 %collective-permute-done.12.refs_0_ = bf16[128,512]{1,0:T(8,128)(2,1)S(1)} collective-permute-done((bf16[128,512]{1,0:T(8,128)(2,1)S(1)}, bf16[128,512]{1,0:T(8,128)(2,1)S(1)}, u32[]{:S(2)}, u32[]{:S(2)}) %collective-permute-start.12) | collective-permute-done | bytes 131104 | tf_op jit(solution)/shard_map/ppermute | solution.py:45
  34.0 1.1 %collective-permute-done.14.refs_2_.refs_0_ = bf16[2,128,512]{2,1,0:T(8,128)(2,1)S(1)} collective-permute-done((bf16[2,128,512]{2,1,0:T(8,128)(2,1)S(1)}, bf16[2,128,512]{2,1,0:T(8,128)(2,1)S(1)}, u32[]{:S(2)}, u32[]{:S(2)}) %collective-permute-start.14) | collective-permute-done | bytes 262176 | tf_op jit(solution)/shard_map/ppermute | solution.py:40
  35.3 1.8 %collective-permute-start.15 = (bf16[2,128,512]{2,1,0:T(8,128)(2,1)S(1)}, bf16[2,128,512]{2,1,0:T(8,128)(2,1)S(1)}, u32[]{:S(2)}, u32[]{:S(2)}) collective-permute-start(bf16[2,128,512]{2,1,0:T(8,128)(2,1)S(1)} %merge.3.refs_1_), channel_id=1, source_target_pairs={{0,1},{1,0},{2,3},{3,2},{4,5},{5,4},{6,7},{7,6},{8,9},{9,8},{10,11... | collective-permute-start | bytes 786440 | tf_op jit(solution)/shard_map/ppermute | solution.py:40
  37.1 1.4 %lags.3.lags_ref = bf16[2112,1024]{1,0:T(8,128)(2,1)S(1)} custom-call(bf16[64,1024]{1,0:T(8,128)(2,1)S(1)} %get-tuple-element.38.own_ref), custom_call_target="tpu_custom_call" | custom-call | bytes 8388608 | tf_op jit(solution)/shard_map/lags/pallas_call | solution.py:178
  38.5 1.3 %accumulate.2.refs_1_ = f32[2112,256]{1,0:T(8,128)S(1)} custom-call(bf16[2112,1024]{1,0:T(8,128)(2,1)S(1)} %lags.3.lags_ref, bf16[2,128,512]{2,1,0:T(8,128)(2,1)S(1)} %merge.2.refs_5_.refs_0_, bf16[2,128,512]{2,1,0:T(8,128)(2,1)S(1)} %merge.3.refs_1_), custom_call_target="tpu_custom_call" | custom-call | tf_op jit(solution)/shard_map/accumulate/pallas_call | solution.py:300
  39.8 0.8 %accumulate.3.acc_ref = f32[2112,256]{1,0:T(8,128)S(1)} custom-call(bf16[2112,1024]{1,0:T(8,128)(2,1)S(1)} %lags.2.refs_6_.lags_ref, bf16[2,128,512]{2,1,0:T(8,128)(2,1)S(1)} %collective-permute-done.14.refs_2_.refs_0_, f32[2112,256]{1,0:T(8,128)S(1)} %accumulate.2.refs_1_), custom_call_target="tpu_custom_call" | custom-call | tf_op jit(solution)/shard_map/accumulate/pallas_call | solution.py:300
  40.6 2.1 %collective-permute-done.15.other_ref = bf16[2,128,512]{2,1,0:T(8,128)(2,1)S(1)} collective-permute-done((bf16[2,128,512]{2,1,0:T(8,128)(2,1)S(1)}, bf16[2,128,512]{2,1,0:T(8,128)(2,1)S(1)}, u32[]{:S(2)}, u32[]{:S(2)}) %collective-permute-start.15) | collective-permute-done | bytes 262176 | tf_op jit(solution)/shard_map/ppermute | solution.py:40
  42.7 1.9 %finish.1 = f32[4224,128]{1,0:T(8,128)} custom-call(s32[1,2]{1,0:T(1,128)S(1)} %copy-done, bf16[2112,1024]{1,0:T(8,128)(2,1)S(1)} %lags.2.refs_6_.lags_ref, bf16[2,128,512]{2,1,0:T(8,128)(2,1)S(1)} %collective-permute-done.15.other_ref, f32[2112,256]{1,0:T(8,128)S(1)} %accumulate.3.acc_ref), custom_call_target="tpu_custom_call" | custom-call | tf_op jit(solution)/shard_map/finish/pallas_call | solution.py:339
  (18 shorter events, 1.6 us)
Async XLA Ops:
  0.0 14.2 %copy-start = (s32[1,2]{1,0:T(1,128)S(1)}, s32[1,2]{1,0:T(1,128)}, u32[]{:S(2)}) copy-start(s32[1,2]{1,0:T(1,128)} %offsets.5) | copy-start | bytes 28
  0.0 0.7 %copy-start.1 = (f32[64]{0:T(128)S(1)}, f32[64]{0:T(128)}, u32[]{:S(2)}) copy-start(f32[64]{0:T(128)} %param.4) | copy-start | bytes 772
  2.0 6.5 %collective-permute-start = (bf16[128,128]{1,0:T(8,128)(2,1)S(1)}, bf16[128,128]{1,0:T(8,128)(2,1)S(1)}, u32[]{:S(2)}, u32[]{:S(2)}) collective-permute-start(bf16[128,128]{1,0:T(8,128)(2,1)S(1)} %get-tuple-element.22), channel_id=1, source_target_pairs={{0,1},{2,3},{4,5},{6,7},{8,9},{10,11},{12,13},{14,15},{16,17},{18,... | collective-permute-start | bytes 98312 | tf_op jit(solution)/shard_map/ppermute | solution.py:361
  8.8 7.8 %collective-permute-start.7 = (bf16[128,512]{1,0:T(8,128)(2,1)S(1)}, bf16[128,512]{1,0:T(8,128)(2,1)S(1)}, u32[]{:S(2)}, u32[]{:S(2)}) collective-permute-start(bf16[128,512]{1,0:T(8,128)(2,1)S(1)} %get-tuple-element.31.refs_1_), channel_id=1, source_target_pairs={{0,8},{2,10},{4,12},{6,14},{8,16},{10,18},{12,20},{14,22},{16,24},... | collective-permute-start | bytes 393224 | tf_op jit(solution)/shard_map/ppermute | solution.py:40
  10.5 6.9 %collective-permute-start.8 = (bf16[128,512]{1,0:T(8,128)(2,1)S(1)}, bf16[128,512]{1,0:T(8,128)(2,1)S(1)}, u32[]{:S(2)}, u32[]{:S(2)}) collective-permute-start(bf16[128,512]{1,0:T(8,128)(2,1)S(1)} %get-tuple-element.31.refs_1_), channel_id=1, source_target_pairs={{0,24},{2,26},{4,28},{6,30},{8,0},{10,2},{12,4},{14,6},{16,8},{18,... | collective-permute-start | bytes 393224 | tf_op jit(solution)/shard_map/ppermute | solution.py:40
  12.7 10.1 %collective-permute-start.5 = (bf16[128,1024]{1,0:T(8,128)(2,1)S(1)}, bf16[128,1024]{1,0:T(8,128)(2,1)S(1)}, u32[]{:S(2)}, u32[]{:S(2)}) collective-permute-start(bf16[128,1024]{1,0:T(8,128)(2,1)S(1)} %get-tuple-element.30), channel_id=1, source_target_pairs={{0,4},{2,6},{4,0},{6,2},{8,12},{10,14},{12,8},{14,10},{16,20},{18,... | collective-permute-start | bytes 786440 | tf_op jit(solution)/shard_map/ppermute | solution.py:45
  14.2 1.1 %collective-permute-start.2 = (s32[1,2]{1,0:T(1,128)S(1)}, s32[1,2]{1,0:T(1,128)S(1)}, u32[]{:S(2)}, u32[]{:S(2)}) collective-permute-start(s32[1,2]{1,0:T(1,128)S(1)} %copy-done), channel_id=1, source_target_pairs={{0,2},{2,0},{4,6},{6,4},{8,10},{10,8},{12,14},{14,12},{16,18},{18,... | collective-permute-start | bytes 32 | tf_op jit(solution)/shard_map/ppermute | solution.py:45
  17.4 5.4 %collective-permute-start.9 = (bf16[128,512]{1,0:T(8,128)(2,1)S(1)}, bf16[128,512]{1,0:T(8,128)(2,1)S(1)}, u32[]{:S(2)}, u32[]{:S(2)}) collective-permute-start(bf16[128,512]{1,0:T(8,128)(2,1)S(1)} %far.3), channel_id=1, source_target_pairs={{0,4},{2,6},{4,0},{6,2},{8,12},{10,14},{12,8},{14,10},{16,20},{18,... | collective-permute-start | bytes 393224 | tf_op jit(solution)/shard_map/ppermute | solution.py:45
  19.0 7.3 %collective-permute-start.3 = (bf16[128,512]{1,0:T(8,128)(2,1)S(1)}, bf16[128,512]{1,0:T(8,128)(2,1)S(1)}, u32[]{:S(2)}, u32[]{:S(2)}) collective-permute-start(bf16[128,512]{1,0:T(8,128)(2,1)S(1)} %get-tuple-element.29.refs_1_), channel_id=1, source_target_pairs={{0,8},{2,10},{4,12},{6,14},{8,16},{10,18},{12,20},{14,22},{16,24},... | collective-permute-start | bytes 393224 | tf_op jit(solution)/shard_map/ppermute | solution.py:40
  20.1 6.8 %collective-permute-start.4 = (bf16[128,512]{1,0:T(8,128)(2,1)S(1)}, bf16[128,512]{1,0:T(8,128)(2,1)S(1)}, u32[]{:S(2)}, u32[]{:S(2)}) collective-permute-start(bf16[128,512]{1,0:T(8,128)(2,1)S(1)} %get-tuple-element.29.refs_1_), channel_id=1, source_target_pairs={{0,24},{2,26},{4,28},{6,30},{8,0},{10,2},{12,4},{14,6},{16,8},{18,... | collective-permute-start | bytes 393224 | tf_op jit(solution)/shard_map/ppermute | solution.py:40
  23.2 4.3 %collective-permute-start.10 = (bf16[128,512]{1,0:T(8,128)(2,1)S(1)}, bf16[128,512]{1,0:T(8,128)(2,1)S(1)}, u32[]{:S(2)}, u32[]{:S(2)}) collective-permute-start(bf16[128,512]{1,0:T(8,128)(2,1)S(1)} %get-tuple-element.33), channel_id=1, source_target_pairs={{0,2},{2,0},{4,6},{6,4},{8,10},{10,8},{12,14},{14,12},{16,18},{18,... | collective-permute-start | bytes 393224 | tf_op jit(solution)/shard_map/ppermute | solution.py:45
  23.3 4.3 %collective-permute-start.11 = (bf16[128,512]{1,0:T(8,128)(2,1)S(1)}, bf16[128,512]{1,0:T(8,128)(2,1)S(1)}, u32[]{:S(2)}, u32[]{:S(2)}) collective-permute-start(bf16[128,512]{1,0:T(8,128)(2,1)S(1)} %get-tuple-element.34), channel_id=1, source_target_pairs={{0,2},{2,0},{4,6},{6,4},{8,10},{10,8},{12,14},{14,12},{16,18},{18,... | collective-permute-start | bytes 393224 | tf_op jit(solution)/shard_map/ppermute | solution.py:45
  23.8 5.9 %collective-permute-start.1 = (bf16[64,1024]{1,0:T(8,128)(2,1)S(1)}, bf16[64,1024]{1,0:T(8,128)(2,1)S(1)}, u32[]{:S(2)}, u32[]{:S(2)}) collective-permute-start(bf16[64,1024]{1,0:T(8,128)(2,1)S(1)} %get-tuple-element.28), channel_id=1, source_target_pairs={{0,1},{1,0},{2,3},{3,2},{4,5},{5,4},{6,7},{7,6},{8,9},{9,8},{10,11... | collective-permute-start | bytes 393224 | tf_op jit(solution)/shard_map/ppermute | solution.py:40
  27.0 5.0 %collective-permute-start.6 = (bf16[128,512]{1,0:T(8,128)(2,1)S(1)}, bf16[128,512]{1,0:T(8,128)(2,1)S(1)}, u32[]{:S(2)}, u32[]{:S(2)}) collective-permute-start(bf16[128,512]{1,0:T(8,128)(2,1)S(1)} %far.2), channel_id=1, source_target_pairs={{0,4},{2,6},{4,0},{6,2},{8,12},{10,14},{12,8},{14,10},{16,20},{18,... | collective-permute-start | bytes 393224 | tf_op jit(solution)/shard_map/ppermute | solution.py:45
  27.7 7.5 %collective-permute-start.14 = (bf16[2,128,512]{2,1,0:T(8,128)(2,1)S(1)}, bf16[2,128,512]{2,1,0:T(8,128)(2,1)S(1)}, u32[]{:S(2)}, u32[]{:S(2)}) collective-permute-start(bf16[2,128,512]{2,1,0:T(8,128)(2,1)S(1)} %merge.2.refs_5_.refs_0_), channel_id=1, source_target_pairs={{0,1},{1,0},{2,3},{3,2},{4,5},{5,4},{6,7},{7,6},{8,9},{9,8},{10,11... | collective-permute-start | bytes 786440 | tf_op jit(solution)/shard_map/ppermute | solution.py:40
  32.4 1.4 %collective-permute-start.12 = (bf16[128,512]{1,0:T(8,128)(2,1)S(1)}, bf16[128,512]{1,0:T(8,128)(2,1)S(1)}, u32[]{:S(2)}, u32[]{:S(2)}) collective-permute-start(bf16[128,512]{1,0:T(8,128)(2,1)S(1)} %get-tuple-element.36), channel_id=1, source_target_pairs={{0,2},{2,0},{4,6},{6,4},{8,10},{10,8},{12,14},{14,12},{16,18},{18,... | collective-permute-start | bytes 393224 | tf_op jit(solution)/shard_map/ppermute | solution.py:45
  32.5 1.5 %collective-permute-start.13 = (bf16[128,512]{1,0:T(8,128)(2,1)S(1)}, bf16[128,512]{1,0:T(8,128)(2,1)S(1)}, u32[]{:S(2)}, u32[]{:S(2)}) collective-permute-start(bf16[128,512]{1,0:T(8,128)(2,1)S(1)} %get-tuple-element.37), channel_id=1, source_target_pairs={{0,2},{2,0},{4,6},{6,4},{8,10},{10,8},{12,14},{14,12},{16,18},{18,... | collective-permute-start | bytes 393224 | tf_op jit(solution)/shard_map/ppermute | solution.py:45
  35.3 7.5 %collective-permute-start.15 = (bf16[2,128,512]{2,1,0:T(8,128)(2,1)S(1)}, bf16[2,128,512]{2,1,0:T(8,128)(2,1)S(1)}, u32[]{:S(2)}, u32[]{:S(2)}) collective-permute-start(bf16[2,128,512]{2,1,0:T(8,128)(2,1)S(1)} %merge.3.refs_1_), channel_id=1, source_target_pairs={{0,1},{1,0},{2,3},{3,2},{4,5},{5,4},{6,7},{7,6},{8,9},{9,8},{10,11... | collective-permute-start | bytes 786440 | tf_op jit(solution)/shard_map/ppermute | solution.py:40

commit v8 on v7

--- a/solution.py
+++ b/solution.py
@@ -22,6 +22,7 @@
 CHUNKS = len(EDGES) - 1
 TEAM = 4
 HEAD_GRANT = 52 << 20
+BIAS = 32
 GROUP = 16
 VMEM = pltpu.VMEM
 F32 = jnp.float32
@@ -217,9 +218,15 @@
     lanes = keep_ref.shape[2]
     here = lax.rem(lax.axis_index("chan"), TEAM)
     second = here >> 1
+    lane = lax.broadcasted_iota(jnp.int32, own_offsets.shape, 1)
+    weight = jnp.ones(own_offsets.shape, jnp.int32)
+    for slot in range(1, slots):
+        weight = jnp.where(lane == slot, 1 << (6 * slot), weight)
+    packed = (own_offsets[...] + BIAS) * weight + (core_offsets[...] + BIAS) * (weight << (6 * slots))
+    code = jnp.sum(packed.astype(F32)).astype(jnp.int32)
     for slot in range(slots):
-        for offsets, place in ((own_offsets, here), (core_offsets, here ^ 1)):
-            target = place + offsets[...][0, slot]
+        for which, place in enumerate((here, here ^ 1)):
+            target = place + ((code >> (6 * (slots * which + slot))) & 63) - BIAS
             hop = jnp.clip(target >> 2, -hops, hops)
             same = ((target >> 1) & 1) == second
             other = jnp.where(jnp.abs(hop) < hops, 3 * hops + hop, 4 * hops)
@@ -227,7 +234,7 @@
             for source, ref in enumerate(sources):
 
                 @pl.when(index == source)
-                def _(ref=ref, slot=slot, own=offsets is own_offsets):
+                def _(ref=ref, slot=slot, own=which == 0):
                     block = ref[...] if ref.shape[1] == lanes else ref[:, first : first + lanes]
                     if own:
                         keep_ref[slot] = block
@@ -386,7 +393,7 @@
     lags = [lay_out_lags(part) for part in own]
 
     pieces = []
-    after_far, after_pick, after_merge = [core_offsets], [], []
+    after_far, after_pick, after_merge = [core_offsets] + own[1:], [], []
     for chunk in range(CHUNKS):
         piece, send = gather(chunk, directs[chunk], after_far, after_pick, after_merge)
         after_far, after_pick, after_merge = [], [piece[0]] + lags[1:], piece[1:]

time: 44.8 us -> 44.7 us (level)
  waiting for transfers between devices: 10.4 us -> 11.1 us
  starting transfers between devices: 22.9 us -> 22.4 us
    ppermute x7, starting transfers between devices: 13.2 us -> 11.8 us  [shift(): return lax.ppermute(x, axis, [(i, (i + by) % n) for i in range(n)])]
    ppermute x8, waiting for transfers between devices: 3.04 us -> 4.19 us  [swap(): return lax.ppermute(x, 'chan', [(i, i ^ bit) for i in range(n)])]
    ppermute x8, starting transfers between devices: 4.8 us -> 5.69 us  [swap(): return lax.ppermute(x, 'chan', [(i, i ^ bit) for i in range(n)])]
    ppermute x7, waiting for transfers between devices: 6.8 us -> 6.31 us  [shift(): return lax.ppermute(x, axis, [(i, (i + by) % n) for i in range(n)])]
  transfers between devices with their start and end apart: 16 -> 16, of which waited for: 12 -> 10; matrix products, arithmetic and copies ran while one was open for 0% -> 0% of each run, Pallas kernels for 15% -> 15%
where the time goes in v8:
time: 44.7 us; the launch traced here: 44.5 us
  starting transfers between devices  22.4 us (50%)
  waiting for transfers between devices  11.1 us (25%)
  Pallas kernels  10.3 us (23%)
  local copies, waits for them, and re-layouts  0.67 us (1%)
    ppermute x7, starting transfers between devices, shift(): return lax.ppermute(x, axis, [(i, (i + by) % n) for i in range(n)])  11.8 us
    ppermute x7, waiting for transfers between devices, shift(): return lax.ppermute(x, axis, [(i, (i + by) % n) for i in range(n)])  6.31 us
    ppermute x8, starting transfers between devices, swap(): return lax.ppermute(x, 'chan', [(i, i ^ bit) for i in range(n)])  5.69 us
    ppermute x1, starting transfers between devices, body(): before = lax.ppermute(tail, 'win', [(i, i + 1) for i in range(win - 1)])  4.87 us
    ppermute x8, waiting for transfers between devices, swap(): return lax.ppermute(x, 'chan', [(i, i ^ bit) for i in range(n)])  4.19 us
    pallas_call x2, Pallas kernels, lay_out_lags(): pl.pallas_call(lags_kernel, out_shape=jax.ShapeDtypeStruct((rows * LAGS,...  2.84 us
    pallas_call x2, Pallas kernels, accumulate(): pl.pallas_call(functools.partial(accumulate_kernel, firsts, acc is not No...  2.09 us
    pallas_call x1, Pallas kernels, finish(): pl.pallas_call(functools.partial(finish_kernel, reach, factor, first), ou...  1.91 us
  transfers between devices with their start and end apart: 16, of which 10 were waited for; matrix products, arithmetic and copies ran while one was open for 0% of the time, Pallas kernels for 15%

profile of v8, /device:TPU:0, one launch (start us, length us, event | category | flops | bytes accessed | tf_op | source)
XLA Modules:
  0.0 44.5 jit_solution(9005769342941686579)
XLA Ops:
  0.0 0.7 %copy-done.1 = f32[64]{0:T(128)S(1)} copy-done((f32[64]{0:T(128)S(1)}, f32[64]{0:T(128)}, u32[]{:S(2)}) %copy-start.1) | copy-done | bytes 280
  0.7 1.3 %head.1 = (bf16[128,128]{1,0:T(8,128)(2,1)S(1)}, bf16[128,4096]{1,0:T(8,128)(2,1)S(1)}, f32[1,64]{1,0:T(1,128)S(1)}) custom-call(bf16[128,4096]{1,0:T(8,128)(2,1)} %records_ref.1, f32[1,64]{1,0:T(1,128)S(1)} %bitcast.4), custom_call_target="tpu_custom_call" | custom-call | tf_op jit(solution)/shard_map/head/pallas_call | solution.py:63
  2.0 4.9 %collective-permute-start = (bf16[128,128]{1,0:T(8,128)(2,1)S(1)}, bf16[128,128]{1,0:T(8,128)(2,1)S(1)}, u32[]{:S(2)}, u32[]{:S(2)}) collective-permute-start(bf16[128,128]{1,0:T(8,128)(2,1)S(1)} %get-tuple-element.22), channel_id=1, source_target_pairs={{0,1},{2,3},{4,5},{6,7},{8,9},{10,11},{12,13},{14,15},{16,17},{18,... | collective-permute-start | bytes 98312 | tf_op jit(solution)/shard_map/ppermute | solution.py:368
  6.9 1.0 %bulk_filter.1 = (f32[128,1024]{1,0:T(8,128)S(1)}, f32[128,128]{1,0:T(8,128)S(1)}, bf16[384,128]{1,0:T(8,128)(2,1)S(1)}) custom-call(bf16[128,4096]{1,0:T(8,128)(2,1)S(1)} %get-tuple-element.23.records_ref, f32[1,64]{1,0:T(1,128)S(1)} %get-tuple-element.24.taps_ref), custom_call_target="tpu_custom_call" | custom-call | tf_op jit(solution)/shard_map/bulk_filter/pallas_call | solution.py:106
  7.9 0.6 %collective-permute-done.tail_ref = bf16[128,128]{1,0:T(8,128)(2,1)S(1)} collective-permute-done((bf16[128,128]{1,0:T(8,128)(2,1)S(1)}, bf16[128,128]{1,0:T(8,128)(2,1)S(1)}, u32[]{:S(2)}, u32[]{:S(2)}) %collective-permute-start) | collective-permute-done | bytes 32800 | tf_op jit(solution)/shard_map/ppermute | solution.py:368
  8.5 0.4 whiten.1
  8.8 1.6 %collective-permute-start.7 = (bf16[128,512]{1,0:T(8,128)(2,1)S(1)}, bf16[128,512]{1,0:T(8,128)(2,1)S(1)}, u32[]{:S(2)}, u32[]{:S(2)}) collective-permute-start(bf16[128,512]{1,0:T(8,128)(2,1)S(1)} %get-tuple-element.31.refs_1_), channel_id=1, source_target_pairs={{0,8},{2,10},{4,12},{6,14},{8,16},{10,18},{12,20},{14,22},{16,24},... | collective-permute-start | bytes 393224 | tf_op jit(solution)/shard_map/ppermute | solution.py:41
  10.5 2.2 %collective-permute-start.8 = (bf16[128,512]{1,0:T(8,128)(2,1)S(1)}, bf16[128,512]{1,0:T(8,128)(2,1)S(1)}, u32[]{:S(2)}, u32[]{:S(2)}) collective-permute-start(bf16[128,512]{1,0:T(8,128)(2,1)S(1)} %get-tuple-element.31.refs_1_), channel_id=1, source_target_pairs={{0,24},{2,26},{4,28},{6,30},{8,0},{10,2},{12,4},{14,6},{16,8},{18,... | collective-permute-start | bytes 393224 | tf_op jit(solution)/shard_map/ppermute | solution.py:41
  12.7 2.3 %collective-permute-start.1 = (bf16[64,1024]{1,0:T(8,128)(2,1)S(1)}, bf16[64,1024]{1,0:T(8,128)(2,1)S(1)}, u32[]{:S(2)}, u32[]{:S(2)}) collective-permute-start(bf16[64,1024]{1,0:T(8,128)(2,1)S(1)} %get-tuple-element.28), channel_id=1, source_target_pairs={{0,1},{1,0},{2,3},{3,2},{4,5},{5,4},{6,7},{7,6},{8,9},{9,8},{10,11... | collective-permute-start | bytes 393224 | tf_op jit(solution)/shard_map/ppermute | solution.py:41
  15.0 1.5 %collective-permute-start.5 = (bf16[128,1024]{1,0:T(8,128)(2,1)S(1)}, bf16[128,1024]{1,0:T(8,128)(2,1)S(1)}, u32[]{:S(2)}, u32[]{:S(2)}) collective-permute-start(bf16[128,1024]{1,0:T(8,128)(2,1)S(1)} %get-tuple-element.30), channel_id=1, source_target_pairs={{0,4},{2,6},{4,0},{6,2},{8,12},{10,14},{12,8},{14,10},{16,20},{18,... | collective-permute-start | bytes 786440 | tf_op jit(solution)/shard_map/ppermute | solution.py:46
  16.5 1.1 %collective-permute-done.2.refs_0_.core_offsets = s32[1,2]{1,0:T(1,128)S(1)} collective-permute-done((s32[1,2]{1,0:T(1,128)S(1)}, s32[1,2]{1,0:T(1,128)S(1)}, u32[]{:S(2)}, u32[]{:S(2)}) %collective-permute-start.2) | collective-permute-done | bytes 40 | tf_op jit(solution)/shard_map/ppermute | solution.py:46
  17.7 0.3 collective-permute-done.1.own_ref.refs_1_
  18.0 1.6 %collective-permute-start.9 = (bf16[128,512]{1,0:T(8,128)(2,1)S(1)}, bf16[128,512]{1,0:T(8,128)(2,1)S(1)}, u32[]{:S(2)}, u32[]{:S(2)}) collective-permute-start(bf16[128,512]{1,0:T(8,128)(2,1)S(1)} %far.3), channel_id=1, source_target_pairs={{0,4},{2,6},{4,0},{6,2},{8,12},{10,14},{12,8},{14,10},{16,20},{18,... | collective-permute-start | bytes 393224 | tf_op jit(solution)/shard_map/ppermute | solution.py:46
  19.6 0.6 %collective-permute-start.3 = (bf16[128,512]{1,0:T(8,128)(2,1)S(1)}, bf16[128,512]{1,0:T(8,128)(2,1)S(1)}, u32[]{:S(2)}, u32[]{:S(2)}) collective-permute-start(bf16[128,512]{1,0:T(8,128)(2,1)S(1)} %get-tuple-element.29.refs_1_), channel_id=1, source_target_pairs={{0,8},{2,10},{4,12},{6,14},{8,16},{10,18},{12,20},{14,22},{16,24},... | collective-permute-start | bytes 393224 | tf_op jit(solution)/shard_map/ppermute | solution.py:41
  20.1 3.3 %collective-permute-start.4 = (bf16[128,512]{1,0:T(8,128)(2,1)S(1)}, bf16[128,512]{1,0:T(8,128)(2,1)S(1)}, u32[]{:S(2)}, u32[]{:S(2)}) collective-permute-start(bf16[128,512]{1,0:T(8,128)(2,1)S(1)} %get-tuple-element.29.refs_1_), channel_id=1, source_target_pairs={{0,24},{2,26},{4,28},{6,30},{8,0},{10,2},{12,4},{14,6},{16,8},{18,... | collective-permute-start | bytes 393224 | tf_op jit(solution)/shard_map/ppermute | solution.py:41
  23.4 0.8 %collective-permute-done.9.refs_4_ = bf16[128,512]{1,0:T(8,128)(2,1)S(1)} collective-permute-done((bf16[128,512]{1,0:T(8,128)(2,1)S(1)}, bf16[128,512]{1,0:T(8,128)(2,1)S(1)}, u32[]{:S(2)}, u32[]{:S(2)}) %collective-permute-start.9) | collective-permute-done | bytes 131104 | tf_op jit(solution)/shard_map/ppermute | solution.py:46
  24.2 0.3 pick.2
  24.6 0.5 %collective-permute-start.11 = (bf16[128,512]{1,0:T(8,128)(2,1)S(1)}, bf16[128,512]{1,0:T(8,128)(2,1)S(1)}, u32[]{:S(2)}, u32[]{:S(2)}) collective-permute-start(bf16[128,512]{1,0:T(8,128)(2,1)S(1)} %get-tuple-element.34), channel_id=1, source_target_pairs={{0,2},{2,0},{4,6},{6,4},{8,10},{10,8},{12,14},{14,12},{16,18},{18,... | collective-permute-start | bytes 393224 | tf_op jit(solution)/shard_map/ppermute | solution.py:46
  25.1 1.9 %collective-permute-done.3.behind_ref.refs_0_ = bf16[128,512]{1,0:T(8,128)(2,1)S(1)} collective-permute-done((bf16[128,512]{1,0:T(8,128)(2,1)S(1)}, bf16[128,512]{1,0:T(8,128)(2,1)S(1)}, u32[]{:S(2)}, u32[]{:S(2)}) %collective-permute-start.3) | collective-permute-done | bytes 131104 | tf_op jit(solution)/shard_map/ppermute | solution.py:41
  27.0 1.5 %collective-permute-start.6 = (bf16[128,512]{1,0:T(8,128)(2,1)S(1)}, bf16[128,512]{1,0:T(8,128)(2,1)S(1)}, u32[]{:S(2)}, u32[]{:S(2)}) collective-permute-start(bf16[128,512]{1,0:T(8,128)(2,1)S(1)} %far.2), channel_id=1, source_target_pairs={{0,4},{2,6},{4,0},{6,2},{8,12},{10,14},{12,8},{14,10},{16,20},{18,... | collective-permute-start | bytes 393224 | tf_op jit(solution)/shard_map/ppermute | solution.py:46
  28.6 0.8 %collective-permute-start.14 = (bf16[2,128,512]{2,1,0:T(8,128)(2,1)S(1)}, bf16[2,128,512]{2,1,0:T(8,128)(2,1)S(1)}, u32[]{:S(2)}, u32[]{:S(2)}) collective-permute-start(bf16[2,128,512]{2,1,0:T(8,128)(2,1)S(1)} %merge.2.refs_5_.refs_0_), channel_id=1, source_target_pairs={{0,1},{1,0},{2,3},{3,2},{4,5},{5,4},{6,7},{7,6},{8,9},{9,8},{10,11... | collective-permute-start | bytes 786440 | tf_op jit(solution)/shard_map/ppermute | solution.py:41
  29.4 1.4 %lags.2.refs_6_.lags_ref = bf16[2112,1024]{1,0:T(8,128)(2,1)S(1)} custom-call(bf16[64,1024]{1,0:T(8,128)(2,1)S(1)} %collective-permute-done.1.own_ref.refs_1_), custom_call_target="tpu_custom_call" | custom-call | bytes 8388608 | tf_op jit(solution)/shard_map/lags/pallas_call | solution.py:179
  30.8 1.2 %collective-permute-done.6.refs_4_ = bf16[128,512]{1,0:T(8,128)(2,1)S(1)} collective-permute-done((bf16[128,512]{1,0:T(8,128)(2,1)S(1)}, bf16[128,512]{1,0:T(8,128)(2,1)S(1)}, u32[]{:S(2)}, u32[]{:S(2)}) %collective-permute-start.6) | collective-permute-done | bytes 131104 | tf_op jit(solution)/shard_map/ppermute | solution.py:46
  32.4 0.5 %collective-permute-start.13 = (bf16[128,512]{1,0:T(8,128)(2,1)S(1)}, bf16[128,512]{1,0:T(8,128)(2,1)S(1)}, u32[]{:S(2)}, u32[]{:S(2)}) collective-permute-start(bf16[128,512]{1,0:T(8,128)(2,1)S(1)} %get-tuple-element.37), channel_id=1, source_target_pairs={{0,2},{2,0},{4,6},{6,4},{8,10},{10,8},{12,14},{14,12},{16,18},{18,... | collective-permute-start | bytes 393224 | tf_op jit(solution)/shard_map/ppermute | solution.py:46
  32.9 0.8 %collective-permute-done.12.refs_0_ = bf16[128,512]{1,0:T(8,128)(2,1)S(1)} collective-permute-done((bf16[128,512]{1,0:T(8,128)(2,1)S(1)}, bf16[128,512]{1,0:T(8,128)(2,1)S(1)}, u32[]{:S(2)}, u32[]{:S(2)}) %collective-permute-start.12) | collective-permute-done | bytes 131104 | tf_op jit(solution)/shard_map/ppermute | solution.py:46
  33.9 1.1 %collective-permute-done.14.refs_2_.refs_0_ = bf16[2,128,512]{2,1,0:T(8,128)(2,1)S(1)} collective-permute-done((bf16[2,128,512]{2,1,0:T(8,128)(2,1)S(1)}, bf16[2,128,512]{2,1,0:T(8,128)(2,1)S(1)}, u32[]{:S(2)}, u32[]{:S(2)}) %collective-permute-start.14) | collective-permute-done | bytes 262176 | tf_op jit(solution)/shard_map/ppermute | solution.py:41
  35.2 1.0 %collective-permute-start.15 = (bf16[2,128,512]{2,1,0:T(8,128)(2,1)S(1)}, bf16[2,128,512]{2,1,0:T(8,128)(2,1)S(1)}, u32[]{:S(2)}, u32[]{:S(2)}) collective-permute-start(bf16[2,128,512]{2,1,0:T(8,128)(2,1)S(1)} %merge.3.refs_1_), channel_id=1, source_target_pairs={{0,1},{1,0},{2,3},{3,2},{4,5},{5,4},{6,7},{7,6},{8,9},{9,8},{10,11... | collective-permute-start | bytes 786440 | tf_op jit(solution)/shard_map/ppermute | solution.py:41
  36.2 1.4 %lags.3.lags_ref = bf16[2112,1024]{1,0:T(8,128)(2,1)S(1)} custom-call(bf16[64,1024]{1,0:T(8,128)(2,1)S(1)} %get-tuple-element.38.own_ref), custom_call_target="tpu_custom_call" | custom-call | bytes 8388608 | tf_op jit(solution)/shard_map/lags/pallas_call | solution.py:179
  37.6 1.3 %accumulate.2.refs_1_ = f32[2112,256]{1,0:T(8,128)S(1)} custom-call(bf16[2112,1024]{1,0:T(8,128)(2,1)S(1)} %lags.3.lags_ref, bf16[2,128,512]{2,1,0:T(8,128)(2,1)S(1)} %merge.2.refs_5_.refs_0_, bf16[2,128,512]{2,1,0:T(8,128)(2,1)S(1)} %merge.3.refs_1_), custom_call_target="tpu_custom_call" | custom-call | tf_op jit(solution)/shard_map/accumulate/pallas_call | solution.py:307
  38.9 0.8 %accumulate.3.acc_ref = f32[2112,256]{1,0:T(8,128)S(1)} custom-call(bf16[2112,1024]{1,0:T(8,128)(2,1)S(1)} %lags.2.refs_6_.lags_ref, bf16[2,128,512]{2,1,0:T(8,128)(2,1)S(1)} %collective-permute-done.14.refs_2_.refs_0_, f32[2112,256]{1,0:T(8,128)S(1)} %accumulate.2.refs_1_), custom_call_target="tpu_custom_call" | custom-call | tf_op jit(solution)/shard_map/accumulate/pallas_call | solution.py:307
  39.7 2.9 %collective-permute-done.15.other_ref = bf16[2,128,512]{2,1,0:T(8,128)(2,1)S(1)} collective-permute-done((bf16[2,128,512]{2,1,0:T(8,128)(2,1)S(1)}, bf16[2,128,512]{2,1,0:T(8,128)(2,1)S(1)}, u32[]{:S(2)}, u32[]{:S(2)}) %collective-permute-start.15) | collective-permute-done | bytes 262176 | tf_op jit(solution)/shard_map/ppermute | solution.py:41
  42.6 1.9 %finish.1 = f32[4224,128]{1,0:T(8,128)} custom-call(s32[1,2]{1,0:T(1,128)S(1)} %copy-done, bf16[2112,1024]{1,0:T(8,128)(2,1)S(1)} %lags.2.refs_6_.lags_ref, bf16[2,128,512]{2,1,0:T(8,128)(2,1)S(1)} %collective-permute-done.15.other_ref, f32[2112,256]{1,0:T(8,128)S(1)} %accumulate.3.acc_ref), custom_call_target="tpu_custom_call" | custom-call | tf_op jit(solution)/shard_map/finish/pallas_call | solution.py:346
  (18 shorter events, 0.8 us)
Async XLA Ops:
  0.0 16.5 %copy-start = (s32[1,2]{1,0:T(1,128)S(1)}, s32[1,2]{1,0:T(1,128)}, u32[]{:S(2)}) copy-start(s32[1,2]{1,0:T(1,128)} %offsets.5) | copy-start | bytes 28
  0.0 0.7 %copy-start.1 = (f32[64]{0:T(128)S(1)}, f32[64]{0:T(128)}, u32[]{:S(2)}) copy-start(f32[64]{0:T(128)} %param.4) | copy-start | bytes 772
  2.0 6.5 %collective-permute-start = (bf16[128,128]{1,0:T(8,128)(2,1)S(1)}, bf16[128,128]{1,0:T(8,128)(2,1)S(1)}, u32[]{:S(2)}, u32[]{:S(2)}) collective-permute-start(bf16[128,128]{1,0:T(8,128)(2,1)S(1)} %get-tuple-element.22), channel_id=1, source_target_pairs={{0,1},{2,3},{4,5},{6,7},{8,9},{10,11},{12,13},{14,15},{16,17},{18,... | collective-permute-start | bytes 98312 | tf_op jit(solution)/shard_map/ppermute | solution.py:368
  8.8 8.8 %collective-permute-start.7 = (bf16[128,512]{1,0:T(8,128)(2,1)S(1)}, bf16[128,512]{1,0:T(8,128)(2,1)S(1)}, u32[]{:S(2)}, u32[]{:S(2)}) collective-permute-start(bf16[128,512]{1,0:T(8,128)(2,1)S(1)} %get-tuple-element.31.refs_1_), channel_id=1, source_target_pairs={{0,8},{2,10},{4,12},{6,14},{8,16},{10,18},{12,20},{14,22},{16,24},... | collective-permute-start | bytes 393224 | tf_op jit(solution)/shard_map/ppermute | solution.py:41
  10.5 7.2 %collective-permute-start.8 = (bf16[128,512]{1,0:T(8,128)(2,1)S(1)}, bf16[128,512]{1,0:T(8,128)(2,1)S(1)}, u32[]{:S(2)}, u32[]{:S(2)}) collective-permute-start(bf16[128,512]{1,0:T(8,128)(2,1)S(1)} %get-tuple-element.31.refs_1_), channel_id=1, source_target_pairs={{0,24},{2,26},{4,28},{6,30},{8,0},{10,2},{12,4},{14,6},{16,8},{18,... | collective-permute-start | bytes 393224 | tf_op jit(solution)/shard_map/ppermute | solution.py:41
  12.7 5.3 %collective-permute-start.1 = (bf16[64,1024]{1,0:T(8,128)(2,1)S(1)}, bf16[64,1024]{1,0:T(8,128)(2,1)S(1)}, u32[]{:S(2)}, u32[]{:S(2)}) collective-permute-start(bf16[64,1024]{1,0:T(8,128)(2,1)S(1)} %get-tuple-element.28), channel_id=1, source_target_pairs={{0,1},{1,0},{2,3},{3,2},{4,5},{5,4},{6,7},{7,6},{8,9},{9,8},{10,11... | collective-permute-start | bytes 393224 | tf_op jit(solution)/shard_map/ppermute | solution.py:41
  15.0 9.2 %collective-permute-start.5 = (bf16[128,1024]{1,0:T(8,128)(2,1)S(1)}, bf16[128,1024]{1,0:T(8,128)(2,1)S(1)}, u32[]{:S(2)}, u32[]{:S(2)}) collective-permute-start(bf16[128,1024]{1,0:T(8,128)(2,1)S(1)} %get-tuple-element.30), channel_id=1, source_target_pairs={{0,4},{2,6},{4,0},{6,2},{8,12},{10,14},{12,8},{14,10},{16,20},{18,... | collective-permute-start | bytes 786440 | tf_op jit(solution)/shard_map/ppermute | solution.py:46
  16.5 1.1 %collective-permute-start.2 = (s32[1,2]{1,0:T(1,128)S(1)}, s32[1,2]{1,0:T(1,128)S(1)}, u32[]{:S(2)}, u32[]{:S(2)}) collective-permute-start(s32[1,2]{1,0:T(1,128)S(1)} %copy-done), channel_id=1, source_target_pairs={{0,2},{2,0},{4,6},{6,4},{8,10},{10,8},{12,14},{14,12},{16,18},{18,... | collective-permute-start | bytes 32 | tf_op jit(solution)/shard_map/ppermute | solution.py:46
  18.0 6.2 %collective-permute-start.9 = (bf16[128,512]{1,0:T(8,128)(2,1)S(1)}, bf16[128,512]{1,0:T(8,128)(2,1)S(1)}, u32[]{:S(2)}, u32[]{:S(2)}) collective-permute-start(bf16[128,512]{1,0:T(8,128)(2,1)S(1)} %far.3), channel_id=1, source_target_pairs={{0,4},{2,6},{4,0},{6,2},{8,12},{10,14},{12,8},{14,10},{16,20},{18,... | collective-permute-start | bytes 393224 | tf_op jit(solution)/shard_map/ppermute | solution.py:46
  19.6 7.4 %collective-permute-start.3 = (bf16[128,512]{1,0:T(8,128)(2,1)S(1)}, bf16[128,512]{1,0:T(8,128)(2,1)S(1)}, u32[]{:S(2)}, u32[]{:S(2)}) collective-permute-start(bf16[128,512]{1,0:T(8,128)(2,1)S(1)} %get-tuple-element.29.refs_1_), channel_id=1, source_target_pairs={{0,8},{2,10},{4,12},{6,14},{8,16},{10,18},{12,20},{14,22},{16,24},... | collective-permute-start | bytes 393224 | tf_op jit(solution)/shard_map/ppermute | solution.py:41
  20.1 6.9 %collective-permute-start.4 = (bf16[128,512]{1,0:T(8,128)(2,1)S(1)}, bf16[128,512]{1,0:T(8,128)(2,1)S(1)}, u32[]{:S(2)}, u32[]{:S(2)}) collective-permute-start(bf16[128,512]{1,0:T(8,128)(2,1)S(1)} %get-tuple-element.29.refs_1_), channel_id=1, source_target_pairs={{0,24},{2,26},{4,28},{6,30},{8,0},{10,2},{12,4},{14,6},{16,8},{18,... | collective-permute-start | bytes 393224 | tf_op jit(solution)/shard_map/ppermute | solution.py:41
  24.5 4.0 %collective-permute-start.10 = (bf16[128,512]{1,0:T(8,128)(2,1)S(1)}, bf16[128,512]{1,0:T(8,128)(2,1)S(1)}, u32[]{:S(2)}, u32[]{:S(2)}) collective-permute-start(bf16[128,512]{1,0:T(8,128)(2,1)S(1)} %get-tuple-element.33), channel_id=1, source_target_pairs={{0,2},{2,0},{4,6},{6,4},{8,10},{10,8},{12,14},{14,12},{16,18},{18,... | collective-permute-start | bytes 393224 | tf_op jit(solution)/shard_map/ppermute | solution.py:46
  24.6 3.9 %collective-permute-start.11 = (bf16[128,512]{1,0:T(8,128)(2,1)S(1)}, bf16[128,512]{1,0:T(8,128)(2,1)S(1)}, u32[]{:S(2)}, u32[]{:S(2)}) collective-permute-start(bf16[128,512]{1,0:T(8,128)(2,1)S(1)} %get-tuple-element.34), channel_id=1, source_target_pairs={{0,2},{2,0},{4,6},{6,4},{8,10},{10,8},{12,14},{14,12},{16,18},{18,... | collective-permute-start | bytes 393224 | tf_op jit(solution)/shard_map/ppermute | solution.py:46
  27.0 5.0 %collective-permute-start.6 = (bf16[128,512]{1,0:T(8,128)(2,1)S(1)}, bf16[128,512]{1,0:T(8,128)(2,1)S(1)}, u32[]{:S(2)}, u32[]{:S(2)}) collective-permute-start(bf16[128,512]{1,0:T(8,128)(2,1)S(1)} %far.2), channel_id=1, source_target_pairs={{0,4},{2,6},{4,0},{6,2},{8,12},{10,14},{12,8},{14,10},{16,20},{18,... | collective-permute-start | bytes 393224 | tf_op jit(solution)/shard_map/ppermute | solution.py:46
  28.6 6.4 %collective-permute-start.14 = (bf16[2,128,512]{2,1,0:T(8,128)(2,1)S(1)}, bf16[2,128,512]{2,1,0:T(8,128)(2,1)S(1)}, u32[]{:S(2)}, u32[]{:S(2)}) collective-permute-start(bf16[2,128,512]{2,1,0:T(8,128)(2,1)S(1)} %merge.2.refs_5_.refs_0_), channel_id=1, source_target_pairs={{0,1},{1,0},{2,3},{3,2},{4,5},{5,4},{6,7},{7,6},{8,9},{9,8},{10,11... | collective-permute-start | bytes 786440 | tf_op jit(solution)/shard_map/ppermute | solution.py:41
  32.3 1.4 %collective-permute-start.12 = (bf16[128,512]{1,0:T(8,128)(2,1)S(1)}, bf16[128,512]{1,0:T(8,128)(2,1)S(1)}, u32[]{:S(2)}, u32[]{:S(2)}) collective-permute-start(bf16[128,512]{1,0:T(8,128)(2,1)S(1)} %get-tuple-element.36), channel_id=1, source_target_pairs={{0,2},{2,0},{4,6},{6,4},{8,10},{10,8},{12,14},{14,12},{16,18},{18,... | collective-permute-start | bytes 393224 | tf_op jit(solution)/shard_map/ppermute | solution.py:46
  32.4 1.5 %collective-permute-start.13 = (bf16[128,512]{1,0:T(8,128)(2,1)S(1)}, bf16[128,512]{1,0:T(8,128)(2,1)S(1)}, u32[]{:S(2)}, u32[]{:S(2)}) collective-permute-start(bf16[128,512]{1,0:T(8,128)(2,1)S(1)} %get-tuple-element.37), channel_id=1, source_target_pairs={{0,2},{2,0},{4,6},{6,4},{8,10},{10,8},{12,14},{14,12},{16,18},{18,... | collective-permute-start | bytes 393224 | tf_op jit(solution)/shard_map/ppermute | solution.py:46
  35.2 7.5 %collective-permute-start.15 = (bf16[2,128,512]{2,1,0:T(8,128)(2,1)S(1)}, bf16[2,128,512]{2,1,0:T(8,128)(2,1)S(1)}, u32[]{:S(2)}, u32[]{:S(2)}) collective-permute-start(bf16[2,128,512]{2,1,0:T(8,128)(2,1)S(1)} %merge.3.refs_1_), channel_id=1, source_target_pairs={{0,1},{1,0},{2,3},{3,2},{4,5},{5,4},{6,7},{7,6},{8,9},{9,8},{10,11... | collective-permute-start | bytes 786440 | tf_op jit(solution)/shard_map/ppermute | solution.py:41

commit v9 on v7

--- a/solution.py
+++ b/solution.py
@@ -386,7 +386,7 @@
     lags = [lay_out_lags(part) for part in own]
 
     pieces = []
-    after_far, after_pick, after_merge = [core_offsets], [], []
+    after_far, after_pick, after_merge = [core_offsets] + own[1:], [], []
     for chunk in range(CHUNKS):
         piece, send = gather(chunk, directs[chunk], after_far, after_pick, after_merge)
         after_far, after_pick, after_merge = [], [piece[0]] + lags[1:], piece[1:]

time: 44.8 us -> 44.9 us (level)
    ppermute x7, starting transfers between devices: 13.2 us -> 12 us  [shift(): return lax.ppermute(x, axis, [(i, (i + by) % n) for i in range(n)])]
    ppermute x8, waiting for transfers between devices: 3.04 us -> 4.19 us  [swap(): return lax.ppermute(x, 'chan', [(i, i ^ bit) for i in range(n)])]
    ppermute x8, starting transfers between devices: 4.8 us -> 5.69 us  [swap(): return lax.ppermute(x, 'chan', [(i, i ^ bit) for i in range(n)])]
    ppermute x7, waiting for transfers between devices: 6.8 us -> 6.02 us  [shift(): return lax.ppermute(x, axis, [(i, (i + by) % n) for i in range(n)])]
  transfers between devices with their start and end apart: 16 -> 16, of which waited for: 12 -> 10; matrix products, arithmetic and copies ran while one was open for 0% -> 0% of each run, Pallas kernels for 15% -> 15%
where the time goes in v9:
time: 44.9 us; the launch traced here: 44.7 us
  starting transfers between devices  22.5 us (50%)
  waiting for transfers between devices  10.8 us (24%)
  Pallas kernels  10.6 us (24%)
  local copies, waits for them, and re-layouts  0.67 us (1%)
    ppermute x7, starting transfers between devices, shift(): return lax.ppermute(x, axis, [(i, (i + by) % n) for i in range(n)])  12 us
    ppermute x7, waiting for transfers between devices, shift(): return lax.ppermute(x, axis, [(i, (i + by) % n) for i in range(n)])  6.02 us
    ppermute x8, starting transfers between devices, swap(): return lax.ppermute(x, 'chan', [(i, i ^ bit) for i in range(n)])  5.69 us
    ppermute x1, starting transfers between devices, body(): before = lax.ppermute(tail, 'win', [(i, i + 1) for i in range(win - 1)])  4.87 us
    ppermute x8, waiting for transfers between devices, swap(): return lax.ppermute(x, 'chan', [(i, i ^ bit) for i in range(n)])  4.19 us
    pallas_call x2, Pallas kernels, lay_out_lags(): pl.pallas_call(lags_kernel, out_shape=jax.ShapeDtypeStruct((rows * LAGS,...  2.84 us
    pallas_call x2, Pallas kernels, accumulate(): pl.pallas_call(functools.partial(accumulate_kernel, firsts, acc is not No...  2.1 us
    pallas_call x1, Pallas kernels, finish(): pl.pallas_call(functools.partial(finish_kernel, reach, factor, first), ou...  1.92 us
  transfers between devices with their start and end apart: 16, of which 10 were waited for; matrix products, arithmetic and copies ran while one was open for 0% of the time, Pallas kernels for 15%

profile of v9, /device:TPU:0, one launch (start us, length us, event | category | flops | bytes accessed | tf_op | source)
XLA Modules:
  0.0 44.7 jit_solution(16736700446261333674)
XLA Ops:
  0.0 0.7 %copy-done.1 = f32[64]{0:T(128)S(1)} copy-done((f32[64]{0:T(128)S(1)}, f32[64]{0:T(128)}, u32[]{:S(2)}) %copy-start.1) | copy-done | bytes 280
  0.7 1.3 %head.1 = (bf16[128,128]{1,0:T(8,128)(2,1)S(1)}, bf16[128,4096]{1,0:T(8,128)(2,1)S(1)}, f32[1,64]{1,0:T(1,128)S(1)}) custom-call(bf16[128,4096]{1,0:T(8,128)(2,1)} %records_ref.1, f32[1,64]{1,0:T(1,128)S(1)} %bitcast.4), custom_call_target="tpu_custom_call" | custom-call | tf_op jit(solution)/shard_map/head/pallas_call | solution.py:62
  2.0 4.9 %collective-permute-start = (bf16[128,128]{1,0:T(8,128)(2,1)S(1)}, bf16[128,128]{1,0:T(8,128)(2,1)S(1)}, u32[]{:S(2)}, u32[]{:S(2)}) collective-permute-start(bf16[128,128]{1,0:T(8,128)(2,1)S(1)} %get-tuple-element.22), channel_id=1, source_target_pairs={{0,1},{2,3},{4,5},{6,7},{8,9},{10,11},{12,13},{14,15},{16,17},{18,... | collective-permute-start | bytes 98312 | tf_op jit(solution)/shard_map/ppermute | solution.py:361
  6.9 1.0 %bulk_filter.1 = (f32[128,1024]{1,0:T(8,128)S(1)}, f32[128,128]{1,0:T(8,128)S(1)}, bf16[384,128]{1,0:T(8,128)(2,1)S(1)}) custom-call(bf16[128,4096]{1,0:T(8,128)(2,1)S(1)} %get-tuple-element.23.records_ref, f32[1,64]{1,0:T(1,128)S(1)} %get-tuple-element.24.taps_ref), custom_call_target="tpu_custom_call" | custom-call | tf_op jit(solution)/shard_map/bulk_filter/pallas_call | solution.py:105
  7.9 0.6 %collective-permute-done.tail_ref = bf16[128,128]{1,0:T(8,128)(2,1)S(1)} collective-permute-done((bf16[128,128]{1,0:T(8,128)(2,1)S(1)}, bf16[128,128]{1,0:T(8,128)(2,1)S(1)}, u32[]{:S(2)}, u32[]{:S(2)}) %collective-permute-start) | collective-permute-done | bytes 32800 | tf_op jit(solution)/shard_map/ppermute | solution.py:361
  8.5 0.4 whiten.1
  8.8 1.6 %collective-permute-start.7 = (bf16[128,512]{1,0:T(8,128)(2,1)S(1)}, bf16[128,512]{1,0:T(8,128)(2,1)S(1)}, u32[]{:S(2)}, u32[]{:S(2)}) collective-permute-start(bf16[128,512]{1,0:T(8,128)(2,1)S(1)} %get-tuple-element.31.refs_1_), channel_id=1, source_target_pairs={{0,8},{2,10},{4,12},{6,14},{8,16},{10,18},{12,20},{14,22},{16,24},... | collective-permute-start | bytes 393224 | tf_op jit(solution)/shard_map/ppermute | solution.py:40
  10.5 2.2 %collective-permute-start.8 = (bf16[128,512]{1,0:T(8,128)(2,1)S(1)}, bf16[128,512]{1,0:T(8,128)(2,1)S(1)}, u32[]{:S(2)}, u32[]{:S(2)}) collective-permute-start(bf16[128,512]{1,0:T(8,128)(2,1)S(1)} %get-tuple-element.31.refs_1_), channel_id=1, source_target_pairs={{0,24},{2,26},{4,28},{6,30},{8,0},{10,2},{12,4},{14,6},{16,8},{18,... | collective-permute-start | bytes 393224 | tf_op jit(solution)/shard_map/ppermute | solution.py:40
  12.7 2.3 %collective-permute-start.1 = (bf16[64,1024]{1,0:T(8,128)(2,1)S(1)}, bf16[64,1024]{1,0:T(8,128)(2,1)S(1)}, u32[]{:S(2)}, u32[]{:S(2)}) collective-permute-start(bf16[64,1024]{1,0:T(8,128)(2,1)S(1)} %get-tuple-element.28), channel_id=1, source_target_pairs={{0,1},{1,0},{2,3},{3,2},{4,5},{5,4},{6,7},{7,6},{8,9},{9,8},{10,11... | collective-permute-start | bytes 393224 | tf_op jit(solution)/shard_map/ppermute | solution.py:40
  15.0 1.5 %collective-permute-start.5 = (bf16[128,1024]{1,0:T(8,128)(2,1)S(1)}, bf16[128,1024]{1,0:T(8,128)(2,1)S(1)}, u32[]{:S(2)}, u32[]{:S(2)}) collective-permute-start(bf16[128,1024]{1,0:T(8,128)(2,1)S(1)} %get-tuple-element.30), channel_id=1, source_target_pairs={{0,4},{2,6},{4,0},{6,2},{8,12},{10,14},{12,8},{14,10},{16,20},{18,... | collective-permute-start | bytes 786440 | tf_op jit(solution)/shard_map/ppermute | solution.py:45
  16.5 1.1 %collective-permute-done.2.refs_0_.core_offsets = s32[1,2]{1,0:T(1,128)S(1)} collective-permute-done((s32[1,2]{1,0:T(1,128)S(1)}, s32[1,2]{1,0:T(1,128)S(1)}, u32[]{:S(2)}, u32[]{:S(2)}) %collective-permute-start.2) | collective-permute-done | bytes 40 | tf_op jit(solution)/shard_map/ppermute | solution.py:45
  18.0 1.6 %collective-permute-start.9 = (bf16[128,512]{1,0:T(8,128)(2,1)S(1)}, bf16[128,512]{1,0:T(8,128)(2,1)S(1)}, u32[]{:S(2)}, u32[]{:S(2)}) collective-permute-start(bf16[128,512]{1,0:T(8,128)(2,1)S(1)} %far.3), channel_id=1, source_target_pairs={{0,4},{2,6},{4,0},{6,2},{8,12},{10,14},{12,8},{14,10},{16,20},{18,... | collective-permute-start | bytes 393224 | tf_op jit(solution)/shard_map/ppermute | solution.py:45
  19.6 0.6 %collective-permute-start.3 = (bf16[128,512]{1,0:T(8,128)(2,1)S(1)}, bf16[128,512]{1,0:T(8,128)(2,1)S(1)}, u32[]{:S(2)}, u32[]{:S(2)}) collective-permute-start(bf16[128,512]{1,0:T(8,128)(2,1)S(1)} %get-tuple-element.29.refs_1_), channel_id=1, source_target_pairs={{0,8},{2,10},{4,12},{6,14},{8,16},{10,18},{12,20},{14,22},{16,24},... | collective-permute-start | bytes 393224 | tf_op jit(solution)/shard_map/ppermute | solution.py:40
  20.1 3.3 %collective-permute-start.4 = (bf16[128,512]{1,0:T(8,128)(2,1)S(1)}, bf16[128,512]{1,0:T(8,128)(2,1)S(1)}, u32[]{:S(2)}, u32[]{:S(2)}) collective-permute-start(bf16[128,512]{1,0:T(8,128)(2,1)S(1)} %get-tuple-element.29.refs_1_), channel_id=1, source_target_pairs={{0,24},{2,26},{4,28},{6,30},{8,0},{10,2},{12,4},{14,6},{16,8},{18,... | collective-permute-start | bytes 393224 | tf_op jit(solution)/shard_map/ppermute | solution.py:40
  23.4 0.8 %collective-permute-done.9.refs_4_ = bf16[128,512]{1,0:T(8,128)(2,1)S(1)} collective-permute-done((bf16[128,512]{1,0:T(8,128)(2,1)S(1)}, bf16[128,512]{1,0:T(8,128)(2,1)S(1)}, u32[]{:S(2)}, u32[]{:S(2)}) %collective-permute-start.9) | collective-permute-done | bytes 131104 | tf_op jit(solution)/shard_map/ppermute | solution.py:45
  24.2 0.4 pick.2
  24.7 0.5 %collective-permute-start.11 = (bf16[128,512]{1,0:T(8,128)(2,1)S(1)}, bf16[128,512]{1,0:T(8,128)(2,1)S(1)}, u32[]{:S(2)}, u32[]{:S(2)}) collective-permute-start(bf16[128,512]{1,0:T(8,128)(2,1)S(1)} %get-tuple-element.34), channel_id=1, source_target_pairs={{0,2},{2,0},{4,6},{6,4},{8,10},{10,8},{12,14},{14,12},{16,18},{18,... | collective-permute-start | bytes 393224 | tf_op jit(solution)/shard_map/ppermute | solution.py:45
  25.2 1.8 %collective-permute-done.3.behind_ref.refs_0_ = bf16[128,512]{1,0:T(8,128)(2,1)S(1)} collective-permute-done((bf16[128,512]{1,0:T(8,128)(2,1)S(1)}, bf16[128,512]{1,0:T(8,128)(2,1)S(1)}, u32[]{:S(2)}, u32[]{:S(2)}) %collective-permute-start.3) | collective-permute-done | bytes 131104 | tf_op jit(solution)/shard_map/ppermute | solution.py:40
  27.0 1.5 %collective-permute-start.6 = (bf16[128,512]{1,0:T(8,128)(2,1)S(1)}, bf16[128,512]{1,0:T(8,128)(2,1)S(1)}, u32[]{:S(2)}, u32[]{:S(2)}) collective-permute-start(bf16[128,512]{1,0:T(8,128)(2,1)S(1)} %far.2), channel_id=1, source_target_pairs={{0,4},{2,6},{4,0},{6,2},{8,12},{10,14},{12,8},{14,10},{16,20},{18,... | collective-permute-start | bytes 393224 | tf_op jit(solution)/shard_map/ppermute | solution.py:45
  28.6 0.8 %collective-permute-start.14 = (bf16[2,128,512]{2,1,0:T(8,128)(2,1)S(1)}, bf16[2,128,512]{2,1,0:T(8,128)(2,1)S(1)}, u32[]{:S(2)}, u32[]{:S(2)}) collective-permute-start(bf16[2,128,512]{2,1,0:T(8,128)(2,1)S(1)} %merge.2.refs_5_.refs_0_), channel_id=1, source_target_pairs={{0,1},{1,0},{2,3},{3,2},{4,5},{5,4},{6,7},{7,6},{8,9},{9,8},{10,11... | collective-permute-start | bytes 786440 | tf_op jit(solution)/shard_map/ppermute | solution.py:40
  29.4 1.4 %lags.2.refs_6_.lags_ref = bf16[2112,1024]{1,0:T(8,128)(2,1)S(1)} custom-call(bf16[64,1024]{1,0:T(8,128)(2,1)S(1)} %collective-permute-done.1.own_ref.refs_1_), custom_call_target="tpu_custom_call" | custom-call | bytes 8388608 | tf_op jit(solution)/shard_map/lags/pallas_call | solution.py:178
  30.8 1.2 %collective-permute-done.6.refs_4_ = bf16[128,512]{1,0:T(8,128)(2,1)S(1)} collective-permute-done((bf16[128,512]{1,0:T(8,128)(2,1)S(1)}, bf16[128,512]{1,0:T(8,128)(2,1)S(1)}, u32[]{:S(2)}, u32[]{:S(2)}) %collective-permute-start.6) | collective-permute-done | bytes 131104 | tf_op jit(solution)/shard_map/ppermute | solution.py:45
  32.0 0.4 pick.3
  32.5 0.5 %collective-permute-start.13 = (bf16[128,512]{1,0:T(8,128)(2,1)S(1)}, bf16[128,512]{1,0:T(8,128)(2,1)S(1)}, u32[]{:S(2)}, u32[]{:S(2)}) collective-permute-start(bf16[128,512]{1,0:T(8,128)(2,1)S(1)} %get-tuple-element.37), channel_id=1, source_target_pairs={{0,2},{2,0},{4,6},{6,4},{8,10},{10,8},{12,14},{14,12},{16,18},{18,... | collective-permute-start | bytes 393224 | tf_op jit(solution)/shard_map/ppermute | solution.py:45
  33.0 0.8 %collective-permute-done.12.refs_0_ = bf16[128,512]{1,0:T(8,128)(2,1)S(1)} collective-permute-done((bf16[128,512]{1,0:T(8,128)(2,1)S(1)}, bf16[128,512]{1,0:T(8,128)(2,1)S(1)}, u32[]{:S(2)}, u32[]{:S(2)}) %collective-permute-start.12) | collective-permute-done | bytes 131104 | tf_op jit(solution)/shard_map/ppermute | solution.py:45
  34.1 1.0 %collective-permute-done.14.refs_2_.refs_0_ = bf16[2,128,512]{2,1,0:T(8,128)(2,1)S(1)} collective-permute-done((bf16[2,128,512]{2,1,0:T(8,128)(2,1)S(1)}, bf16[2,128,512]{2,1,0:T(8,128)(2,1)S(1)}, u32[]{:S(2)}, u32[]{:S(2)}) %collective-permute-start.14) | collective-permute-done | bytes 262176 | tf_op jit(solution)/shard_map/ppermute | solution.py:40
  35.2 1.1 %collective-permute-start.15 = (bf16[2,128,512]{2,1,0:T(8,128)(2,1)S(1)}, bf16[2,128,512]{2,1,0:T(8,128)(2,1)S(1)}, u32[]{:S(2)}, u32[]{:S(2)}) collective-permute-start(bf16[2,128,512]{2,1,0:T(8,128)(2,1)S(1)} %merge.3.refs_1_), channel_id=1, source_target_pairs={{0,1},{1,0},{2,3},{3,2},{4,5},{5,4},{6,7},{7,6},{8,9},{9,8},{10,11... | collective-permute-start | bytes 786440 | tf_op jit(solution)/shard_map/ppermute | solution.py:40
  36.3 1.4 %lags.3.lags_ref = bf16[2112,1024]{1,0:T(8,128)(2,1)S(1)} custom-call(bf16[64,1024]{1,0:T(8,128)(2,1)S(1)} %get-tuple-element.38.own_ref), custom_call_target="tpu_custom_call" | custom-call | bytes 8388608 | tf_op jit(solution)/shard_map/lags/pallas_call | solution.py:178
  37.7 1.3 %accumulate.2.refs_1_ = f32[2112,256]{1,0:T(8,128)S(1)} custom-call(bf16[2112,1024]{1,0:T(8,128)(2,1)S(1)} %lags.3.lags_ref, bf16[2,128,512]{2,1,0:T(8,128)(2,1)S(1)} %merge.2.refs_5_.refs_0_, bf16[2,128,512]{2,1,0:T(8,128)(2,1)S(1)} %merge.3.refs_1_), custom_call_target="tpu_custom_call" | custom-call | tf_op jit(solution)/shard_map/accumulate/pallas_call | solution.py:300
  39.0 0.8 %accumulate.3.acc_ref = f32[2112,256]{1,0:T(8,128)S(1)} custom-call(bf16[2112,1024]{1,0:T(8,128)(2,1)S(1)} %lags.2.refs_6_.lags_ref, bf16[2,128,512]{2,1,0:T(8,128)(2,1)S(1)} %collective-permute-done.14.refs_2_.refs_0_, f32[2112,256]{1,0:T(8,128)S(1)} %accumulate.2.refs_1_), custom_call_target="tpu_custom_call" | custom-call | tf_op jit(solution)/shard_map/accumulate/pallas_call | solution.py:300
  39.8 2.9 %collective-permute-done.15.other_ref = bf16[2,128,512]{2,1,0:T(8,128)(2,1)S(1)} collective-permute-done((bf16[2,128,512]{2,1,0:T(8,128)(2,1)S(1)}, bf16[2,128,512]{2,1,0:T(8,128)(2,1)S(1)}, u32[]{:S(2)}, u32[]{:S(2)}) %collective-permute-start.15) | collective-permute-done | bytes 262176 | tf_op jit(solution)/shard_map/ppermute | solution.py:40
  42.8 1.9 %finish.1 = f32[4224,128]{1,0:T(8,128)} custom-call(s32[1,2]{1,0:T(1,128)S(1)} %copy-done, bf16[2112,1024]{1,0:T(8,128)(2,1)S(1)} %lags.2.refs_6_.lags_ref, bf16[2,128,512]{2,1,0:T(8,128)(2,1)S(1)} %collective-permute-done.15.other_ref, f32[2112,256]{1,0:T(8,128)S(1)} %accumulate.3.acc_ref), custom_call_target="tpu_custom_call" | custom-call | tf_op jit(solution)/shard_map/finish/pallas_call | solution.py:339
  (18 shorter events, 0.9 us)
Async XLA Ops:
  0.0 16.5 %copy-start = (s32[1,2]{1,0:T(1,128)S(1)}, s32[1,2]{1,0:T(1,128)}, u32[]{:S(2)}) copy-start(s32[1,2]{1,0:T(1,128)} %offsets.5) | copy-start | bytes 28
  0.0 0.7 %copy-start.1 = (f32[64]{0:T(128)S(1)}, f32[64]{0:T(128)}, u32[]{:S(2)}) copy-start(f32[64]{0:T(128)} %param.4) | copy-start | bytes 772
  2.0 6.5 %collective-permute-start = (bf16[128,128]{1,0:T(8,128)(2,1)S(1)}, bf16[128,128]{1,0:T(8,128)(2,1)S(1)}, u32[]{:S(2)}, u32[]{:S(2)}) collective-permute-start(bf16[128,128]{1,0:T(8,128)(2,1)S(1)} %get-tuple-element.22), channel_id=1, source_target_pairs={{0,1},{2,3},{4,5},{6,7},{8,9},{10,11},{12,13},{14,15},{16,17},{18,... | collective-permute-start | bytes 98312 | tf_op jit(solution)/shard_map/ppermute | solution.py:361
  8.8 8.8 %collective-permute-start.7 = (bf16[128,512]{1,0:T(8,128)(2,1)S(1)}, bf16[128,512]{1,0:T(8,128)(2,1)S(1)}, u32[]{:S(2)}, u32[]{:S(2)}) collective-permute-start(bf16[128,512]{1,0:T(8,128)(2,1)S(1)} %get-tuple-element.31.refs_1_), channel_id=1, source_target_pairs={{0,8},{2,10},{4,12},{6,14},{8,16},{10,18},{12,20},{14,22},{16,24},... | collective-permute-start | bytes 393224 | tf_op jit(solution)/shard_map/ppermute | solution.py:40
  10.5 7.2 %collective-permute-start.8 = (bf16[128,512]{1,0:T(8,128)(2,1)S(1)}, bf16[128,512]{1,0:T(8,128)(2,1)S(1)}, u32[]{:S(2)}, u32[]{:S(2)}) collective-permute-start(bf16[128,512]{1,0:T(8,128)(2,1)S(1)} %get-tuple-element.31.refs_1_), channel_id=1, source_target_pairs={{0,24},{2,26},{4,28},{6,30},{8,0},{10,2},{12,4},{14,6},{16,8},{18,... | collective-permute-start | bytes 393224 | tf_op jit(solution)/shard_map/ppermute | solution.py:40
  12.7 5.3 %collective-permute-start.1 = (bf16[64,1024]{1,0:T(8,128)(2,1)S(1)}, bf16[64,1024]{1,0:T(8,128)(2,1)S(1)}, u32[]{:S(2)}, u32[]{:S(2)}) collective-permute-start(bf16[64,1024]{1,0:T(8,128)(2,1)S(1)} %get-tuple-element.28), channel_id=1, source_target_pairs={{0,1},{1,0},{2,3},{3,2},{4,5},{5,4},{6,7},{7,6},{8,9},{9,8},{10,11... | collective-permute-start | bytes 393224 | tf_op jit(solution)/shard_map/ppermute | solution.py:40
  15.0 9.2 %collective-permute-start.5 = (bf16[128,1024]{1,0:T(8,128)(2,1)S(1)}, bf16[128,1024]{1,0:T(8,128)(2,1)S(1)}, u32[]{:S(2)}, u32[]{:S(2)}) collective-permute-start(bf16[128,1024]{1,0:T(8,128)(2,1)S(1)} %get-tuple-element.30), channel_id=1, source_target_pairs={{0,4},{2,6},{4,0},{6,2},{8,12},{10,14},{12,8},{14,10},{16,20},{18,... | collective-permute-start | bytes 786440 | tf_op jit(solution)/shard_map/ppermute | solution.py:45
  16.5 1.1 %collective-permute-start.2 = (s32[1,2]{1,0:T(1,128)S(1)}, s32[1,2]{1,0:T(1,128)S(1)}, u32[]{:S(2)}, u32[]{:S(2)}) collective-permute-start(s32[1,2]{1,0:T(1,128)S(1)} %copy-done), channel_id=1, source_target_pairs={{0,2},{2,0},{4,6},{6,4},{8,10},{10,8},{12,14},{14,12},{16,18},{18,... | collective-permute-start | bytes 32 | tf_op jit(solution)/shard_map/ppermute | solution.py:45
  18.0 6.2 %collective-permute-start.9 = (bf16[128,512]{1,0:T(8,128)(2,1)S(1)}, bf16[128,512]{1,0:T(8,128)(2,1)S(1)}, u32[]{:S(2)}, u32[]{:S(2)}) collective-permute-start(bf16[128,512]{1,0:T(8,128)(2,1)S(1)} %far.3), channel_id=1, source_target_pairs={{0,4},{2,6},{4,0},{6,2},{8,12},{10,14},{12,8},{14,10},{16,20},{18,... | collective-permute-start | bytes 393224 | tf_op jit(solution)/shard_map/ppermute | solution.py:45
  19.6 7.4 %collective-permute-start.3 = (bf16[128,512]{1,0:T(8,128)(2,1)S(1)}, bf16[128,512]{1,0:T(8,128)(2,1)S(1)}, u32[]{:S(2)}, u32[]{:S(2)}) collective-permute-start(bf16[128,512]{1,0:T(8,128)(2,1)S(1)} %get-tuple-element.29.refs_1_), channel_id=1, source_target_pairs={{0,8},{2,10},{4,12},{6,14},{8,16},{10,18},{12,20},{14,22},{16,24},... | collective-permute-start | bytes 393224 | tf_op jit(solution)/shard_map/ppermute | solution.py:40
  20.1 6.9 %collective-permute-start.4 = (bf16[128,512]{1,0:T(8,128)(2,1)S(1)}, bf16[128,512]{1,0:T(8,128)(2,1)S(1)}, u32[]{:S(2)}, u32[]{:S(2)}) collective-permute-start(bf16[128,512]{1,0:T(8,128)(2,1)S(1)} %get-tuple-element.29.refs_1_), channel_id=1, source_target_pairs={{0,24},{2,26},{4,28},{6,30},{8,0},{10,2},{12,4},{14,6},{16,8},{18,... | collective-permute-start | bytes 393224 | tf_op jit(solution)/shard_map/ppermute | solution.py:40
  24.6 3.9 %collective-permute-start.10 = (bf16[128,512]{1,0:T(8,128)(2,1)S(1)}, bf16[128,512]{1,0:T(8,128)(2,1)S(1)}, u32[]{:S(2)}, u32[]{:S(2)}) collective-permute-start(bf16[128,512]{1,0:T(8,128)(2,1)S(1)} %get-tuple-element.33), channel_id=1, source_target_pairs={{0,2},{2,0},{4,6},{6,4},{8,10},{10,8},{12,14},{14,12},{16,18},{18,... | collective-permute-start | bytes 393224 | tf_op jit(solution)/shard_map/ppermute | solution.py:45
  24.7 3.8 %collective-permute-start.11 = (bf16[128,512]{1,0:T(8,128)(2,1)S(1)}, bf16[128,512]{1,0:T(8,128)(2,1)S(1)}, u32[]{:S(2)}, u32[]{:S(2)}) collective-permute-start(bf16[128,512]{1,0:T(8,128)(2,1)S(1)} %get-tuple-element.34), channel_id=1, source_target_pairs={{0,2},{2,0},{4,6},{6,4},{8,10},{10,8},{12,14},{14,12},{16,18},{18,... | collective-permute-start | bytes 393224 | tf_op jit(solution)/shard_map/ppermute | solution.py:45
  27.0 5.0 %collective-permute-start.6 = (bf16[128,512]{1,0:T(8,128)(2,1)S(1)}, bf16[128,512]{1,0:T(8,128)(2,1)S(1)}, u32[]{:S(2)}, u32[]{:S(2)}) collective-permute-start(bf16[128,512]{1,0:T(8,128)(2,1)S(1)} %far.2), channel_id=1, source_target_pairs={{0,4},{2,6},{4,0},{6,2},{8,12},{10,14},{12,8},{14,10},{16,20},{18,... | collective-permute-start | bytes 393224 | tf_op jit(solution)/shard_map/ppermute | solution.py:45
  28.6 6.4 %collective-permute-start.14 = (bf16[2,128,512]{2,1,0:T(8,128)(2,1)S(1)}, bf16[2,128,512]{2,1,0:T(8,128)(2,1)S(1)}, u32[]{:S(2)}, u32[]{:S(2)}) collective-permute-start(bf16[2,128,512]{2,1,0:T(8,128)(2,1)S(1)} %merge.2.refs_5_.refs_0_), channel_id=1, source_target_pairs={{0,1},{1,0},{2,3},{3,2},{4,5},{5,4},{6,7},{7,6},{8,9},{9,8},{10,11... | collective-permute-start | bytes 786440 | tf_op jit(solution)/shard_map/ppermute | solution.py:40
  32.5 1.4 %collective-permute-start.12 = (bf16[128,512]{1,0:T(8,128)(2,1)S(1)}, bf16[128,512]{1,0:T(8,128)(2,1)S(1)}, u32[]{:S(2)}, u32[]{:S(2)}) collective-permute-start(bf16[128,512]{1,0:T(8,128)(2,1)S(1)} %get-tuple-element.36), channel_id=1, source_target_pairs={{0,2},{2,0},{4,6},{6,4},{8,10},{10,8},{12,14},{14,12},{16,18},{18,... | collective-permute-start | bytes 393224 | tf_op jit(solution)/shard_map/ppermute | solution.py:45
  32.5 1.5 %collective-permute-start.13 = (bf16[128,512]{1,0:T(8,128)(2,1)S(1)}, bf16[128,512]{1,0:T(8,128)(2,1)S(1)}, u32[]{:S(2)}, u32[]{:S(2)}) collective-permute-start(bf16[128,512]{1,0:T(8,128)(2,1)S(1)} %get-tuple-element.37), channel_id=1, source_target_pairs={{0,2},{2,0},{4,6},{6,4},{8,10},{10,8},{12,14},{14,12},{16,18},{18,... | collective-permute-start | bytes 393224 | tf_op jit(solution)/shard_map/ppermute | solution.py:45
  35.2 7.6 %collective-permute-start.15 = (bf16[2,128,512]{2,1,0:T(8,128)(2,1)S(1)}, bf16[2,128,512]{2,1,0:T(8,128)(2,1)S(1)}, u32[]{:S(2)}, u32[]{:S(2)}) collective-permute-start(bf16[2,128,512]{2,1,0:T(8,128)(2,1)S(1)} %merge.3.refs_1_), channel_id=1, source_target_pairs={{0,1},{1,0},{2,3},{3,2},{4,5},{5,4},{6,7},{7,6},{8,9},{9,8},{10,11... | collective-permute-start | bytes 786440 | tf_op jit(solution)/shard_map/ppermute | solution.py:40
